TPU v7x, 32 devices: a whole 2x2x4 slice. The times are simulated.
32 devices in a mesh: ax: 8 (over y, x, core), th: 4 (over z).
Axes of the slice: x: 2, y: 2, z: 4, core: 2. Of those that a mesh axis runs over, the one named last changes fastest.
Arguments:
- populations: float32 [26, 16, 32, 1024], P(None, None, 'th', 'ax')
- wall_free: float32 [128, 32768], P(None, ('ax', 'th')), may hold values from 0 to 1
- wall_bound: float32 [128, 32768], P(None, ('ax', 'th')), may hold values from 0 to 0.5
- wall_propagator: float32 [128, 128], replicated
- bind_on: float32 [128], replicated, may hold values from 0.02 to 0.2
- bind_off: float32 [128], replicated, may hold values from 0.02 to 0.2
- iface_sector: int32 [32768, 1], P(('ax', 'th')), may hold values from 0 to 3; in each aligned block of 1024 rows (0 to 1023, 1024 to 2047, ...) at most 256 rows name the same one
- iface_line: int32 [32768], P(('ax', 'th')), may hold values from 0 to 1023
- strut_mask: int32 [32768], P(('ax', 'th')), may hold values 0 or 1
Outputs:
- drug_field: float32 [16, 32, 1024], P(None, 'th', 'ax')
- axial_flow: float32 [16, 32, 1024], P(None, 'th', 'ax')
- free_drug: float32 [128, 32768], P(None, ('ax', 'th'))
- bound_drug: float32 [128, 32768], P(None, ('ax', 'th'))
Inputs may be any that keep to these rules, and one draw needn't show every extreme that they name: `iface_sector`: among the rows of one device at most 256 name one sector, and in some device exactly 256 do.
All inputs are finite; a program needn't handle non-finite values. No bound on the sum of `strut_mask` on one device may be relied on, other than what follows from the above.
Results may differ from a plain program's by a relative error of at most 0.00023.
Values sent between devices are 32-bit elements; how exact they have to be, the bound alone decides.
No kernel may reach another device: no remote copies, remote signals or barrier semaphores. Data moves between devices by JAX's collectives and lax.ppermute only.
A program may use at most 64 MiB of HBM per device.

v0:
```python
import functools

import jax
import jax.numpy as jnp
from jax import lax
from jax.experimental import pallas as pl
from jax.experimental.pallas import tpu as pltpu
from jax.sharding import PartitionSpec as P

STEPS = 4
SUB = 2

VELOCITIES = [
    (0, 0, 0), (1, 0, 0), (-1, 0, 0), (0, 1, 0), (0, -1, 0), (0, 0, 1), (0, 0, -1),
    (1, 1, 0), (-1, -1, 0), (1, -1, 0), (-1, 1, 0),
    (1, 0, 1), (-1, 0, -1), (1, 0, -1), (-1, 0, 1),
    (0, 1, 1), (0, -1, -1), (0, 1, -1), (0, -1, 1),
    (0, 0, 0), (1, 0, 0), (-1, 0, 0), (0, 1, 0), (0, -1, 0), (0, 0, 1), (0, 0, -1),
]
WEIGHTS = [1.0 / 3.0] + [1.0 / 18.0] * 6 + [1.0 / 36.0] * 12 + [0.25] + [0.125] * 6
OPPOSITE = [0, 2, 1, 4, 3, 6, 5, 8, 7, 10, 9, 12, 11, 14, 13, 16, 15, 18, 17, 19, 21, 20, 23, 22, 25, 24]
MIRROR = [0, 1, 2, 3, 4, 6, 5, 7, 8, 9, 10, 13, 14, 11, 12, 17, 18, 15, 16, 19, 20, 21, 22, 23, 25, 24]
SECTOR_RISING = [3, 7, 10, 15, 17, 22]
SECTOR_FALLING = [4, 8, 9, 16, 18, 23]
SLAB_RISING = [1, 7, 9, 11, 13, 20]
SLAB_FALLING = [2, 8, 10, 12, 14, 21]
PAIRS = [(1, 2), (3, 4), (5, 6), (7, 8), (9, 10), (11, 12), (13, 14), (15, 16), (17, 18)]
DRUG_PAIRS = [(20, 21), (22, 23), (24, 25)]
FLOWS = 19
MEMBERS = 26
RELAX_FLOW = 1.25
RELAX_DRUG = 1.1
PUSH_AXIAL = 0.0001
PERMEABILITY = 0.3
RELEASE_RATE = 0.5

F32 = jnp.float32
BF16 = jnp.bfloat16
VMEM = pltpu.VMEM


def shifted(block, axis, distance):
    count = lax.axis_size(axis)
    return lax.ppermute(block, axis, [((i - distance) % count, i) for i in range(count)])


def lanes(shape):
    return lax.broadcasted_iota(jnp.int32, shape, len(shape) - 1)


def sublanes(shape):
    return lax.broadcasted_iota(jnp.int32, shape, len(shape) - 2)


def split3(value):
    high = value.astype(BF16)
    rest = value - high.astype(F32)
    middle = rest.astype(BF16)
    low = (rest - middle.astype(F32)).astype(BF16)
    return high, middle, low


def one_hot_lines(low_row, width):
    shape = (width, low_row.shape[-1])
    return jnp.where(sublanes(shape) == low_row, 1.0, 0.0).astype(BF16)


def scatter_rows(value_rows, code_rows, groups, width):
    terms, hots = [], []
    for value, code in zip(value_rows, code_rows, strict=True):
        group = code // width
        shape = (groups, value.shape[-1])
        hit = sublanes(shape) == group
        terms.append(jnp.concatenate([jnp.where(hit, part.astype(F32), 0.0) for part in split3(value)], axis=0).astype(BF16))
        hots.append(one_hot_lines(code - group * width, width))
    left = jnp.concatenate(terms, axis=1)
    right = jnp.concatenate(hots, axis=1)
    total = lax.dot_general(left, right, (((1,), (1,)), ((), ())), preferred_element_type=F32)
    return total[:groups] + total[groups:2 * groups] + total[2 * groups:3 * groups]


def gather_rows(table, code_rows, width):
    groups = table.shape[0]
    left = jnp.concatenate(split3(table), axis=0)
    lows = [code - (code // width) * width for code in code_rows]
    right = jnp.concatenate([one_hot_lines(low, width) for low in lows], axis=1)
    picked = jnp.dot(left, right, preferred_element_type=F32)
    picked = picked[:groups] + picked[groups:2 * groups] + picked[2 * groups:3 * groups]
    results, start = [], 0
    for code in code_rows:
        count = code.shape[-1]
        hit = sublanes((groups, count)) == code // width
        results.append(jnp.sum(jnp.where(hit, picked[:, start:start + count], 0.0), axis=0, keepdims=True))
        start += count
    return results


def source_plane(member, level, radial):
    step_r = VELOCITIES[member][2]
    if step_r == 1:
        return ((MIRROR[member], 0) if level == 0 else (member, level - 1)), True
    if step_r == -1:
        return ((OPPOSITE[member], radial - 1), False) if level == radial - 1 else ((member, level + 1), True)
    return (member, level), True


def axial_shift(value, step, member, level, radial, behind, ahead):
    along = value.shape[-1]
    lane = lanes(value.shape)
    if step == 1:
        slot = SLAB_RISING.index(member) * radial + level
        return jnp.where(lane == 0, pltpu.roll(behind, (-slot) % along, 1), pltpu.roll(value, 1, 1))
    slot = SLAB_FALLING.index(member) * radial + level
    return jnp.where(lane == along - 1, pltpu.roll(ahead, (along - 1 - slot) % along, 1), pltpu.roll(value, along - 1, 1))


def streamed(post, member, level, radial, behind, ahead, below_row, above_row):
    (origin, depth), moves = source_plane(member, level, radial)
    value = post[origin, depth]
    if not moves:
        return value
    step_z, step_s, _ = VELOCITIES[member]
    across = value.shape[0]
    if step_z:
        value = axial_shift(value, step_z, origin, depth, radial, behind, ahead)
    if step_s == 1:
        row = below_row(SECTOR_RISING.index(origin) * radial + depth)
        value = jnp.where(sublanes(value.shape) == 0, row, pltpu.roll(value, 1, 0))
    elif step_s == -1:
        row = above_row(SECTOR_FALLING.index(origin) * radial + depth)
        value = jnp.where(sublanes(value.shape) == across - 1, row, pltpu.roll(value, across - 1, 0))
    return value


def collide(members):
    def total(component):
        up, down = None, None
        for member in range(1, FLOWS):
            factor = VELOCITIES[member][component]
            if factor > 0:
                up = members[member] if up is None else up + members[member]
            elif factor < 0:
                down = members[member] if down is None else down + members[member]
        return up - down

    density = members[0]
    for member in range(1, FLOWS):
        density = density + members[member]
    inverse = 1.0 / density
    velocity = [(total(0) + PUSH_AXIAL) * inverse, total(1) * inverse, total(2) * inverse]
    speed_sq = velocity[0] * velocity[0] + velocity[1] * velocity[1] + velocity[2] * velocity[2]
    base = 1.0 - 1.5 * speed_sq
    weighted = {}
    for weight in sorted(set(WEIGHTS[:FLOWS])):
        weighted[weight] = (RELAX_FLOW * weight) * density

    def projected(member):
        result = None
        for component in range(3):
            factor = VELOCITIES[member][component]
            if factor == 0:
                continue
            if result is None:
                result = velocity[component] if factor > 0 else -velocity[component]
            else:
                result = result + velocity[component] if factor > 0 else result - velocity[component]
        return result

    results = [None] * MEMBERS
    results[0] = (1.0 - RELAX_FLOW) * members[0] + weighted[WEIGHTS[0]] * base
    for first, second in PAIRS:
        along = projected(first)
        even = weighted[WEIGHTS[first]] * (base + 4.5 * along * along)
        odd = weighted[WEIGHTS[first]] * (3.0 * along)
        results[first] = (1.0 - RELAX_FLOW) * members[first] + (even + odd)
        results[second] = (1.0 - RELAX_FLOW) * members[second] + (even - odd)
    concentration = members[FLOWS]
    for member in range(FLOWS + 1, MEMBERS):
        concentration = concentration + members[member]
    rest = (RELAX_DRUG * WEIGHTS[FLOWS]) * concentration
    results[FLOWS] = (1.0 - RELAX_DRUG) * members[FLOWS] + rest
    even = (RELAX_DRUG * WEIGHTS[FLOWS + 1]) * concentration
    for first, second in DRUG_PAIRS:
        odd = even * (4.0 * projected(first))
        results[first] = (1.0 - RELAX_DRUG) * members[first] + (even + odd)
        results[second] = (1.0 - RELAX_DRUG) * members[second] + (even - odd)
    return results


def code_list(codes):
    return [codes[row:row + 1, :] for row in range(codes.shape[0])]


def pack_lines(row, width):
    return jnp.concatenate([row[:, start:start + width] for start in range(0, row.shape[-1], width)], axis=0)


def first_kernel(sectors, drug_ref, code_ref, strut_ref, free_ref, *outs):
    across, width = code_ref.shape
    codes = code_ref[...]
    surface = drug_ref[0, 0]
    for member in range(1, drug_ref.shape[0]):
        surface = surface + drug_ref[member, 0]
    rows = code_list(codes)
    groups = sectors * across
    sums = scatter_rows(code_list(surface), rows, groups, width)
    counts = scatter_rows(code_list(jnp.ones_like(surface)), rows, groups, width)
    first = pack_lines(free_ref[0:1, :], width)
    openness = PERMEABILITY * (1.0 - strut_ref[...].astype(F32))
    for rel in range(sectors):
        out = outs[rel]
        out[0:across] = sums[rel * across:(rel + 1) * across]
        out[across:2 * across] = counts[rel * across:(rel + 1) * across]
        out[2 * across:3 * across] = first
        out[3 * across:4 * across] = openness
        if rel in (1, sectors - 1):
            edge = codes[across - 1:across] if rel == 1 else codes[0:1]
            out[4 * across:5 * across] = jnp.broadcast_to(edge, (across, width)).astype(F32)


def step_kernel(sectors, first, *refs):
    refs = list(refs)
    post_ref, code_ref = refs[0], refs[1]
    inbox = refs[2:2 + sectors]
    refs = refs[2 + sectors:]
    if first:
        new_ref, rise_ref, fall_ref, open_ref = refs
    else:
        behind_ref, ahead_ref, open_ref, new_ref, rise_ref, fall_ref = refs
    radial, across, along = post_ref.shape[1:]
    codes = code_list(code_ref[...])
    offset = 2 * across if first else across
    table = jnp.concatenate([box[offset:offset + across, :] for box in inbox], axis=0)
    picked = jnp.concatenate(gather_rows(table, codes, along), axis=0)
    if first:
        table = jnp.concatenate([box[3 * across:4 * across, :] for box in inbox], axis=0)
        openness = jnp.concatenate(gather_rows(table, codes, along), axis=0)
        open_ref[...] = openness
    else:
        openness = open_ref[...]
        behind, ahead = behind_ref[...], ahead_ref[...]
        below, above = inbox[sectors - 1], inbox[1]
        start = 2 * across

        def below_row(row):
            return jnp.broadcast_to(below[start + row:start + row + 1, :], (across, along))

        def above_row(row):
            return jnp.broadcast_to(above[start + row:start + row + 1, :], (across, along))

    rise = jnp.zeros((across, along), F32)
    fall = jnp.zeros((across, along), F32)
    lane = lanes((across, along))
    for level in range(radial):
        if first:
            members = [post_ref[member, level] for member in range(MEMBERS)]
        else:
            members = [streamed(post_ref, member, level, radial, behind, ahead, below_row, above_row) for member in range(MEMBERS)]
        if level == radial - 1:
            surface = members[FLOWS]
            for member in range(FLOWS + 1, MEMBERS):
                surface = surface + members[member]
            flux = openness * (surface - picked)
            for member in range(FLOWS, MEMBERS):
                members[member] = members[member] - WEIGHTS[member] * flux
        results = collide(members)
        for member in range(MEMBERS):
            new_ref[member, level] = results[member]
        for place, member in enumerate(SLAB_RISING):
            slot = place * radial + level
            rise = jnp.where(lane == slot, pltpu.roll(results[member], (slot + 1) % along, 1), rise)
        for place, member in enumerate(SLAB_FALLING):
            slot = place * radial + level
            fall = jnp.where(lane == slot, pltpu.roll(results[member], slot, 1), fall)
    rise_ref[...] = rise
    fall_ref[...] = fall


def wall_kernel(sectors, free_ref, bound_ref, spread_ref, on_ref, off_ref, strut_ref, counts_ref, *refs):
    inbox, (new_free, new_bound, top_ref) = refs[:sectors], refs[sectors:]
    across, width = strut_ref.shape
    depth = spread_ref.shape[0]
    total = inbox[0][0:across, :]
    for box in inbox[1:]:
        total = total + box[0:across, :]
    strut = strut_ref[...].astype(F32)
    first = pack_lines(free_ref[0:1, :], width)
    added = (PERMEABILITY * (1.0 - strut)) * (total - counts_ref[...] * first) + RELEASE_RATE * strut
    spread = spread_ref[...]
    rate_on = jnp.transpose(jnp.broadcast_to(on_ref[...], (depth, depth)))
    rate_off = jnp.transpose(jnp.broadcast_to(off_ref[...], (depth, depth)))
    is_top = sublanes((depth, width)) == 0
    for row in range(across):
        place = slice(row * width, (row + 1) * width)
        free = free_ref[:, place] + jnp.where(is_top, added[row:row + 1, :], 0.0)
        bound = bound_ref[:, place]
        for _ in range(SUB):
            free = jnp.dot(spread, free, precision=lax.Precision.HIGHEST, preferred_element_type=F32)
            rate = rate_on * free * (1.0 - bound) - rate_off * bound
            free = free - rate
            bound = bound + rate
        new_free[:, place] = free
        new_bound[:, place] = bound
        top_ref[row:row + 1, :] = free[0:1, :]


def edge_rows(post_ref, behind, ahead, rows_up, rows_down):
    radial, across, along = post_ref.shape[1:]
    for place, member in enumerate(SECTOR_RISING):
        for level in range(radial):
            value = post_ref[member, level]
            if VELOCITIES[member][0]:
                value = axial_shift(value, VELOCITIES[member][0], member, level, radial, behind, ahead)
            rows_up(place * radial + level, value[across - 1:across, :])
    for place, member in enumerate(SECTOR_FALLING):
        for level in range(radial):
            value = post_ref[member, level]
            if VELOCITIES[member][0]:
                value = axial_shift(value, VELOCITIES[member][0], member, level, radial, behind, ahead)
            rows_down(place * radial + level, value[0:1, :])


def send_kernel(sectors, last, *refs):
    if last:
        post_ref, behind_ref, ahead_ref, up_ref, down_ref = refs
        start = 0
    else:
        post_ref, behind_ref, ahead_ref, code_ref, edges_ref, top_ref = refs[:6]
        outs = refs[6:]
        up_ref, down_ref = outs[1], outs[sectors - 1]
    radial, across, along = post_ref.shape[1:]
    behind, ahead = behind_ref[...], ahead_ref[...]
    if not last:
        start = 2 * across
        end = radial - 1
        row = sublanes((across, along))
        surface = post_ref[FLOWS, end] + post_ref[FLOWS + 5, end - 1] + post_ref[FLOWS + 5, end]
        surface = surface + axial_shift(post_ref[FLOWS + 1, end], 1, FLOWS + 1, end, radial, behind, ahead)
        surface = surface + axial_shift(post_ref[FLOWS + 2, end], -1, FLOWS + 2, end, radial, behind, ahead)
        rising = post_ref[FLOWS + 3, end]
        falling = post_ref[FLOWS + 4, end]
        surface = surface + jnp.where(row == 0, 0.0, pltpu.roll(rising, 1, 0))
        surface = surface + jnp.where(row == across - 1, 0.0, pltpu.roll(falling, across - 1, 0))
        values = code_list(surface) + [rising[across - 1:across, :], falling[0:1, :]]
        codes = code_list(code_ref[...]) + [edges_ref[0:1, :], edges_ref[1:2, :]]
        sums = scatter_rows(values, codes, sectors * across, along)
        top = top_ref[...]
        for rel in range(sectors):
            outs[rel][0:across] = sums[rel * across:(rel + 1) * across]
            outs[rel][across:2 * across] = top

    def rows_up(index, value):
        up_ref[start + index:start + index + 1, :] = value

    def rows_down(index, value):
        down_ref[start + index:start + index + 1, :] = value

    edge_rows(post_ref, behind, ahead, rows_up, rows_down)


def last_kernel(post_ref, behind_ref, ahead_ref, below, above, drug_ref, flow_ref):
    radial, across, along = post_ref.shape[1:]
    behind, ahead = behind_ref[...], ahead_ref[...]

    def below_row(row):
        return jnp.broadcast_to(below[row:row + 1, :], (across, along))

    def above_row(row):
        return jnp.broadcast_to(above[row:row + 1, :], (across, along))

    for level in range(radial):
        def member_of(member):
            return streamed(post_ref, member, level, radial, behind, ahead, below_row, above_row)

        drug = member_of(FLOWS)
        for member in range(FLOWS + 1, MEMBERS):
            drug = drug + member_of(member)
        drug_ref[level] = drug
        flow = None
        for member in range(FLOWS):
            factor = VELOCITIES[member][0]
            if factor:
                value = member_of(member)
                flow = (value if factor > 0 else -value) if flow is None else (flow + value if factor > 0 else flow - value)
        flow_ref[level] = flow


def kernel_call(body, name, outs, count, **kwargs):
    return pl.pallas_call(
        body,
        name=name,
        out_shape=[jax.ShapeDtypeStruct(shape, F32) for shape in outs],
        in_specs=[pl.BlockSpec(memory_space=VMEM)] * count,
        out_specs=[pl.BlockSpec(memory_space=VMEM)] * len(outs),
        compiler_params=pltpu.CompilerParams(vmem_limit_bytes=24 * 1024 * 1024),
        **kwargs,
    )


def per_device(populations, wall_free, wall_bound, wall_propagator, bind_on, bind_off, iface_sector, iface_line, strut_mask):
    members, radial, across, along = populations.shape
    sectors = lax.axis_size("th")
    surface_count = iface_line.shape[0]
    plane = (across, along)
    rims = len(SECTOR_RISING) * radial
    mine = lax.axis_index("th")
    rel = (iface_sector[:, 0] - mine) % sectors
    codes = (rel * surface_count + iface_line).reshape(plane)
    strut = strut_mask.reshape(plane)
    rate_on = bind_on.reshape(1, -1)
    rate_off = bind_off.reshape(1, -1)

    def exchange(boxes):
        inbox = [boxes[0]] + [None] * (sectors - 1)
        for hop in range(1, sectors):
            inbox[sectors - hop] = shifted(boxes[hop], "th", hop)
        return inbox

    sizes = [((5 if hop in (1, sectors - 1) else 4) * across, along) for hop in range(sectors)]
    drug = populations[FLOWS:, radial - 1:]
    boxes = kernel_call(functools.partial(first_kernel, sectors), "first", sizes, 4)(drug, codes, strut, wall_free)
    inbox = exchange(boxes)
    counts = inbox[0][across:2 * across]
    for box in inbox[1:]:
        counts = counts + box[across:2 * across]
    above_edge = inbox[1][4 * across:4 * across + 1].astype(jnp.int32)
    below_edge = inbox[sectors - 1][4 * across:4 * across + 1].astype(jnp.int32)
    limit = sectors * surface_count
    edges = jnp.concatenate([(above_edge + surface_count) % limit, (below_edge + limit - surface_count) % limit], axis=0)

    state, free, bound, openness = populations, wall_free, wall_bound, None
    behind = ahead = None
    for step in range(STEPS):
        first, last = step == 0, step == STEPS - 1
        outs = [populations.shape, plane, plane] + ([plane] if first else [])
        extra = [] if first else [behind, ahead, openness]
        results = kernel_call(functools.partial(step_kernel, sectors, first), "step", outs, 2 + sectors + len(extra))(
            state, codes, *inbox, *extra
        )
        state, rise, fall = results[:3]
        openness = results[3] if first else openness
        free, bound, top = kernel_call(
            functools.partial(wall_kernel, sectors), "wall", [wall_free.shape, wall_free.shape, plane], 7 + sectors
        )(free, bound, wall_propagator, rate_on, rate_off, strut, counts, *inbox)
        behind = shifted(rise, "ax", 1)
        ahead = shifted(fall, "ax", -1)
        if last:
            up, down = kernel_call(
                functools.partial(send_kernel, sectors, True), "send", [(rims, along)] * 2, 3
            )(state, behind, ahead)
            below, above = shifted(up, "th", 1), shifted(down, "th", -1)
        else:
            sizes = [(2 * across + (rims if hop in (1, sectors - 1) else 0), along) for hop in range(sectors)]
            boxes = kernel_call(functools.partial(send_kernel, sectors, False), "send", sizes, 6)(
                state, behind, ahead, codes, edges, top
            )
            inbox = exchange(boxes)
    drug_field, axial_flow = kernel_call(last_kernel, "last", [(radial,) + plane] * 2, 5)(state, behind, ahead, below, above)
    return drug_field, axial_flow, free, bound


def solution(mesh):
    placed = (
        P(None, None, "th", "ax"),
        P(None, ("ax", "th")),
        P(None, ("ax", "th")),
        P(),
        P(),
        P(),
        P(("ax", "th"), None),
        P(("ax", "th")),
        P(("ax", "th")),
    )
    return jax.shard_map(
        per_device,
        mesh=mesh,
        in_specs=placed,
        out_specs=(
            P(None, "th", "ax"),
            P(None, "th", "ax"),
            P(None, ("ax", "th")),
            P(None, ("ax", "th")),
        ),
        check_vma=False,
    )
```

profile of v0, /device:TPU:0, one launch (start us, length us, event | category | flops | bytes accessed | tf_op | source)
XLA Modules:
  0.0 73.8 jit_solution(6413275770630750631)
XLA Ops:
  0.7 0.8 %slice.21.drug_ref = f32[7,1,8,128]{3,2,1,0:T(8,128)S(1)} slice(f32[26,16,8,128]{3,2,1,0:T(8,128)} %refs_0_.1), slice={[19:26], [15:16], [0:8], [0:128]} | slice | bytes 57344 | tf_op jit(solution)/shard_map/slice | solution.py:420
  2.9 1.0 %copy-done = f32[128,1024]{1,0:T(8,128)S(1)} copy-done((f32[128,1024]{1,0:T(8,128)S(1)}, f32[128,1024]{1,0:T(8,128)}, u32[]{:S(2)}) %copy-start) | copy-done | bytes 524312
  4.9 5.1 %collective-permute-start = (f32[40,128]{1,0:T(8,128)S(1)}, f32[40,128]{1,0:T(8,128)S(1)}, u32[]{:S(2)}, u32[]{:S(2)}) collective-permute-start(f32[40,128]{1,0:T(8,128)S(1)} %get-tuple-element.49), channel_id=1, source_target_pairs={{1,0},{2,1},{3,2},{0,3},{5,4},{6,5},{7,6},{4,7},{9,8},{10,9},{11,1... | collective-permute-start | bytes 61448 | tf_op jit(solution)/shard_map/ppermute | solution.py:44
  10.0 1.0 %collective-permute-start.1 = (f32[32,128]{1,0:T(8,128)S(1)}, f32[32,128]{1,0:T(8,128)S(1)}, u32[]{:S(2)}, u32[]{:S(2)}) collective-permute-start(f32[32,128]{1,0:T(8,128)S(1)} %get-tuple-element.50), channel_id=1, source_target_pairs={{2,0},{3,1},{0,2},{1,3},{6,4},{7,5},{4,6},{5,7},{10,8},{11,9},{8,1... | collective-permute-start | bytes 49160 | tf_op jit(solution)/shard_map/ppermute | solution.py:44
  11.0 3.6 %collective-permute-done.1.refs_4_.refs_2_ = f32[32,128]{1,0:T(8,128)S(1)} collective-permute-done((f32[32,128]{1,0:T(8,128)S(1)}, f32[32,128]{1,0:T(8,128)S(1)}, u32[]{:S(2)}, u32[]{:S(2)}) %collective-permute-start.1) | collective-permute-done | bytes 16416 | tf_op jit(solution)/shard_map/ppermute | solution.py:44
  14.6 0.9 %collective-permute-done.2.refs_5_.refs_3_ = f32[40,128]{1,0:T(8,128)S(1)} collective-permute-done((f32[40,128]{1,0:T(8,128)S(1)}, f32[40,128]{1,0:T(8,128)S(1)}, u32[]{:S(2)}, u32[]{:S(2)}) %collective-permute-start.2) | collective-permute-done | bytes 20512 | tf_op jit(solution)/shard_map/ppermute | solution.py:44
  15.6 1.5 %copy-done.2 = f32[26,16,8,128]{3,2,1,0:T(8,128)S(1)} copy-done((f32[26,16,8,128]{3,2,1,0:T(8,128)S(1)}, f32[26,16,8,128]{3,2,1,0:T(8,128)}, u32[]{:S(2)}) %copy-start.2) | copy-done | bytes 1703960
  17.0 0.9 %step.4 = (f32[26,16,8,128]{3,2,1,0:T(8,128)S(1)}, f32[8,128]{1,0:T(8,128)S(1)}, f32[8,128]{1,0:T(8,128)S(1)}, f32[8,128]{1,0:T(8,128)S(1)}) custom-call(f32[26,16,8,128]{3,2,1,0:T(8,128)S(1)} %copy-done.2, s32[8,128]{1,0:T(8,128)S(1)} %fusion.3.code_ref.refs_1_.refs_3_, f32[32,128]{1,0:T(8,128)S(1)} %get-tuple-element.48.refs_2_.refs_0_, ...), custom_call_target="tpu_custom_call" | custom-call | tf_op jit(solution)/shard_map/step/pallas_call | solution.py:437
  17.9 2.6 %collective-permute-start.4 = (f32[8,128]{1,0:T(8,128)S(1)}, f32[8,128]{1,0:T(8,128)S(1)}, u32[]{:S(2)}, u32[]{:S(2)}) collective-permute-start(f32[8,128]{1,0:T(8,128)S(1)} %get-tuple-element.54), channel_id=1, source_target_pairs={{4,0},{8,4},{12,8},{16,12},{20,16},{24,20},{28,24},{0,28},{5,1},{9... | collective-permute-start | bytes 12296 | tf_op jit(solution)/shard_map/ppermute | solution.py:44
  20.7 1.3 %wall.4 = (f32[128,1024]{1,0:T(8,128)S(1)}, f32[128,1024]{1,0:T(8,128)S(1)}, f32[8,128]{1,0:T(8,128)S(1)}) custom-call(f32[128,1024]{1,0:T(8,128)S(1)} %copy-done.1, f32[128,1024]{1,0:T(8,128)S(1)} %copy-done.4, f32[128,128]{1,0:T(8,128)S(1)} %copy-done.3, f32[1,128]{1,0:T(1,128)S(1)} %bitcast.11, f32[1,128]{1,0:T(1,128)S(1)} %bitcast.15, ...), custom_call_target="tpu_custom_call" | custom-call | tf_op jit(solution)/shard_map/wall/pallas_call | solution.py:442
  22.3 2.9 %collective-permute-start.5 = (f32[112,128]{1,0:T(8,128)S(1)}, f32[112,128]{1,0:T(8,128)S(1)}, u32[]{:S(2)}, u32[]{:S(2)}) collective-permute-start(f32[112,128]{1,0:T(8,128)S(1)} %get-tuple-element.57), channel_id=1, source_target_pairs={{1,0},{2,1},{3,2},{0,3},{5,4},{6,5},{7,6},{4,7},{9,8},{10,9},{11,1... | collective-permute-start | bytes 172040 | tf_op jit(solution)/shard_map/ppermute | solution.py:44
  25.9 3.9 %collective-permute-done.6.refs_4_.refs_2_ = f32[16,128]{1,0:T(8,128)S(1)} collective-permute-done((f32[16,128]{1,0:T(8,128)S(1)}, f32[16,128]{1,0:T(8,128)S(1)}, u32[]{:S(2)}, u32[]{:S(2)}) %collective-permute-start.6) | collective-permute-done | bytes 8224 | tf_op jit(solution)/shard_map/ppermute | solution.py:44
  29.8 1.4 %collective-permute-done.7.refs_5_.refs_3_ = f32[112,128]{1,0:T(8,128)S(1)} collective-permute-done((f32[112,128]{1,0:T(8,128)S(1)}, f32[112,128]{1,0:T(8,128)S(1)}, u32[]{:S(2)}, u32[]{:S(2)}) %collective-permute-start.7) | collective-permute-done | bytes 57376 | tf_op jit(solution)/shard_map/ppermute | solution.py:44
  31.2 1.9 %step.5 = (f32[26,16,8,128]{3,2,1,0:T(8,128)S(1)}, f32[8,128]{1,0:T(8,128)S(1)}, f32[8,128]{1,0:T(8,128)S(1)}) custom-call(f32[26,16,8,128]{3,2,1,0:T(8,128)S(1)} %get-tuple-element.52.refs_0_, s32[8,128]{1,0:T(8,128)S(1)} %fusion.3.code_ref.refs_1_.refs_3_, f32[16,128]{1,0:T(8,128)S(1)} %get-tuple-element.56.refs_2_.refs_0_, ...), custom_call_target="tpu_custom_call" | custom-call | tf_op jit(solution)/shard_map/step/pallas_call | solution.py:437
  33.1 2.6 %collective-permute-start.9 = (f32[8,128]{1,0:T(8,128)S(1)}, f32[8,128]{1,0:T(8,128)S(1)}, u32[]{:S(2)}, u32[]{:S(2)}) collective-permute-start(f32[8,128]{1,0:T(8,128)S(1)} %get-tuple-element.63), channel_id=1, source_target_pairs={{4,0},{8,4},{12,8},{16,12},{20,16},{24,20},{28,24},{0,28},{5,1},{9... | collective-permute-start | bytes 12296 | tf_op jit(solution)/shard_map/ppermute | solution.py:44
  35.8 1.3 %wall.5 = (f32[128,1024]{1,0:T(8,128)S(1)}, f32[128,1024]{1,0:T(8,128)S(1)}, f32[8,128]{1,0:T(8,128)S(1)}) custom-call(f32[128,1024]{1,0:T(8,128)S(1)} %get-tuple-element.64.free_ref, f32[128,1024]{1,0:T(8,128)S(1)} %get-tuple-element.65.bound_ref, f32[128,128]{1,0:T(8,128)S(1)} %copy-done.3, f32[1,128]{1,0:T(1,128)S(1)} %bitcast.12, f32[1,128]{1,0:T(1,128)S(1)} %bitcast.16, ...), custom_call_target="tpu_custom_call" | custom-call | tf_op jit(solution)/shard_map/wall/pallas_call | solution.py:442
  37.4 2.5 %collective-permute-start.10 = (f32[112,128]{1,0:T(8,128)S(1)}, f32[112,128]{1,0:T(8,128)S(1)}, u32[]{:S(2)}, u32[]{:S(2)}) collective-permute-start(f32[112,128]{1,0:T(8,128)S(1)} %get-tuple-element.68), channel_id=1, source_target_pairs={{1,0},{2,1},{3,2},{0,3},{5,4},{6,5},{7,6},{4,7},{9,8},{10,9},{11,1... | collective-permute-start | bytes 172040 | tf_op jit(solution)/shard_map/ppermute | solution.py:44
  40.5 4.3 %collective-permute-done.11.refs_4_.refs_2_ = f32[16,128]{1,0:T(8,128)S(1)} collective-permute-done((f32[16,128]{1,0:T(8,128)S(1)}, f32[16,128]{1,0:T(8,128)S(1)}, u32[]{:S(2)}, u32[]{:S(2)}) %collective-permute-start.11) | collective-permute-done | bytes 8224 | tf_op jit(solution)/shard_map/ppermute | solution.py:44
  44.8 1.0 %collective-permute-done.12.refs_5_.refs_3_ = f32[112,128]{1,0:T(8,128)S(1)} collective-permute-done((f32[112,128]{1,0:T(8,128)S(1)}, f32[112,128]{1,0:T(8,128)S(1)}, u32[]{:S(2)}, u32[]{:S(2)}) %collective-permute-start.12) | collective-permute-done | bytes 57376 | tf_op jit(solution)/shard_map/ppermute | solution.py:44
  45.8 1.9 %step.6 = (f32[26,16,8,128]{3,2,1,0:T(8,128)S(1)}, f32[8,128]{1,0:T(8,128)S(1)}, f32[8,128]{1,0:T(8,128)S(1)}) custom-call(f32[26,16,8,128]{3,2,1,0:T(8,128)S(1)} %get-tuple-element.61.refs_0_, s32[8,128]{1,0:T(8,128)S(1)} %fusion.3.code_ref.refs_1_.refs_3_, f32[16,128]{1,0:T(8,128)S(1)} %get-tuple-element.67.refs_2_.refs_0_, ...), custom_call_target="tpu_custom_call" | custom-call | tf_op jit(solution)/shard_map/step/pallas_call | solution.py:437
  47.8 2.6 %collective-permute-start.14 = (f32[8,128]{1,0:T(8,128)S(1)}, f32[8,128]{1,0:T(8,128)S(1)}, u32[]{:S(2)}, u32[]{:S(2)}) collective-permute-start(f32[8,128]{1,0:T(8,128)S(1)} %get-tuple-element.73), channel_id=1, source_target_pairs={{4,0},{8,4},{12,8},{16,12},{20,16},{24,20},{28,24},{0,28},{5,1},{9... | collective-permute-start | bytes 12296 | tf_op jit(solution)/shard_map/ppermute | solution.py:44
  50.4 1.3 %wall.6 = (f32[128,1024]{1,0:T(8,128)S(1)}, f32[128,1024]{1,0:T(8,128)S(1)}, f32[8,128]{1,0:T(8,128)S(1)}) custom-call(f32[128,1024]{1,0:T(8,128)S(1)} %get-tuple-element.74.free_ref, f32[128,1024]{1,0:T(8,128)S(1)} %get-tuple-element.75.bound_ref, f32[128,128]{1,0:T(8,128)S(1)} %copy-done.3, f32[1,128]{1,0:T(1,128)S(1)} %bitcast.13, f32[1,128]{1,0:T(1,128)S(1)} %bitcast.17, ...), custom_call_target="tpu_custom_call" | custom-call | tf_op jit(solution)/shard_map/wall/pallas_call | solution.py:442
  52.0 2.5 %collective-permute-start.15 = (f32[112,128]{1,0:T(8,128)S(1)}, f32[112,128]{1,0:T(8,128)S(1)}, u32[]{:S(2)}, u32[]{:S(2)}) collective-permute-start(f32[112,128]{1,0:T(8,128)S(1)} %get-tuple-element.78), channel_id=1, source_target_pairs={{1,0},{2,1},{3,2},{0,3},{5,4},{6,5},{7,6},{4,7},{9,8},{10,9},{11,1... | collective-permute-start | bytes 172040 | tf_op jit(solution)/shard_map/ppermute | solution.py:44
  55.1 3.9 %collective-permute-done.16.refs_4_.refs_2_ = f32[16,128]{1,0:T(8,128)S(1)} collective-permute-done((f32[16,128]{1,0:T(8,128)S(1)}, f32[16,128]{1,0:T(8,128)S(1)}, u32[]{:S(2)}, u32[]{:S(2)}) %collective-permute-start.16) | collective-permute-done | bytes 8224 | tf_op jit(solution)/shard_map/ppermute | solution.py:44
  59.0 1.4 %collective-permute-done.17.refs_5_.refs_3_ = f32[112,128]{1,0:T(8,128)S(1)} collective-permute-done((f32[112,128]{1,0:T(8,128)S(1)}, f32[112,128]{1,0:T(8,128)S(1)}, u32[]{:S(2)}, u32[]{:S(2)}) %collective-permute-start.17) | collective-permute-done | bytes 57376 | tf_op jit(solution)/shard_map/ppermute | solution.py:44
  60.4 1.9 %step.7 = (f32[26,16,8,128]{3,2,1,0:T(8,128)S(1)}, f32[8,128]{1,0:T(8,128)S(1)}, f32[8,128]{1,0:T(8,128)S(1)}) custom-call(f32[26,16,8,128]{3,2,1,0:T(8,128)S(1)} %get-tuple-element.71.refs_0_, s32[8,128]{1,0:T(8,128)S(1)} %fusion.3.code_ref.refs_1_.refs_3_, f32[16,128]{1,0:T(8,128)S(1)} %get-tuple-element.77.refs_2_.refs_0_, ...), custom_call_target="tpu_custom_call" | custom-call | tf_op jit(solution)/shard_map/step/pallas_call | solution.py:437
  62.4 2.6 %collective-permute-start.19 = (f32[8,128]{1,0:T(8,128)S(1)}, f32[8,128]{1,0:T(8,128)S(1)}, u32[]{:S(2)}, u32[]{:S(2)}) collective-permute-start(f32[8,128]{1,0:T(8,128)S(1)} %get-tuple-element.83), channel_id=1, source_target_pairs={{4,0},{8,4},{12,8},{16,12},{20,16},{24,20},{28,24},{0,28},{5,1},{9... | collective-permute-start | bytes 12296 | tf_op jit(solution)/shard_map/ppermute | solution.py:44
  65.0 1.3 %collective-permute-done.18.refs_1_.behind_ref = f32[8,128]{1,0:T(8,128)S(1)} collective-permute-done((f32[8,128]{1,0:T(8,128)S(1)}, f32[8,128]{1,0:T(8,128)S(1)}, u32[]{:S(2)}, u32[]{:S(2)}) %collective-permute-start.18) | collective-permute-done | bytes 4128 | tf_op jit(solution)/shard_map/ppermute | solution.py:44
  66.5 0.7 collective-permute-start.20
  67.3 3.2 %collective-permute-start.21 = (f32[96,128]{1,0:T(8,128)S(1)}, f32[96,128]{1,0:T(8,128)S(1)}, u32[]{:S(2)}, u32[]{:S(2)}) collective-permute-start(f32[96,128]{1,0:T(8,128)S(1)} %get-tuple-element.85), channel_id=1, source_target_pairs={{1,0},{2,1},{3,2},{0,3},{5,4},{6,5},{7,6},{4,7},{9,8},{10,9},{11,1... | collective-permute-start | bytes 147464 | tf_op jit(solution)/shard_map/ppermute | solution.py:44
  70.4 2.3 %wall.7 = (f32[128,1024]{1,0:T(8,128)}, f32[128,1024]{1,0:T(8,128)}, f32[8,128]{1,0:T(8,128)}) custom-call(f32[128,1024]{1,0:T(8,128)S(1)} %get-tuple-element.88.free_ref, f32[128,1024]{1,0:T(8,128)S(1)} %get-tuple-element.89.bound_ref, f32[128,128]{1,0:T(8,128)S(1)} %copy-done.3, f32[1,128]{1,0:T(1,128)S(1)} %bitcast.14, f32[1,128]{1,0:T(1,128)S(1)} %bitcast.18, ...), custom_call_target="tpu_custom_call" | custom-call | tf_op jit(solution)/shard_map/wall/pallas_call | solution.py:442
  72.7 1.1 %last.1 = (f32[16,8,128]{2,1,0:T(8,128)}, f32[16,8,128]{2,1,0:T(8,128)}) custom-call(f32[26,16,8,128]{3,2,1,0:T(8,128)S(1)} %get-tuple-element.81.refs_0_.post_ref, f32[8,128]{1,0:T(8,128)S(1)} %collective-permute-done.18.refs_1_.behind_ref, f32[8,128]{1,0:T(8,128)S(1)} %collective-permute-done.19.refs_2_.ahead_ref, ...), custom_call_target="tpu_custom_call" | custom-call | tf_op jit(solution)/shard_map/last/pallas_call | solution.py:458
  (51 shorter events, 5.7 us)
Async XLA Ops:
  0.6 20.0 %copy-start.6 = (s32[1024]{0:T(1024)S(1)}, s32[1024]{0:T(1024)}, u32[]{:S(2)}) copy-start(s32[1024]{0:T(1024)} %param.17) | copy-start | bytes 12292
  0.6 20.0 %copy-start.3 = (f32[128,128]{1,0:T(8,128)S(1)}, f32[128,128]{1,0:T(8,128)}, u32[]{:S(2)}) copy-start(f32[128,128]{1,0:T(8,128)} %spread_ref.7) | copy-start | bytes 196612
  0.7 20.0 %copy-start.8 = (f32[128]{0:T(128)S(1)}, f32[128]{0:T(128)}, u32[]{:S(2)}) copy-start(f32[128]{0:T(128)} %param.14) | copy-start | bytes 1540
  0.7 20.0 %copy-start.7 = (f32[128]{0:T(128)S(1)}, f32[128]{0:T(128)}, u32[]{:S(2)}) copy-start(f32[128]{0:T(128)} %param.13) | copy-start | bytes 1540
  2.9 1.0 %copy-start = (f32[128,1024]{1,0:T(8,128)S(1)}, f32[128,1024]{1,0:T(8,128)}, u32[]{:S(2)}) copy-start(f32[128,1024]{1,0:T(8,128)} %free_ref.3) | copy-start | bytes 1572868
  3.9 0.7 copy-start.5
  4.6 16.1 %copy-start.1 = (f32[128,1024]{1,0:T(8,128)S(1)}, f32[128,1024]{1,0:T(8,128)}, u32[]{:S(2)}) copy-start(f32[128,1024]{1,0:T(8,128)} %free_ref.3) | copy-start | bytes 1572868
  4.9 9.7 %collective-permute-start = (f32[40,128]{1,0:T(8,128)S(1)}, f32[40,128]{1,0:T(8,128)S(1)}, u32[]{:S(2)}, u32[]{:S(2)}) collective-permute-start(f32[40,128]{1,0:T(8,128)S(1)} %get-tuple-element.49), channel_id=1, source_target_pairs={{1,0},{2,1},{3,2},{0,3},{5,4},{6,5},{7,6},{4,7},{9,8},{10,9},{11,1... | collective-permute-start | bytes 61448 | tf_op jit(solution)/shard_map/ppermute | solution.py:44
  10.0 5.6 %collective-permute-start.2 = (f32[40,128]{1,0:T(8,128)S(1)}, f32[40,128]{1,0:T(8,128)S(1)}, u32[]{:S(2)}, u32[]{:S(2)}) collective-permute-start(f32[40,128]{1,0:T(8,128)S(1)} %get-tuple-element.51), channel_id=1, source_target_pairs={{3,0},{0,1},{1,2},{2,3},{7,4},{4,5},{5,6},{6,7},{11,8},{8,9},{9,10... | collective-permute-start | bytes 61448 | tf_op jit(solution)/shard_map/ppermute | solution.py:44
  10.0 4.6 %collective-permute-start.1 = (f32[32,128]{1,0:T(8,128)S(1)}, f32[32,128]{1,0:T(8,128)S(1)}, u32[]{:S(2)}, u32[]{:S(2)}) collective-permute-start(f32[32,128]{1,0:T(8,128)S(1)} %get-tuple-element.50), channel_id=1, source_target_pairs={{2,0},{3,1},{0,2},{1,3},{6,4},{7,5},{4,6},{5,7},{10,8},{11,9},{8,1... | collective-permute-start | bytes 49160 | tf_op jit(solution)/shard_map/ppermute | solution.py:44
  15.6 1.5 %copy-start.2 = (f32[26,16,8,128]{3,2,1,0:T(8,128)S(1)}, f32[26,16,8,128]{3,2,1,0:T(8,128)}, u32[]{:S(2)}) copy-start(f32[26,16,8,128]{3,2,1,0:T(8,128)} %refs_0_.1) | copy-start | bytes 5111812
  17.0 3.7 %copy-start.4 = (f32[128,1024]{1,0:T(8,128)S(1)}, f32[128,1024]{1,0:T(8,128)}, u32[]{:S(2)}) copy-start(f32[128,1024]{1,0:T(8,128)} %bound_ref.1) | copy-start | bytes 1572868
  17.9 4.1 %collective-permute-start.3 = (f32[8,128]{1,0:T(8,128)S(1)}, f32[8,128]{1,0:T(8,128)S(1)}, u32[]{:S(2)}, u32[]{:S(2)}) collective-permute-start(f32[8,128]{1,0:T(8,128)S(1)} %get-tuple-element.53), channel_id=1, source_target_pairs={{28,0},{0,4},{4,8},{8,12},{12,16},{16,20},{20,24},{24,28},{29,1},{... | collective-permute-start | bytes 12296 | tf_op jit(solution)/shard_map/ppermute | solution.py:44
  17.9 4.1 %collective-permute-start.4 = (f32[8,128]{1,0:T(8,128)S(1)}, f32[8,128]{1,0:T(8,128)S(1)}, u32[]{:S(2)}, u32[]{:S(2)}) collective-permute-start(f32[8,128]{1,0:T(8,128)S(1)} %get-tuple-element.54), channel_id=1, source_target_pairs={{4,0},{8,4},{12,8},{16,12},{20,16},{24,20},{28,24},{0,28},{5,1},{9... | collective-permute-start | bytes 12296 | tf_op jit(solution)/shard_map/ppermute | solution.py:44
  22.3 7.5 %collective-permute-start.5 = (f32[112,128]{1,0:T(8,128)S(1)}, f32[112,128]{1,0:T(8,128)S(1)}, u32[]{:S(2)}, u32[]{:S(2)}) collective-permute-start(f32[112,128]{1,0:T(8,128)S(1)} %get-tuple-element.57), channel_id=1, source_target_pairs={{1,0},{2,1},{3,2},{0,3},{5,4},{6,5},{7,6},{4,7},{9,8},{10,9},{11,1... | collective-permute-start | bytes 172040 | tf_op jit(solution)/shard_map/ppermute | solution.py:44
  25.2 6.0 %collective-permute-start.7 = (f32[112,128]{1,0:T(8,128)S(1)}, f32[112,128]{1,0:T(8,128)S(1)}, u32[]{:S(2)}, u32[]{:S(2)}) collective-permute-start(f32[112,128]{1,0:T(8,128)S(1)} %get-tuple-element.59), channel_id=1, source_target_pairs={{3,0},{0,1},{1,2},{2,3},{7,4},{4,5},{5,6},{6,7},{11,8},{8,9},{9,10... | collective-permute-start | bytes 172040 | tf_op jit(solution)/shard_map/ppermute | solution.py:44
  25.2 4.5 %collective-permute-start.6 = (f32[16,128]{1,0:T(8,128)S(1)}, f32[16,128]{1,0:T(8,128)S(1)}, u32[]{:S(2)}, u32[]{:S(2)}) collective-permute-start(f32[16,128]{1,0:T(8,128)S(1)} %get-tuple-element.58), channel_id=1, source_target_pairs={{2,0},{3,1},{0,2},{1,3},{6,4},{7,5},{4,6},{5,7},{10,8},{11,9},{8,1... | collective-permute-start | bytes 24584 | tf_op jit(solution)/shard_map/ppermute | solution.py:44
  33.1 4.0 %collective-permute-start.8 = (f32[8,128]{1,0:T(8,128)S(1)}, f32[8,128]{1,0:T(8,128)S(1)}, u32[]{:S(2)}, u32[]{:S(2)}) collective-permute-start(f32[8,128]{1,0:T(8,128)S(1)} %get-tuple-element.62), channel_id=1, source_target_pairs={{28,0},{0,4},{4,8},{8,12},{12,16},{16,20},{20,24},{24,28},{29,1},{... | collective-permute-start | bytes 12296 | tf_op jit(solution)/shard_map/ppermute | solution.py:44
  33.1 4.0 %collective-permute-start.9 = (f32[8,128]{1,0:T(8,128)S(1)}, f32[8,128]{1,0:T(8,128)S(1)}, u32[]{:S(2)}, u32[]{:S(2)}) collective-permute-start(f32[8,128]{1,0:T(8,128)S(1)} %get-tuple-element.63), channel_id=1, source_target_pairs={{4,0},{8,4},{12,8},{16,12},{20,16},{24,20},{28,24},{0,28},{5,1},{9... | collective-permute-start | bytes 12296 | tf_op jit(solution)/shard_map/ppermute | solution.py:44
  37.4 7.4 %collective-permute-start.10 = (f32[112,128]{1,0:T(8,128)S(1)}, f32[112,128]{1,0:T(8,128)S(1)}, u32[]{:S(2)}, u32[]{:S(2)}) collective-permute-start(f32[112,128]{1,0:T(8,128)S(1)} %get-tuple-element.68), channel_id=1, source_target_pairs={{1,0},{2,1},{3,2},{0,3},{5,4},{6,5},{7,6},{4,7},{9,8},{10,9},{11,1... | collective-permute-start | bytes 172040 | tf_op jit(solution)/shard_map/ppermute | solution.py:44
  39.9 6.0 %collective-permute-start.12 = (f32[112,128]{1,0:T(8,128)S(1)}, f32[112,128]{1,0:T(8,128)S(1)}, u32[]{:S(2)}, u32[]{:S(2)}) collective-permute-start(f32[112,128]{1,0:T(8,128)S(1)} %get-tuple-element.70), channel_id=1, source_target_pairs={{3,0},{0,1},{1,2},{2,3},{7,4},{4,5},{5,6},{6,7},{11,8},{8,9},{9,10... | collective-permute-start | bytes 172040 | tf_op jit(solution)/shard_map/ppermute | solution.py:44
  39.9 4.9 %collective-permute-start.11 = (f32[16,128]{1,0:T(8,128)S(1)}, f32[16,128]{1,0:T(8,128)S(1)}, u32[]{:S(2)}, u32[]{:S(2)}) collective-permute-start(f32[16,128]{1,0:T(8,128)S(1)} %get-tuple-element.69), channel_id=1, source_target_pairs={{2,0},{3,1},{0,2},{1,3},{6,4},{7,5},{4,6},{5,7},{10,8},{11,9},{8,1... | collective-permute-start | bytes 24584 | tf_op jit(solution)/shard_map/ppermute | solution.py:44
  47.7 4.0 %collective-permute-start.13 = (f32[8,128]{1,0:T(8,128)S(1)}, f32[8,128]{1,0:T(8,128)S(1)}, u32[]{:S(2)}, u32[]{:S(2)}) collective-permute-start(f32[8,128]{1,0:T(8,128)S(1)} %get-tuple-element.72), channel_id=1, source_target_pairs={{28,0},{0,4},{4,8},{8,12},{12,16},{16,20},{20,24},{24,28},{29,1},{... | collective-permute-start | bytes 12296 | tf_op jit(solution)/shard_map/ppermute | solution.py:44
  47.8 4.0 %collective-permute-start.14 = (f32[8,128]{1,0:T(8,128)S(1)}, f32[8,128]{1,0:T(8,128)S(1)}, u32[]{:S(2)}, u32[]{:S(2)}) collective-permute-start(f32[8,128]{1,0:T(8,128)S(1)} %get-tuple-element.73), channel_id=1, source_target_pairs={{4,0},{8,4},{12,8},{16,12},{20,16},{24,20},{28,24},{0,28},{5,1},{9... | collective-permute-start | bytes 12296 | tf_op jit(solution)/shard_map/ppermute | solution.py:44
  52.0 7.0 %collective-permute-start.15 = (f32[112,128]{1,0:T(8,128)S(1)}, f32[112,128]{1,0:T(8,128)S(1)}, u32[]{:S(2)}, u32[]{:S(2)}) collective-permute-start(f32[112,128]{1,0:T(8,128)S(1)} %get-tuple-element.78), channel_id=1, source_target_pairs={{1,0},{2,1},{3,2},{0,3},{5,4},{6,5},{7,6},{4,7},{9,8},{10,9},{11,1... | collective-permute-start | bytes 172040 | tf_op jit(solution)/shard_map/ppermute | solution.py:44
  54.5 6.0 %collective-permute-start.17 = (f32[112,128]{1,0:T(8,128)S(1)}, f32[112,128]{1,0:T(8,128)S(1)}, u32[]{:S(2)}, u32[]{:S(2)}) collective-permute-start(f32[112,128]{1,0:T(8,128)S(1)} %get-tuple-element.80), channel_id=1, source_target_pairs={{3,0},{0,1},{1,2},{2,3},{7,4},{4,5},{5,6},{6,7},{11,8},{8,9},{9,10... | collective-permute-start | bytes 172040 | tf_op jit(solution)/shard_map/ppermute | solution.py:44
  54.5 4.5 %collective-permute-start.16 = (f32[16,128]{1,0:T(8,128)S(1)}, f32[16,128]{1,0:T(8,128)S(1)}, u32[]{:S(2)}, u32[]{:S(2)}) collective-permute-start(f32[16,128]{1,0:T(8,128)S(1)} %get-tuple-element.79), channel_id=1, source_target_pairs={{2,0},{3,1},{0,2},{1,3},{6,4},{7,5},{4,6},{5,7},{10,8},{11,9},{8,1... | collective-permute-start | bytes 24584 | tf_op jit(solution)/shard_map/ppermute | solution.py:44
  62.3 4.0 %collective-permute-start.18 = (f32[8,128]{1,0:T(8,128)S(1)}, f32[8,128]{1,0:T(8,128)S(1)}, u32[]{:S(2)}, u32[]{:S(2)}) collective-permute-start(f32[8,128]{1,0:T(8,128)S(1)} %get-tuple-element.82), channel_id=1, source_target_pairs={{28,0},{0,4},{4,8},{8,12},{12,16},{16,20},{20,24},{24,28},{29,1},{... | collective-permute-start | bytes 12296 | tf_op jit(solution)/shard_map/ppermute | solution.py:44
  62.4 4.0 %collective-permute-start.19 = (f32[8,128]{1,0:T(8,128)S(1)}, f32[8,128]{1,0:T(8,128)S(1)}, u32[]{:S(2)}, u32[]{:S(2)}) collective-permute-start(f32[8,128]{1,0:T(8,128)S(1)} %get-tuple-element.83), channel_id=1, source_target_pairs={{4,0},{8,4},{12,8},{16,12},{20,16},{24,20},{28,24},{0,28},{5,1},{9... | collective-permute-start | bytes 12296 | tf_op jit(solution)/shard_map/ppermute | solution.py:44
  66.5 6.2 %collective-permute-start.20 = (f32[96,128]{1,0:T(8,128)S(1)}, f32[96,128]{1,0:T(8,128)S(1)}, u32[]{:S(2)}, u32[]{:S(2)}) collective-permute-start(f32[96,128]{1,0:T(8,128)S(1)} %get-tuple-element.84), channel_id=1, source_target_pairs={{3,0},{0,1},{1,2},{2,3},{7,4},{4,5},{5,6},{6,7},{11,8},{8,9},{9,10... | collective-permute-start | bytes 147464 | tf_op jit(solution)/shard_map/ppermute | solution.py:44
  67.3 5.5 %collective-permute-start.21 = (f32[96,128]{1,0:T(8,128)S(1)}, f32[96,128]{1,0:T(8,128)S(1)}, u32[]{:S(2)}, u32[]{:S(2)}) collective-permute-start(f32[96,128]{1,0:T(8,128)S(1)} %get-tuple-element.85), channel_id=1, source_target_pairs={{1,0},{2,1},{3,2},{0,3},{5,4},{6,5},{7,6},{4,7},{9,8},{10,9},{11,1... | collective-permute-start | bytes 147464 | tf_op jit(solution)/shard_map/ppermute | solution.py:44
where the time goes:
time: 74.2 us; the launch traced here: 73.8 us
  starting transfers between devices  30.5 us (41%)
  waiting for transfers between devices  21.9 us (30%)
  Pallas kernels  15.1 us (20%)
  local copies, waits for them, and re-layouts  3.99 us (5%)
  other arithmetic  1.42 us (2%)
  between operations  0.88 us (1%)
    ppermute x22, starting transfers between devices, shifted(): lax.ppermute(block, axis, [((i - distance) % count, i) for i in range(cou...  30.5 us
    ppermute x22, waiting for transfers between devices, shifted(): lax.ppermute(block, axis, [((i - distance) % count, i) for i in range(cou...  21.9 us
    pallas_call x4, Pallas kernels, per_device(): kernel_call(functools.partial(step_kernel, sectors, first), 'step', outs,...  6.44 us
    pallas_call x4, Pallas kernels, per_device(): kernel_call(functools.partial(wall_kernel, sectors), 'wall', [wall_free.s...  6.22 us
    unnamed x18, local copies, waits for them, and re-layouts  3.21 us
  transfers between devices with their start and end apart: 22, of which 9 were waited for; matrix products, arithmetic and copies ran while one was open for 0% of the time, Pallas kernels for 8%

commit v1 on v0

v1 whole, which is shorter than its diff:
```python
import functools

import jax
import jax.numpy as jnp
from jax import lax
from jax.experimental import pallas as pl
from jax.experimental.pallas import tpu as pltpu
from jax.sharding import PartitionSpec as P

STEPS = 4
SUB = 2

VELOCITIES = [
    (0, 0, 0), (1, 0, 0), (-1, 0, 0), (0, 1, 0), (0, -1, 0), (0, 0, 1), (0, 0, -1),
    (1, 1, 0), (-1, -1, 0), (1, -1, 0), (-1, 1, 0),
    (1, 0, 1), (-1, 0, -1), (1, 0, -1), (-1, 0, 1),
    (0, 1, 1), (0, -1, -1), (0, 1, -1), (0, -1, 1),
    (0, 0, 0), (1, 0, 0), (-1, 0, 0), (0, 1, 0), (0, -1, 0), (0, 0, 1), (0, 0, -1),
]
WEIGHTS = [1.0 / 3.0] + [1.0 / 18.0] * 6 + [1.0 / 36.0] * 12 + [0.25] + [0.125] * 6
OPPOSITE = [0, 2, 1, 4, 3, 6, 5, 8, 7, 10, 9, 12, 11, 14, 13, 16, 15, 18, 17, 19, 21, 20, 23, 22, 25, 24]
MIRROR = [0, 1, 2, 3, 4, 6, 5, 7, 8, 9, 10, 13, 14, 11, 12, 17, 18, 15, 16, 19, 20, 21, 22, 23, 25, 24]
SECTOR_RISING = [3, 7, 10, 15, 17, 22]
SECTOR_FALLING = [4, 8, 9, 16, 18, 23]
SLAB_RISING = [1, 7, 9, 11, 13, 20]
SLAB_FALLING = [2, 8, 10, 12, 14, 21]
PAIRS = [(1, 2), (3, 4), (5, 6), (7, 8), (9, 10), (11, 12), (13, 14), (15, 16), (17, 18)]
FLOWS = 19
MEMBERS = 26
RELAX_FLOW = 1.25
RELAX_DRUG = 1.1
PUSH_AXIAL = 0.0001
PERMEABILITY = 0.3
RELEASE_RATE = 0.5

F32 = jnp.float32
BF16 = jnp.bfloat16
VMEM = pltpu.VMEM


def shifted(block, axis, distance):
    count = lax.axis_size(axis)
    return lax.ppermute(block, axis, [((i - distance) % count, i) for i in range(count)])


def lanes(shape):
    return lax.broadcasted_iota(jnp.int32, shape, len(shape) - 1)


def sublanes(shape):
    return lax.broadcasted_iota(jnp.int32, shape, len(shape) - 2)


def split3(value):
    high = value.astype(BF16)
    rest = value - high.astype(F32)
    middle = rest.astype(BF16)
    low = (rest - middle.astype(F32)).astype(BF16)
    return high, middle, low


def one_hot_lines(low_row, width):
    shape = (width, low_row.shape[-1])
    return jnp.where(sublanes(shape) == low_row, 1.0, 0.0).astype(BF16)


def scatter_rows(value_rows, code_rows, groups, width):
    terms, hots = [], []
    for value, code in zip(value_rows, code_rows, strict=True):
        group = code // width
        shape = (groups, value.shape[-1])
        hit = sublanes(shape) == group
        terms.append(jnp.concatenate([jnp.where(hit, part.astype(F32), 0.0) for part in split3(value)], axis=0).astype(BF16))
        hots.append(one_hot_lines(code - group * width, width))
    left = jnp.concatenate(terms, axis=1)
    right = jnp.concatenate(hots, axis=1)
    total = lax.dot_general(left, right, (((1,), (1,)), ((), ())), preferred_element_type=F32)
    return total[:groups] + total[groups:2 * groups] + total[2 * groups:3 * groups]


def gather_rows(table, code_rows, width):
    groups = table.shape[0]
    left = jnp.concatenate(split3(table), axis=0)
    lows = [code - (code // width) * width for code in code_rows]
    right = jnp.concatenate([one_hot_lines(low, width) for low in lows], axis=1)
    picked = jnp.dot(left, right, preferred_element_type=F32)
    picked = picked[:groups] + picked[groups:2 * groups] + picked[2 * groups:3 * groups]
    results, start = [], 0
    for code in code_rows:
        count = code.shape[-1]
        hit = sublanes((groups, count)) == code // width
        results.append(jnp.sum(jnp.where(hit, picked[:, start:start + count], 0.0), axis=0, keepdims=True))
        start += count
    return results


def source_plane(member, level, radial):
    step_r = VELOCITIES[member][2]
    if step_r == 1:
        return ((MIRROR[member], 0) if level == 0 else (member, level - 1)), True
    if step_r == -1:
        return ((OPPOSITE[member], radial - 1), False) if level == radial - 1 else ((member, level + 1), True)
    return (member, level), True


class Planes:
    def __init__(self, ref, radial, across):
        self.ref, self.radial, self.across = ref, radial, across

    def base(self, member, level):
        return (member * self.radial + level) * self.across

    def get(self, member, level):
        return self.ref[pl.ds(self.base(member, level), self.across), :]

    def put(self, member, level, value):
        self.ref[pl.ds(self.base(member, level), self.across), :] = value

    def rows(self, member, level, count, row):
        return self.ref[pl.ds(self.base(member, level) + row, count, stride=self.across), :]

    def put_rows(self, member, level, count, row, value):
        self.ref[pl.ds(self.base(member, level) + row, count, stride=self.across), :] = value


def axial_shift(value, step, member, level, radial, behind, ahead):
    along = value.shape[-1]
    lane = lanes(value.shape)
    if step == 1:
        slot = SLAB_RISING.index(member) * radial + level
        return jnp.where(lane == 0, pltpu.roll(behind, (-slot) % along, 1), pltpu.roll(value, 1, 1))
    slot = SLAB_FALLING.index(member) * radial + level
    return jnp.where(lane == along - 1, pltpu.roll(ahead, (along - 1 - slot) % along, 1), pltpu.roll(value, along - 1, 1))


def streamed(post, member, level, behind, ahead):
    radial, across = post.radial, post.across
    (origin, depth), moves = source_plane(member, level, radial)
    value = post.get(origin, depth)
    if not moves:
        return value
    step_z, step_s, _ = VELOCITIES[member]
    if step_z:
        value = axial_shift(value, step_z, origin, depth, radial, behind, ahead)
    if step_s:
        value = pltpu.roll(value, step_s % across, 0)
    return value


def incoming_rows(box, start, places, state, member, level, count, row):
    radial = state.radial
    step_r = VELOCITIES[member][2]
    here = start + places.index(member) * radial + level
    value = box[here - step_r:here - step_r + count, :]
    if step_r == 1 and level == 0:
        mirrored = start + places.index(MIRROR[member]) * radial
        value = jnp.where(sublanes(value.shape) == 0, box[mirrored:mirrored + 1, :], value)
    if step_r == -1 and level + count == radial:
        value = jnp.where(sublanes(value.shape) == count - 1, state.rows(member, level, count, row), value)
    return value


def relax_flow(members):
    def total(component):
        up, down = None, None
        for member in range(1, FLOWS):
            factor = VELOCITIES[member][component]
            if factor > 0:
                up = members[member] if up is None else up + members[member]
            elif factor < 0:
                down = members[member] if down is None else down + members[member]
        return up - down

    density = members[0]
    for member in range(1, FLOWS):
        density = density + members[member]
    inverse = 1.0 / density
    velocity = [(total(0) + PUSH_AXIAL) * inverse, total(1) * inverse, total(2) * inverse]
    speed_sq = velocity[0] * velocity[0] + velocity[1] * velocity[1] + velocity[2] * velocity[2]
    base = 1.0 - 1.5 * speed_sq
    weighted = {}
    for weight in sorted(set(WEIGHTS[:FLOWS])):
        weighted[weight] = (RELAX_FLOW * weight) * density

    def projected(member):
        result = None
        for component in range(3):
            factor = VELOCITIES[member][component]
            if factor == 0:
                continue
            if result is None:
                result = velocity[component] if factor > 0 else -velocity[component]
            else:
                result = result + velocity[component] if factor > 0 else result - velocity[component]
        return result

    results = [None] * FLOWS
    results[0] = (1.0 - RELAX_FLOW) * members[0] + weighted[WEIGHTS[0]] * base
    for first, second in PAIRS:
        along = projected(first)
        even = weighted[WEIGHTS[first]] * (base + 4.5 * along * along)
        odd = weighted[WEIGHTS[first]] * (3.0 * along)
        results[first] = (1.0 - RELAX_FLOW) * members[first] + (even + odd)
        results[second] = (1.0 - RELAX_FLOW) * members[second] + (even - odd)
    return results, velocity


def relax_drug(members, velocity):
    concentration = members[0]
    for member in members[1:]:
        concentration = concentration + member
    rest = (RELAX_DRUG * WEIGHTS[FLOWS]) * concentration
    results = [(1.0 - RELAX_DRUG) * members[0] + rest]
    even = (RELAX_DRUG * WEIGHTS[FLOWS + 1]) * concentration
    for component in range(3):
        odd = even * (4.0 * velocity[component])
        results.append((1.0 - RELAX_DRUG) * members[1 + 2 * component] + (even + odd))
        results.append((1.0 - RELAX_DRUG) * members[2 + 2 * component] + (even - odd))
    return results


def code_list(codes):
    return [codes[row:row + 1, :] for row in range(codes.shape[0])]


def pack_lines(row, width):
    return jnp.concatenate([row[:, start:start + width] for start in range(0, row.shape[-1], width)], axis=0)


def first_kernel(sectors, pops_ref, sector_ref, line_ref, strut_ref, free_ref, *refs):
    code_ref, boxes = refs[0], refs[1:1 + sectors]
    drug, sector, line, strut, top, sems = refs[1 + sectors:]
    across, width = code_ref.shape
    count = drug.shape[0]
    radial = pops_ref.shape[1]
    copies = [
        pltpu.make_async_copy(pops_ref.at[FLOWS:FLOWS + count, radial - 1], drug, sems.at[0]),
        pltpu.make_async_copy(sector_ref, sector, sems.at[1]),
        pltpu.make_async_copy(line_ref, line, sems.at[2]),
        pltpu.make_async_copy(strut_ref, strut, sems.at[3]),
        pltpu.make_async_copy(free_ref.at[0:across, :], top, sems.at[4]),
    ]
    for copy in copies:
        copy.start()
    for copy in copies:
        copy.wait()
    relative = sector[...] - lax.axis_index("th")
    relative = jnp.where(relative < 0, relative + sectors, relative)
    codes = relative * (across * width) + line[...]
    code_ref[...] = codes
    surface = drug[0]
    for member in range(1, count):
        surface = surface + drug[member]
    rows = code_list(codes)
    groups = sectors * across
    sums = scatter_rows(code_list(surface), rows, groups, width)
    counts = scatter_rows(code_list(jnp.ones_like(surface)), rows, groups, width)
    first = pack_lines(top[0:1, :], width)
    openness = PERMEABILITY * (1.0 - strut[...].astype(F32))
    for rel in range(sectors):
        out = boxes[rel]
        out[0:across] = sums[rel * across:(rel + 1) * across]
        out[across:2 * across] = counts[rel * across:(rel + 1) * across]
        out[2 * across:3 * across] = first
        out[3 * across:4 * across] = openness
        if rel in (1, sectors - 1):
            edge = codes[across - 1:across] if rel == 1 else codes[0:1]
            out[4 * across:5 * across] = jnp.broadcast_to(edge, (across, width)).astype(F32)


def bulk_kernel(first, radial, across, *refs):
    if first:
        state_ref, post_ref, speed_ref = refs
    else:
        old_ref, behind_ref, ahead_ref, state_ref, post_ref, speed_ref = refs
        old = Planes(old_ref, radial, across)
        behind, ahead = behind_ref[...], ahead_ref[...]
    state, post = Planes(state_ref, radial, across), Planes(post_ref, radial, across)
    for level in range(radial):
        if first:
            members = [state.get(member, level) for member in range(MEMBERS)]
        else:
            members = [streamed(old, member, level, behind, ahead) for member in range(MEMBERS)]
            for member in range(MEMBERS):
                state.put(member, level, members[member])
        results, velocity = relax_flow(members[:FLOWS])
        if level == radial - 1:
            for component in range(3):
                speed_ref[component * across:(component + 1) * across, :] = velocity[component]
        else:
            results = results + relax_drug(members[FLOWS:], velocity)
        for member, value in enumerate(results):
            post.put(member, level, value)


def flux_kernel(sectors, first, radial, *refs):
    refs = list(refs)
    state_ref, bulk_ref, speed_ref, code_ref = refs[:4]
    inbox = refs[4:4 + sectors]
    refs = refs[4 + sectors:]
    if first:
        post_ref, rise_ref, fall_ref, open_ref, counts_ref, edges_ref = refs
    else:
        open_ref, post_ref, rise_ref, fall_ref = refs
    del bulk_ref
    across, along = code_ref.shape
    end = radial - 1
    state, post = Planes(state_ref, radial, across), Planes(post_ref, radial, across)
    codes = code_list(code_ref[...])
    offset = 2 * across if first else across
    table = jnp.concatenate([box[offset:offset + across, :] for box in inbox], axis=0)
    picked = jnp.concatenate(gather_rows(table, codes, along), axis=0)
    below, above = inbox[sectors - 1], inbox[1]
    if first:
        table = jnp.concatenate([box[3 * across:4 * across, :] for box in inbox], axis=0)
        openness = jnp.concatenate(gather_rows(table, codes, along), axis=0)
        open_ref[...] = openness
        counts = inbox[0][across:2 * across, :]
        for box in inbox[1:]:
            counts = counts + box[across:2 * across, :]
        counts_ref[...] = counts
        count, limit = across * along, sectors * across * along
        up = above[4 * across:5 * across, :].astype(jnp.int32) + count
        down = below[4 * across:5 * across, :].astype(jnp.int32) - count
        up = jnp.where(up >= limit, up - limit, up)
        down = jnp.where(down < 0, down + limit, down)
        edges_ref[...] = jnp.where(sublanes(up.shape) == 0, up, down)
    else:
        openness = open_ref[...]
    start = 2 * across
    row = sublanes((across, along))
    drugs = [state.get(member, end) for member in range(FLOWS, MEMBERS)]
    if not first:
        last = start + SECTOR_RISING.index(FLOWS + 3) * radial + end
        drugs[3] = jnp.where(row == 0, below[last:last + 1, :], drugs[3])
        last = start + SECTOR_FALLING.index(FLOWS + 4) * radial + end
        drugs[4] = jnp.where(row == across - 1, above[last:last + 1, :], drugs[4])
    surface = drugs[0]
    for drug in drugs[1:]:
        surface = surface + drug
    flux = openness * (surface - picked)
    drugs = [drug - WEIGHTS[FLOWS + place] * flux for place, drug in enumerate(drugs)]
    velocity = [speed_ref[component * across:(component + 1) * across, :] for component in range(3)]
    for place, value in enumerate(relax_drug(drugs, velocity)):
        post.put(FLOWS + place, end, value)
    if not first:
        block = across
        for side, box, places in ((0, below, SECTOR_RISING), (across - 1, above, SECTOR_FALLING)):
            moving = 1 if side == 0 else -1
            for level in range(0, radial, block):
                members = []
                for member in range(MEMBERS):
                    if VELOCITIES[member][1] == moving:
                        value = incoming_rows(box, start, places, state, member, level, block, side)
                    else:
                        value = state.rows(member, level, block, side)
                    if member >= FLOWS and level + block == radial:
                        lowered = value - WEIGHTS[member] * flux[side:side + 1, :]
                        value = jnp.where(sublanes(value.shape) == block - 1, lowered, value)
                    members.append(value)
                results, velocity = relax_flow(members[:FLOWS])
                results = results + relax_drug(members[FLOWS:], velocity)
                for member, value in enumerate(results):
                    post.put_rows(member, level, block, side, value)
    rise = jnp.zeros((across, along), F32)
    fall = jnp.zeros((across, along), F32)
    lane = lanes((across, along))
    for level in range(radial):
        for place, member in enumerate(SLAB_RISING):
            slot = place * radial + level
            rise = jnp.where(lane == slot, pltpu.roll(post.get(member, level), (slot + 1) % along, 1), rise)
        for place, member in enumerate(SLAB_FALLING):
            slot = place * radial + level
            fall = jnp.where(lane == slot, pltpu.roll(post.get(member, level), slot, 1), fall)
    rise_ref[...] = rise
    fall_ref[...] = fall


def wall_kernel(sectors, free_ref, bound_ref, spread_ref, on_ref, off_ref, strut_ref, counts_ref, *refs):
    inbox, (new_free, new_bound, top_ref) = refs[:sectors], refs[sectors:]
    across, width = strut_ref.shape
    depth = spread_ref.shape[0]
    total = inbox[0][0:across, :]
    for box in inbox[1:]:
        total = total + box[0:across, :]
    strut = strut_ref[...].astype(F32)
    first = pack_lines(free_ref[0:1, :], width)
    added = (PERMEABILITY * (1.0 - strut)) * (total - counts_ref[...] * first) + RELEASE_RATE * strut
    spread = spread_ref[...]
    rate_on = jnp.transpose(jnp.broadcast_to(on_ref[...], (depth, depth)))
    rate_off = jnp.transpose(jnp.broadcast_to(off_ref[...], (depth, depth)))
    is_top = sublanes((depth, width)) == 0
    for row in range(across):
        place = slice(row * width, (row + 1) * width)
        free = free_ref[:, place] + jnp.where(is_top, added[row:row + 1, :], 0.0)
        bound = bound_ref[:, place]
        for _ in range(SUB):
            free = jnp.dot(spread, free, precision=lax.Precision.HIGHEST, preferred_element_type=F32)
            rate = rate_on * free * (1.0 - bound) - rate_off * bound
            free = free - rate
            bound = bound + rate
        new_free[:, place] = free
        new_bound[:, place] = bound
        top_ref[row:row + 1, :] = free[0:1, :]


def send_kernel(sectors, radial, post_ref, behind_ref, ahead_ref, code_ref, edges_ref, top_ref, *outs):
    across, along = code_ref.shape
    post = Planes(post_ref, radial, across)
    behind, ahead = behind_ref[...], ahead_ref[...]
    end = radial - 1
    row = sublanes((across, along))
    surface = post.get(FLOWS, end) + post.get(FLOWS + 5, end - 1) + post.get(FLOWS + 5, end)
    surface = surface + axial_shift(post.get(FLOWS + 1, end), 1, FLOWS + 1, end, radial, behind, ahead)
    surface = surface + axial_shift(post.get(FLOWS + 2, end), -1, FLOWS + 2, end, radial, behind, ahead)
    rising = post.get(FLOWS + 3, end)
    falling = post.get(FLOWS + 4, end)
    surface = surface + jnp.where(row == 0, 0.0, pltpu.roll(rising, 1, 0))
    surface = surface + jnp.where(row == across - 1, 0.0, pltpu.roll(falling, across - 1, 0))
    values = code_list(surface) + [rising[across - 1:across, :], falling[0:1, :]]
    codes = code_list(code_ref[...]) + [edges_ref[0:1, :], edges_ref[1:2, :]]
    sums = scatter_rows(values, codes, sectors * across, along)
    top = top_ref[...]
    for rel in range(sectors):
        outs[rel][0:across] = sums[rel * across:(rel + 1) * across]
        outs[rel][across:2 * across] = top
    start = 2 * across
    for out, places, side in ((outs[1], SECTOR_RISING, across - 1), (outs[sectors - 1], SECTOR_FALLING, 0)):
        for place, member in enumerate(places):
            step = VELOCITIES[member][0]
            base = start + place * radial
            if step:
                for level in range(radial):
                    value = axial_shift(post.get(member, level), step, member, level, radial, behind, ahead)
                    out[base + level:base + level + 1, :] = value[side:side + 1, :]
            else:
                out[base:base + radial, :] = post.rows(member, 0, radial, side)


def last_send_kernel(radial, across, post_ref, behind_ref, ahead_ref, up_ref, down_ref):
    post = Planes(post_ref, radial, across)
    behind, ahead = behind_ref[...], ahead_ref[...]
    for out, drug, plus, minus, side in ((up_ref, FLOWS + 3, 7, 10, across - 1), (down_ref, FLOWS + 4, 9, 8, 0)):
        out[0:radial, :] = post.rows(drug, 0, radial, side)
        for level in range(radial):
            value = axial_shift(post.get(plus, level), 1, plus, level, radial, behind, ahead)
            value = value - axial_shift(post.get(minus, level), -1, minus, level, radial, behind, ahead)
            out[radial + level:radial + level + 1, :] = value[side:side + 1, :]


def fields_kernel(radial, across, post_ref, behind_ref, ahead_ref, drug_ref, flow_ref):
    post = Planes(post_ref, radial, across)
    behind, ahead = behind_ref[...], ahead_ref[...]
    for level in range(radial):
        def member_of(member):
            value = streamed(post, member, level, behind, ahead)
            step = VELOCITIES[member][1]
            if step:
                edge = 0 if step > 0 else across - 1
                value = jnp.where(sublanes(value.shape) == edge, 0.0, value)
            return value

        drug = member_of(FLOWS)
        for member in range(FLOWS + 1, MEMBERS):
            drug = drug + member_of(member)
        drug_ref[level] = drug
        flow = None
        for member in range(FLOWS):
            factor = VELOCITIES[member][0]
            if factor:
                value = member_of(member)
                flow = (value if factor > 0 else -value) if flow is None else (flow + value if factor > 0 else flow - value)
        flow_ref[level] = flow


def last_kernel(drug_part, flow_part, below, above, drug_ref, flow_ref):
    radial, across, along = drug_ref.shape
    row = sublanes((across, along))
    for part, out, base in ((drug_part, drug_ref, 0), (flow_part, flow_ref, radial)):
        for level in range(radial):
            place = base + level
            value = part[level] + jnp.where(row == 0, below[place:place + 1, :], 0.0)
            out[level] = value + jnp.where(row == across - 1, above[place:place + 1, :], 0.0)


def kernel_call(body, name, outs, count, micros, aliases=None):
    shapes = [out if isinstance(out, jax.ShapeDtypeStruct) else jax.ShapeDtypeStruct(out, F32) for out in outs]
    return pl.pallas_call(
        body,
        name=name,
        out_shape=shapes,
        in_specs=[pl.BlockSpec(memory_space=VMEM)] * count,
        out_specs=[pl.BlockSpec(memory_space=VMEM)] * len(outs),
        input_output_aliases=aliases or {},
        cost_estimate=pl.CostEstimate(flops=0, bytes_accessed=int(micros * 3.0e6), transcendentals=0),
        compiler_params=pltpu.CompilerParams(vmem_limit_bytes=24 * 1024 * 1024),
    )


def first_call(sectors, populations, sector, line, strut, free):
    members, radial, across, along = populations.shape
    plane = (across, along)
    sizes = [((5 if hop in (1, sectors - 1) else 4) * across, along) for hop in range(sectors)]
    return pl.pallas_call(
        functools.partial(first_kernel, sectors),
        name="first",
        out_shape=[jax.ShapeDtypeStruct(plane, jnp.int32)] + [jax.ShapeDtypeStruct(size, F32) for size in sizes],
        in_specs=[pl.BlockSpec(memory_space=pltpu.HBM)] * 5,
        out_specs=[pl.BlockSpec(memory_space=VMEM)] * (1 + sectors),
        scratch_shapes=[
            VMEM((members - FLOWS, across, along), F32),
            VMEM(plane, jnp.int32),
            VMEM(plane, jnp.int32),
            VMEM(plane, jnp.int32),
            VMEM((across, free.shape[1]), F32),
            pltpu.SemaphoreType.DMA((5,)),
        ],
    )(populations, sector, line, strut, free)


def per_device(populations, wall_free, wall_bound, wall_propagator, bind_on, bind_off, iface_sector, iface_line, strut_mask):
    members, radial, across, along = populations.shape
    sectors = lax.axis_size("th")
    plane = (across, along)
    flat = (members * radial * across, along)
    rims = len(SECTOR_RISING) * radial
    strut = strut_mask.reshape(plane)
    rate_on = bind_on.reshape(1, -1)
    rate_off = bind_off.reshape(1, -1)

    def exchange(boxes):
        inbox = [boxes[0]] + [None] * (sectors - 1)
        for hop in range(1, sectors):
            inbox[sectors - hop] = shifted(boxes[hop], "th", hop)
        return inbox

    codes, *boxes = first_call(sectors, populations, iface_sector.reshape(plane), iface_line.reshape(plane), strut, wall_free)
    inbox = exchange(boxes)
    state = populations.reshape(flat)
    speeds = (3 * across, along)
    bulk, speed = kernel_call(functools.partial(bulk_kernel, True, radial, across), "bulk", [flat, speeds], 1, 1.5)(state)
    free, bound = wall_free, wall_bound
    openness = counts = edges = None
    for step in range(STEPS):
        first, last = step == 0, step == STEPS - 1
        outs = [flat, plane, plane]
        if first:
            outs = outs + [plane, plane, jax.ShapeDtypeStruct(plane, jnp.int32)]
        extra = [] if first else [openness]
        results = kernel_call(
            functools.partial(flux_kernel, sectors, first, radial), "flux", outs, 4 + sectors + len(extra), 0.8, {1: 0}
        )(state, bulk, speed, codes, *inbox, *extra)
        post, rise, fall = results[:3]
        if first:
            openness, counts, edges = results[3:]
        behind = shifted(rise, "ax", 1)
        ahead = shifted(fall, "ax", -1)
        free, bound, top = kernel_call(
            functools.partial(wall_kernel, sectors), "wall", [wall_free.shape, wall_free.shape, plane], 7 + sectors, 1.3
        )(free, bound, wall_propagator, rate_on, rate_off, strut, counts, *inbox)
        if last:
            continue
        sizes = [(2 * across + (rims if hop in (1, sectors - 1) else 0), along) for hop in range(sectors)]
        boxes = kernel_call(functools.partial(send_kernel, sectors, radial), "send", sizes, 6, 0.3)(
            post, behind, ahead, codes, edges, top
        )
        inbox = exchange(boxes)
        state, bulk, speed = kernel_call(
            functools.partial(bulk_kernel, False, radial, across), "bulk", [flat, flat, speeds], 3, 2.0
        )(post, behind, ahead)
    up, down = kernel_call(
        functools.partial(last_send_kernel, radial, across), "send", [(2 * radial, along)] * 2, 3, 0.2
    )(post, behind, ahead)
    below, above = shifted(up, "th", 1), shifted(down, "th", -1)
    parts = kernel_call(
        functools.partial(fields_kernel, radial, across), "fields", [(radial,) + plane] * 2, 3, 1.0
    )(post, behind, ahead)
    drug_field, axial_flow = kernel_call(last_kernel, "last", [(radial,) + plane] * 2, 4, 0.3)(*parts, below, above)
    return drug_field, axial_flow, free, bound


def solution(mesh):
    placed = (
        P(None, None, "th", "ax"),
        P(None, ("ax", "th")),
        P(None, ("ax", "th")),
        P(),
        P(),
        P(),
        P(("ax", "th"), None),
        P(("ax", "th")),
        P(("ax", "th")),
    )
    return jax.shard_map(
        per_device,
        mesh=mesh,
        in_specs=placed,
        out_specs=(
            P(None, "th", "ax"),
            P(None, "th", "ax"),
            P(None, ("ax", "th")),
            P(None, ("ax", "th")),
        ),
        check_vma=False,
    )
```

time: 74.2 us -> 65.9 us (0.89)
  local copies, waits for them, and re-layouts: 3.99 us -> 0.05 us
  waiting for transfers between devices: 21.9 us -> 19.3 us
  other arithmetic: 1.42 us -> 0 us
    unnamed x18, local copies, waits for them, and re-layouts: 3.21 us -> 0.05 us
    ppermute x22, waiting for transfers between devices: 21.9 us -> 19.3 us  [shifted(): lax.ppermute(block, axis, [((i - distance) % count, i) for i in range(cou...]
    slice x1 -> x0, local copies, waits for them, and re-layouts: 0.79 us -> none  [per_device(): drug = populations[FLOWS:, radial - 1:]]
    pallas_call x10 -> x15, Pallas kernels: 8.89 us -> 8.81 us  [the longest x3 2.28 us: per_device(): kernel_call(functools.partial(bulk_kernel, False, radial, across), 'bulk'...]
  transfers between devices with their start and end apart: 22 -> 22, of which waited for: 9 -> 9; matrix products, arithmetic and copies ran while one was open for 0% -> 0% of each run, Pallas kernels for 8% -> 15%
where the time goes in v1:
time: 65.9 us; the launch traced here: 65.8 us
  starting transfers between devices  30.4 us (46%)
  waiting for transfers between devices  19.3 us (29%)
  Pallas kernels  15 us (23%)
  between operations  0.93 us (1%)
    ppermute x22, starting transfers between devices, shifted(): lax.ppermute(block, axis, [((i - distance) % count, i) for i in range(cou...  30.4 us
    ppermute x22, waiting for transfers between devices, shifted(): lax.ppermute(block, axis, [((i - distance) % count, i) for i in range(cou...  19.3 us
    pallas_call x4, Pallas kernels, per_device(): kernel_call(functools.partial(wall_kernel, sectors), 'wall', [wall_free.s...  6.21 us
    pallas_call x3, Pallas kernels, per_device(): kernel_call(functools.partial(bulk_kernel, False, radial, across), 'bulk'...  2.28 us
    pallas_call x1, Pallas kernels, first_call(): pl.pallas_call(functools.partial(first_kernel, sectors), name='first', ou...  1.93 us
    pallas_call x4, Pallas kernels, per_device(): kernel_call(functools.partial(flux_kernel, sectors, first, radial), 'flux...  1.82 us
  transfers between devices with their start and end apart: 22, of which 9 were waited for; matrix products, arithmetic and copies ran while one was open for 0% of the time, Pallas kernels for 15%

profile of v1, /device:TPU:0, one launch (start us, length us, event | category | flops | bytes accessed | tf_op | source)
XLA Modules:
  0.0 65.8 jit_solution(16380755753134079321)
XLA Ops:
  0.6 1.9 %first.1 = (s32[8,128]{1,0:T(8,128)}, f32[32,128]{1,0:T(8,128)}, f32[40,128]{1,0:T(8,128)}, f32[32,128]{1,0:T(8,128)}, f32[40,128]{1,0:T(8,128)}) custom-call(f32[26,16,8,128]{3,2,1,0:T(8,128)} %pops_ref.1, s32[8,128]{1,0:T(8,128)} %bitcast.21, s32[8,128]{1,0:T(8,128)} %bitcast.22, s32[8,128]{1,0:T(8,128)} %bitcast.8, f32[128,1024]{1,0:T(8,128)} %free_ref.3), custom_call_target="tpu_custom_call" | custom-call | tf_op jit(solution)/shard_map/first/pallas_call | solution.py:504
  2.6 5.1 %collective-permute-start = (f32[40,128]{1,0:T(8,128)}, f32[40,128]{1,0:T(8,128)S(1)}, u32[]{:S(2)}, u32[]{:S(2)}) collective-permute-start(f32[40,128]{1,0:T(8,128)} %get-tuple-element.68), channel_id=1, source_target_pairs={{1,0},{2,1},{3,2},{0,3},{5,4},{6,5},{7,6},{4,7},{9,8},{10,9},{11,1... | collective-permute-start | bytes 61448 | tf_op jit(solution)/shard_map/ppermute | solution.py:43
  7.7 1.0 %collective-permute-start.1 = (f32[32,128]{1,0:T(8,128)}, f32[32,128]{1,0:T(8,128)S(1)}, u32[]{:S(2)}, u32[]{:S(2)}) collective-permute-start(f32[32,128]{1,0:T(8,128)} %get-tuple-element.69), channel_id=1, source_target_pairs={{2,0},{3,1},{0,2},{1,3},{6,4},{7,5},{4,6},{5,7},{10,8},{11,9},{8,1... | collective-permute-start | bytes 49160 | tf_op jit(solution)/shard_map/ppermute | solution.py:43
  9.4 3.2 %collective-permute-done.1.refs_6_.refs_2_ = f32[32,128]{1,0:T(8,128)S(1)} collective-permute-done((f32[32,128]{1,0:T(8,128)}, f32[32,128]{1,0:T(8,128)S(1)}, u32[]{:S(2)}, u32[]{:S(2)}) %collective-permute-start.1) | collective-permute-done | bytes 16416 | tf_op jit(solution)/shard_map/ppermute | solution.py:43
  12.6 0.9 %collective-permute-done.2.refs_7_.refs_3_ = f32[40,128]{1,0:T(8,128)S(1)} collective-permute-done((f32[40,128]{1,0:T(8,128)}, f32[40,128]{1,0:T(8,128)S(1)}, u32[]{:S(2)}, u32[]{:S(2)}) %collective-permute-start.2) | collective-permute-done | bytes 20512 | tf_op jit(solution)/shard_map/ppermute | solution.py:43
  14.0 2.6 %collective-permute-start.4 = (f32[8,128]{1,0:T(8,128)S(1)}, f32[8,128]{1,0:T(8,128)S(1)}, u32[]{:S(2)}, u32[]{:S(2)}) collective-permute-start(f32[8,128]{1,0:T(8,128)S(1)} %get-tuple-element.73), channel_id=1, source_target_pairs={{4,0},{8,4},{12,8},{16,12},{20,16},{24,20},{28,24},{0,28},{5,1},{9... | collective-permute-start | bytes 12296 | tf_op jit(solution)/shard_map/ppermute | solution.py:43
  16.7 1.3 %wall.4 = (f32[128,1024]{1,0:T(8,128)S(1)}, f32[128,1024]{1,0:T(8,128)S(1)}, f32[8,128]{1,0:T(8,128)S(1)}) custom-call(f32[128,1024]{1,0:T(8,128)S(1)} %copy-done.1, f32[128,1024]{1,0:T(8,128)S(1)} %copy-done.3, f32[128,128]{1,0:T(8,128)S(1)} %copy-done.2, f32[1,128]{1,0:T(1,128)S(1)} %bitcast.13, f32[1,128]{1,0:T(1,128)S(1)} %bitcast.17, ...), custom_call_target="tpu_custom_call" | custom-call | bytes 3900000 | tf_op jit(solution)/shard_map/wall/pallas_call | solution.py:558
  18.3 3.0 %collective-permute-start.5 = (f32[112,128]{1,0:T(8,128)S(1)}, f32[112,128]{1,0:T(8,128)S(1)}, u32[]{:S(2)}, u32[]{:S(2)}) collective-permute-start(f32[112,128]{1,0:T(8,128)S(1)} %get-tuple-element.81), channel_id=1, source_target_pairs={{1,0},{2,1},{3,2},{0,3},{5,4},{6,5},{7,6},{4,7},{9,8},{10,9},{11,1... | collective-permute-start | bytes 172040 | tf_op jit(solution)/shard_map/ppermute | solution.py:43
  21.3 0.6 collective-permute-start.6
  21.9 0.8 %bulk.5 = (f32[3328,128]{1,0:T(8,128)S(1)}, f32[3328,128]{1,0:T(8,128)S(1)}, f32[24,128]{1,0:T(8,128)S(1)}) custom-call(f32[3328,128]{1,0:T(8,128)S(1)} %get-tuple-element.71.refs_0_.post_ref, f32[8,128]{1,0:T(8,128)S(1)} %collective-permute-done.3.refs_1_.behind_ref, f32[8,128]{1,0:T(8,128)S(1)} %collective-permute-done.4.refs_2_.ahead_ref), custom_call_target="tpu_custom_call" | custom-call | bytes 6000000 | tf_op jit(solution)/shard_map/bulk/pallas_call | solution.py:568
  22.7 3.2 %collective-permute-done.6.refs_6_.refs_2_ = f32[16,128]{1,0:T(8,128)S(1)} collective-permute-done((f32[16,128]{1,0:T(8,128)S(1)}, f32[16,128]{1,0:T(8,128)S(1)}, u32[]{:S(2)}, u32[]{:S(2)}) %collective-permute-start.6) | collective-permute-done | bytes 8224 | tf_op jit(solution)/shard_map/ppermute | solution.py:43
  25.8 1.5 %collective-permute-done.7.refs_7_.refs_3_ = f32[112,128]{1,0:T(8,128)S(1)} collective-permute-done((f32[112,128]{1,0:T(8,128)S(1)}, f32[112,128]{1,0:T(8,128)S(1)}, u32[]{:S(2)}, u32[]{:S(2)}) %collective-permute-start.7) | collective-permute-done | bytes 57376 | tf_op jit(solution)/shard_map/ppermute | solution.py:43
  27.9 2.6 %collective-permute-start.9 = (f32[8,128]{1,0:T(8,128)S(1)}, f32[8,128]{1,0:T(8,128)S(1)}, u32[]{:S(2)}, u32[]{:S(2)}) collective-permute-start(f32[8,128]{1,0:T(8,128)S(1)} %get-tuple-element.87), channel_id=1, source_target_pairs={{4,0},{8,4},{12,8},{16,12},{20,16},{24,20},{28,24},{0,28},{5,1},{9... | collective-permute-start | bytes 12296 | tf_op jit(solution)/shard_map/ppermute | solution.py:43
  30.5 1.3 %wall.5 = (f32[128,1024]{1,0:T(8,128)S(1)}, f32[128,1024]{1,0:T(8,128)S(1)}, f32[8,128]{1,0:T(8,128)S(1)}) custom-call(f32[128,1024]{1,0:T(8,128)S(1)} %get-tuple-element.91.free_ref, f32[128,1024]{1,0:T(8,128)S(1)} %get-tuple-element.92.bound_ref, f32[128,128]{1,0:T(8,128)S(1)} %copy-done.2, f32[1,128]{1,0:T(1,128)S(1)} %bitcast.14, f32[1,128]{1,0:T(1,128)S(1)} %bitcast.18, ...), custom_call_target="tpu_custom_call" | custom-call | bytes 3900000 | tf_op jit(solution)/shard_map/wall/pallas_call | solution.py:558
  32.1 2.4 %collective-permute-start.10 = (f32[112,128]{1,0:T(8,128)S(1)}, f32[112,128]{1,0:T(8,128)S(1)}, u32[]{:S(2)}, u32[]{:S(2)}) collective-permute-start(f32[112,128]{1,0:T(8,128)S(1)} %get-tuple-element.95), channel_id=1, source_target_pairs={{1,0},{2,1},{3,2},{0,3},{5,4},{6,5},{7,6},{4,7},{9,8},{10,9},{11,1... | collective-permute-start | bytes 172040 | tf_op jit(solution)/shard_map/ppermute | solution.py:43
  34.5 0.6 collective-permute-start.11
  35.1 0.8 %bulk.6 = (f32[3328,128]{1,0:T(8,128)S(1)}, f32[3328,128]{1,0:T(8,128)S(1)}, f32[24,128]{1,0:T(8,128)S(1)}) custom-call(f32[3328,128]{1,0:T(8,128)S(1)} %get-tuple-element.85.refs_0_.post_ref, f32[8,128]{1,0:T(8,128)S(1)} %collective-permute-done.8.refs_1_.behind_ref, f32[8,128]{1,0:T(8,128)S(1)} %collective-permute-done.9.refs_2_.ahead_ref), custom_call_target="tpu_custom_call" | custom-call | bytes 6000000 | tf_op jit(solution)/shard_map/bulk/pallas_call | solution.py:568
  35.9 3.6 %collective-permute-done.11.refs_6_.refs_2_ = f32[16,128]{1,0:T(8,128)S(1)} collective-permute-done((f32[16,128]{1,0:T(8,128)S(1)}, f32[16,128]{1,0:T(8,128)S(1)}, u32[]{:S(2)}, u32[]{:S(2)}) %collective-permute-start.11) | collective-permute-done | bytes 8224 | tf_op jit(solution)/shard_map/ppermute | solution.py:43
  39.4 1.0 %collective-permute-done.12.refs_7_.refs_3_ = f32[112,128]{1,0:T(8,128)S(1)} collective-permute-done((f32[112,128]{1,0:T(8,128)S(1)}, f32[112,128]{1,0:T(8,128)S(1)}, u32[]{:S(2)}, u32[]{:S(2)}) %collective-permute-start.12) | collective-permute-done | bytes 57376 | tf_op jit(solution)/shard_map/ppermute | solution.py:43
  41.0 2.6 %collective-permute-start.14 = (f32[8,128]{1,0:T(8,128)S(1)}, f32[8,128]{1,0:T(8,128)S(1)}, u32[]{:S(2)}, u32[]{:S(2)}) collective-permute-start(f32[8,128]{1,0:T(8,128)S(1)} %get-tuple-element.100), channel_id=1, source_target_pairs={{4,0},{8,4},{12,8},{16,12},{20,16},{24,20},{28,24},{0,28},{5,1},{9... | collective-permute-start | bytes 12296 | tf_op jit(solution)/shard_map/ppermute | solution.py:43
  43.6 1.3 %wall.6 = (f32[128,1024]{1,0:T(8,128)S(1)}, f32[128,1024]{1,0:T(8,128)S(1)}, f32[8,128]{1,0:T(8,128)S(1)}) custom-call(f32[128,1024]{1,0:T(8,128)S(1)} %get-tuple-element.104.free_ref, f32[128,1024]{1,0:T(8,128)S(1)} %get-tuple-element.105.bound_ref, f32[128,128]{1,0:T(8,128)S(1)} %copy-done.2, f32[1,128]{1,0:T(1,128)S(1)} %bitcast.15, ...), custom_call_target="tpu_custom_call" | custom-call | bytes 3900000 | tf_op jit(solution)/shard_map/wall/pallas_call | solution.py:558
  45.3 2.5 %collective-permute-start.15 = (f32[112,128]{1,0:T(8,128)S(1)}, f32[112,128]{1,0:T(8,128)S(1)}, u32[]{:S(2)}, u32[]{:S(2)}) collective-permute-start(f32[112,128]{1,0:T(8,128)S(1)} %get-tuple-element.108), channel_id=1, source_target_pairs={{1,0},{2,1},{3,2},{0,3},{5,4},{6,5},{7,6},{4,7},{9,8},{10,9},{11,1... | collective-permute-start | bytes 172040 | tf_op jit(solution)/shard_map/ppermute | solution.py:43
  47.7 0.6 collective-permute-start.16
  48.4 0.8 %bulk.7 = (f32[3328,128]{1,0:T(8,128)S(1)}, f32[3328,128]{1,0:T(8,128)S(1)}, f32[24,128]{1,0:T(8,128)S(1)}) custom-call(f32[3328,128]{1,0:T(8,128)S(1)} %get-tuple-element.98.refs_0_.post_ref, f32[8,128]{1,0:T(8,128)S(1)} %collective-permute-done.13.refs_1_.behind_ref, f32[8,128]{1,0:T(8,128)S(1)} %collective-permute-done.14.refs_2_.ahead_ref), custom_call_target="tpu_custom_call" | custom-call | bytes 6000000 | tf_op jit(solution)/shard_map/bulk/pallas_call | solution.py:568
  49.1 3.2 %collective-permute-done.16.refs_6_.refs_2_ = f32[16,128]{1,0:T(8,128)S(1)} collective-permute-done((f32[16,128]{1,0:T(8,128)S(1)}, f32[16,128]{1,0:T(8,128)S(1)}, u32[]{:S(2)}, u32[]{:S(2)}) %collective-permute-start.16) | collective-permute-done | bytes 8224 | tf_op jit(solution)/shard_map/ppermute | solution.py:43
  52.3 1.4 %collective-permute-done.17.refs_7_.refs_3_ = f32[112,128]{1,0:T(8,128)S(1)} collective-permute-done((f32[112,128]{1,0:T(8,128)S(1)}, f32[112,128]{1,0:T(8,128)S(1)}, u32[]{:S(2)}, u32[]{:S(2)}) %collective-permute-start.17) | collective-permute-done | bytes 57376 | tf_op jit(solution)/shard_map/ppermute | solution.py:43
  54.3 2.6 %collective-permute-start.19 = (f32[8,128]{1,0:T(8,128)S(1)}, f32[8,128]{1,0:T(8,128)S(1)}, u32[]{:S(2)}, u32[]{:S(2)}) collective-permute-start(f32[8,128]{1,0:T(8,128)S(1)} %get-tuple-element.113), channel_id=1, source_target_pairs={{4,0},{8,4},{12,8},{16,12},{20,16},{24,20},{28,24},{0,28},{5,1},{9... | collective-permute-start | bytes 12296 | tf_op jit(solution)/shard_map/ppermute | solution.py:43
  56.9 1.3 %collective-permute-done.18.behind_ref = f32[8,128]{1,0:T(8,128)S(1)} collective-permute-done((f32[8,128]{1,0:T(8,128)S(1)}, f32[8,128]{1,0:T(8,128)S(1)}, u32[]{:S(2)}, u32[]{:S(2)}) %collective-permute-start.18) | collective-permute-done | bytes 4128 | tf_op jit(solution)/shard_map/ppermute | solution.py:43
  58.4 0.7 %collective-permute-start.20 = (f32[32,128]{1,0:T(8,128)S(1)}, f32[32,128]{1,0:T(8,128)S(1)}, u32[]{:S(2)}, u32[]{:S(2)}) collective-permute-start(f32[32,128]{1,0:T(8,128)S(1)} %get-tuple-element.116), channel_id=1, source_target_pairs={{3,0},{0,1},{1,2},{2,3},{7,4},{4,5},{5,6},{6,7},{11,8},{8,9},{9,10... | collective-permute-start | bytes 49160 | tf_op jit(solution)/shard_map/ppermute | solution.py:43
  59.1 3.2 %collective-permute-start.21 = (f32[32,128]{1,0:T(8,128)S(1)}, f32[32,128]{1,0:T(8,128)S(1)}, u32[]{:S(2)}, u32[]{:S(2)}) collective-permute-start(f32[32,128]{1,0:T(8,128)S(1)} %get-tuple-element.117), channel_id=1, source_target_pairs={{1,0},{2,1},{3,2},{0,3},{5,4},{6,5},{7,6},{4,7},{9,8},{10,9},{11,1... | collective-permute-start | bytes 49160 | tf_op jit(solution)/shard_map/ppermute | solution.py:43
  62.3 2.3 %wall.7 = (f32[128,1024]{1,0:T(8,128)}, f32[128,1024]{1,0:T(8,128)}, f32[8,128]{1,0:T(8,128)}) custom-call(f32[128,1024]{1,0:T(8,128)S(1)} %get-tuple-element.120.free_ref, f32[128,1024]{1,0:T(8,128)S(1)} %get-tuple-element.121.bound_ref, f32[128,128]{1,0:T(8,128)S(1)} %copy-done.2, f32[1,128]{1,0:T(1,128)S(1)} %bitcast.16, f32[1,128]{1,0:T(1,128)S(1)} %bitcast.20, ...), custom_call_target="tpu_custom_call" | custom-call | bytes 3900000 | tf_op jit(solution)/shard_map/wall/pallas_call | solution.py:558
  65.1 0.7 %last.1 = (f32[16,8,128]{2,1,0:T(8,128)}, f32[16,8,128]{2,1,0:T(8,128)}) custom-call(f32[16,8,128]{2,1,0:T(8,128)S(1)} %get-tuple-element.114.drug_part, f32[16,8,128]{2,1,0:T(8,128)S(1)} %get-tuple-element.115.flow_part, f32[32,128]{1,0:T(8,128)S(1)} %collective-permute-done.20.below, f32[32,128]{1,0:T(8,128)S(1)} %collective-permute-done.21.above), custom_call_target="tpu_custom_call" | custom-call | bytes 900000 | tf_op jit(solution)/shard_map/last/pallas_call | solution.py:578
  (49 shorter events, 4.2 us)
Async XLA Ops:
  0.6 8.1 %copy-start = (f32[26,16,8,128]{3,2,1,0:T(8,128)S(1)}, f32[26,16,8,128]{3,2,1,0:T(8,128)}, u32[]{:S(2)}) copy-start(f32[26,16,8,128]{3,2,1,0:T(8,128)} %pops_ref.1) | copy-start | bytes 5111812
  2.6 10.9 %copy-start.4 = (s32[8,128]{1,0:T(8,128)S(1)}, s32[8,128]{1,0:T(8,128)}, u32[]{:S(2)}) copy-start(s32[8,128]{1,0:T(8,128)} %get-tuple-element.66.refs_3_.code_ref) | copy-start | bytes 12292
  2.6 10.9 %copy-start.6 = (f32[32,128]{1,0:T(8,128)S(1)}, f32[32,128]{1,0:T(8,128)}, u32[]{:S(2)}) copy-start(f32[32,128]{1,0:T(8,128)} %get-tuple-element.67.refs_4_.refs_0_) | copy-start | bytes 49156
  2.6 10.0 %collective-permute-start = (f32[40,128]{1,0:T(8,128)}, f32[40,128]{1,0:T(8,128)S(1)}, u32[]{:S(2)}, u32[]{:S(2)}) collective-permute-start(f32[40,128]{1,0:T(8,128)} %get-tuple-element.68), channel_id=1, source_target_pairs={{1,0},{2,1},{3,2},{0,3},{5,4},{6,5},{7,6},{4,7},{9,8},{10,9},{11,1... | collective-permute-start | bytes 61448 | tf_op jit(solution)/shard_map/ppermute | solution.py:43
  7.7 5.8 %collective-permute-start.2 = (f32[40,128]{1,0:T(8,128)}, f32[40,128]{1,0:T(8,128)S(1)}, u32[]{:S(2)}, u32[]{:S(2)}) collective-permute-start(f32[40,128]{1,0:T(8,128)} %get-tuple-element.70), channel_id=1, source_target_pairs={{3,0},{0,1},{1,2},{2,3},{7,4},{4,5},{5,6},{6,7},{11,8},{8,9},{9,10... | collective-permute-start | bytes 61448 | tf_op jit(solution)/shard_map/ppermute | solution.py:43
  7.7 4.8 %collective-permute-start.1 = (f32[32,128]{1,0:T(8,128)}, f32[32,128]{1,0:T(8,128)S(1)}, u32[]{:S(2)}, u32[]{:S(2)}) collective-permute-start(f32[32,128]{1,0:T(8,128)} %get-tuple-element.69), channel_id=1, source_target_pairs={{2,0},{3,1},{0,2},{1,3},{6,4},{7,5},{4,6},{5,7},{10,8},{11,9},{8,1... | collective-permute-start | bytes 49160 | tf_op jit(solution)/shard_map/ppermute | solution.py:43
  13.5 3.1 %copy-start.1 = (f32[128,1024]{1,0:T(8,128)S(1)}, f32[128,1024]{1,0:T(8,128)}, u32[]{:S(2)}) copy-start(f32[128,1024]{1,0:T(8,128)} %free_ref.3) | copy-start | bytes 1572868
  13.5 3.1 %copy-start.2 = (f32[128,128]{1,0:T(8,128)S(1)}, f32[128,128]{1,0:T(8,128)}, u32[]{:S(2)}) copy-start(f32[128,128]{1,0:T(8,128)} %spread_ref.7) | copy-start | bytes 196612
  13.5 3.1 %copy-start.3 = (f32[128,1024]{1,0:T(8,128)S(1)}, f32[128,1024]{1,0:T(8,128)}, u32[]{:S(2)}) copy-start(f32[128,1024]{1,0:T(8,128)} %bound_ref.1) | copy-start | bytes 1572868
  13.6 3.1 %copy-start.5 = (s32[1024]{0:T(1024)S(1)}, s32[1024]{0:T(1024)}, u32[]{:S(2)}) copy-start(s32[1024]{0:T(1024)} %param.17) | copy-start | bytes 12292
  13.6 3.1 %copy-start.7 = (f32[128]{0:T(128)S(1)}, f32[128]{0:T(128)}, u32[]{:S(2)}) copy-start(f32[128]{0:T(128)} %param.13) | copy-start | bytes 1540
  13.6 3.1 %copy-start.8 = (f32[128]{0:T(128)S(1)}, f32[128]{0:T(128)}, u32[]{:S(2)}) copy-start(f32[128]{0:T(128)} %param.14) | copy-start | bytes 1540
  14.0 4.0 %collective-permute-start.3 = (f32[8,128]{1,0:T(8,128)S(1)}, f32[8,128]{1,0:T(8,128)S(1)}, u32[]{:S(2)}, u32[]{:S(2)}) collective-permute-start(f32[8,128]{1,0:T(8,128)S(1)} %get-tuple-element.72), channel_id=1, source_target_pairs={{28,0},{0,4},{4,8},{8,12},{12,16},{16,20},{20,24},{24,28},{29,1},{... | collective-permute-start | bytes 12296 | tf_op jit(solution)/shard_map/ppermute | solution.py:43
  14.0 4.0 %collective-permute-start.4 = (f32[8,128]{1,0:T(8,128)S(1)}, f32[8,128]{1,0:T(8,128)S(1)}, u32[]{:S(2)}, u32[]{:S(2)}) collective-permute-start(f32[8,128]{1,0:T(8,128)S(1)} %get-tuple-element.73), channel_id=1, source_target_pairs={{4,0},{8,4},{12,8},{16,12},{20,16},{24,20},{28,24},{0,28},{5,1},{9... | collective-permute-start | bytes 12296 | tf_op jit(solution)/shard_map/ppermute | solution.py:43
  18.3 7.5 %collective-permute-start.5 = (f32[112,128]{1,0:T(8,128)S(1)}, f32[112,128]{1,0:T(8,128)S(1)}, u32[]{:S(2)}, u32[]{:S(2)}) collective-permute-start(f32[112,128]{1,0:T(8,128)S(1)} %get-tuple-element.81), channel_id=1, source_target_pairs={{1,0},{2,1},{3,2},{0,3},{5,4},{6,5},{7,6},{4,7},{9,8},{10,9},{11,1... | collective-permute-start | bytes 172040 | tf_op jit(solution)/shard_map/ppermute | solution.py:43
  21.3 6.1 %collective-permute-start.7 = (f32[112,128]{1,0:T(8,128)S(1)}, f32[112,128]{1,0:T(8,128)S(1)}, u32[]{:S(2)}, u32[]{:S(2)}) collective-permute-start(f32[112,128]{1,0:T(8,128)S(1)} %get-tuple-element.83), channel_id=1, source_target_pairs={{3,0},{0,1},{1,2},{2,3},{7,4},{4,5},{5,6},{6,7},{11,8},{8,9},{9,10... | collective-permute-start | bytes 172040 | tf_op jit(solution)/shard_map/ppermute | solution.py:43
  21.3 4.5 %collective-permute-start.6 = (f32[16,128]{1,0:T(8,128)S(1)}, f32[16,128]{1,0:T(8,128)S(1)}, u32[]{:S(2)}, u32[]{:S(2)}) collective-permute-start(f32[16,128]{1,0:T(8,128)S(1)} %get-tuple-element.82), channel_id=1, source_target_pairs={{2,0},{3,1},{0,2},{1,3},{6,4},{7,5},{4,6},{5,7},{10,8},{11,9},{8,1... | collective-permute-start | bytes 24584 | tf_op jit(solution)/shard_map/ppermute | solution.py:43
  27.8 4.0 %collective-permute-start.8 = (f32[8,128]{1,0:T(8,128)S(1)}, f32[8,128]{1,0:T(8,128)S(1)}, u32[]{:S(2)}, u32[]{:S(2)}) collective-permute-start(f32[8,128]{1,0:T(8,128)S(1)} %get-tuple-element.86), channel_id=1, source_target_pairs={{28,0},{0,4},{4,8},{8,12},{12,16},{16,20},{20,24},{24,28},{29,1},{... | collective-permute-start | bytes 12296 | tf_op jit(solution)/shard_map/ppermute | solution.py:43
  27.9 4.0 %collective-permute-start.9 = (f32[8,128]{1,0:T(8,128)S(1)}, f32[8,128]{1,0:T(8,128)S(1)}, u32[]{:S(2)}, u32[]{:S(2)}) collective-permute-start(f32[8,128]{1,0:T(8,128)S(1)} %get-tuple-element.87), channel_id=1, source_target_pairs={{4,0},{8,4},{12,8},{16,12},{20,16},{24,20},{28,24},{0,28},{5,1},{9... | collective-permute-start | bytes 12296 | tf_op jit(solution)/shard_map/ppermute | solution.py:43
  32.1 7.3 %collective-permute-start.10 = (f32[112,128]{1,0:T(8,128)S(1)}, f32[112,128]{1,0:T(8,128)S(1)}, u32[]{:S(2)}, u32[]{:S(2)}) collective-permute-start(f32[112,128]{1,0:T(8,128)S(1)} %get-tuple-element.95), channel_id=1, source_target_pairs={{1,0},{2,1},{3,2},{0,3},{5,4},{6,5},{7,6},{4,7},{9,8},{10,9},{11,1... | collective-permute-start | bytes 172040 | tf_op jit(solution)/shard_map/ppermute | solution.py:43
  34.5 6.0 %collective-permute-start.12 = (f32[112,128]{1,0:T(8,128)S(1)}, f32[112,128]{1,0:T(8,128)S(1)}, u32[]{:S(2)}, u32[]{:S(2)}) collective-permute-start(f32[112,128]{1,0:T(8,128)S(1)} %get-tuple-element.97), channel_id=1, source_target_pairs={{3,0},{0,1},{1,2},{2,3},{7,4},{4,5},{5,6},{6,7},{11,8},{8,9},{9,10... | collective-permute-start | bytes 172040 | tf_op jit(solution)/shard_map/ppermute | solution.py:43
  34.5 5.0 %collective-permute-start.11 = (f32[16,128]{1,0:T(8,128)S(1)}, f32[16,128]{1,0:T(8,128)S(1)}, u32[]{:S(2)}, u32[]{:S(2)}) collective-permute-start(f32[16,128]{1,0:T(8,128)S(1)} %get-tuple-element.96), channel_id=1, source_target_pairs={{2,0},{3,1},{0,2},{1,3},{6,4},{7,5},{4,6},{5,7},{10,8},{11,9},{8,1... | collective-permute-start | bytes 24584 | tf_op jit(solution)/shard_map/ppermute | solution.py:43
  40.9 4.0 %collective-permute-start.13 = (f32[8,128]{1,0:T(8,128)S(1)}, f32[8,128]{1,0:T(8,128)S(1)}, u32[]{:S(2)}, u32[]{:S(2)}) collective-permute-start(f32[8,128]{1,0:T(8,128)S(1)} %get-tuple-element.99), channel_id=1, source_target_pairs={{28,0},{0,4},{4,8},{8,12},{12,16},{16,20},{20,24},{24,28},{29,1},{... | collective-permute-start | bytes 12296 | tf_op jit(solution)/shard_map/ppermute | solution.py:43
  41.0 4.0 %collective-permute-start.14 = (f32[8,128]{1,0:T(8,128)S(1)}, f32[8,128]{1,0:T(8,128)S(1)}, u32[]{:S(2)}, u32[]{:S(2)}) collective-permute-start(f32[8,128]{1,0:T(8,128)S(1)} %get-tuple-element.100), channel_id=1, source_target_pairs={{4,0},{8,4},{12,8},{16,12},{20,16},{24,20},{28,24},{0,28},{5,1},{9... | collective-permute-start | bytes 12296 | tf_op jit(solution)/shard_map/ppermute | solution.py:43
  45.3 7.0 %collective-permute-start.15 = (f32[112,128]{1,0:T(8,128)S(1)}, f32[112,128]{1,0:T(8,128)S(1)}, u32[]{:S(2)}, u32[]{:S(2)}) collective-permute-start(f32[112,128]{1,0:T(8,128)S(1)} %get-tuple-element.108), channel_id=1, source_target_pairs={{1,0},{2,1},{3,2},{0,3},{5,4},{6,5},{7,6},{4,7},{9,8},{10,9},{11,1... | collective-permute-start | bytes 172040 | tf_op jit(solution)/shard_map/ppermute | solution.py:43
  47.7 6.0 %collective-permute-start.17 = (f32[112,128]{1,0:T(8,128)S(1)}, f32[112,128]{1,0:T(8,128)S(1)}, u32[]{:S(2)}, u32[]{:S(2)}) collective-permute-start(f32[112,128]{1,0:T(8,128)S(1)} %get-tuple-element.110), channel_id=1, source_target_pairs={{3,0},{0,1},{1,2},{2,3},{7,4},{4,5},{5,6},{6,7},{11,8},{8,9},{9,10... | collective-permute-start | bytes 172040 | tf_op jit(solution)/shard_map/ppermute | solution.py:43
  47.7 4.5 %collective-permute-start.16 = (f32[16,128]{1,0:T(8,128)S(1)}, f32[16,128]{1,0:T(8,128)S(1)}, u32[]{:S(2)}, u32[]{:S(2)}) collective-permute-start(f32[16,128]{1,0:T(8,128)S(1)} %get-tuple-element.109), channel_id=1, source_target_pairs={{2,0},{3,1},{0,2},{1,3},{6,4},{7,5},{4,6},{5,7},{10,8},{11,9},{8,1... | collective-permute-start | bytes 24584 | tf_op jit(solution)/shard_map/ppermute | solution.py:43
  54.2 4.0 %collective-permute-start.18 = (f32[8,128]{1,0:T(8,128)S(1)}, f32[8,128]{1,0:T(8,128)S(1)}, u32[]{:S(2)}, u32[]{:S(2)}) collective-permute-start(f32[8,128]{1,0:T(8,128)S(1)} %get-tuple-element.112), channel_id=1, source_target_pairs={{28,0},{0,4},{4,8},{8,12},{12,16},{16,20},{20,24},{24,28},{29,1},{... | collective-permute-start | bytes 12296 | tf_op jit(solution)/shard_map/ppermute | solution.py:43
  54.3 4.0 %collective-permute-start.19 = (f32[8,128]{1,0:T(8,128)S(1)}, f32[8,128]{1,0:T(8,128)S(1)}, u32[]{:S(2)}, u32[]{:S(2)}) collective-permute-start(f32[8,128]{1,0:T(8,128)S(1)} %get-tuple-element.113), channel_id=1, source_target_pairs={{4,0},{8,4},{12,8},{16,12},{20,16},{24,20},{28,24},{0,28},{5,1},{9... | collective-permute-start | bytes 12296 | tf_op jit(solution)/shard_map/ppermute | solution.py:43
  58.4 6.6 %collective-permute-start.20 = (f32[32,128]{1,0:T(8,128)S(1)}, f32[32,128]{1,0:T(8,128)S(1)}, u32[]{:S(2)}, u32[]{:S(2)}) collective-permute-start(f32[32,128]{1,0:T(8,128)S(1)} %get-tuple-element.116), channel_id=1, source_target_pairs={{3,0},{0,1},{1,2},{2,3},{7,4},{4,5},{5,6},{6,7},{11,8},{8,9},{9,10... | collective-permute-start | bytes 49160 | tf_op jit(solution)/shard_map/ppermute | solution.py:43
  59.1 5.9 %collective-permute-start.21 = (f32[32,128]{1,0:T(8,128)S(1)}, f32[32,128]{1,0:T(8,128)S(1)}, u32[]{:S(2)}, u32[]{:S(2)}) collective-permute-start(f32[32,128]{1,0:T(8,128)S(1)} %get-tuple-element.117), channel_id=1, source_target_pairs={{1,0},{2,1},{3,2},{0,3},{5,4},{6,5},{7,6},{4,7},{9,8},{10,9},{11,1... | collective-permute-start | bytes 49160 | tf_op jit(solution)/shard_map/ppermute | solution.py:43

commit v2 on v1

--- a/solution.py
+++ b/solution.py
@@ -6,6 +6,7 @@
 from jax.experimental import pallas as pl
 from jax.experimental.pallas import tpu as pltpu
 from jax.sharding import PartitionSpec as P
+
 
 STEPS = 4
 SUB = 2
@@ -41,6 +42,22 @@
 def shifted(block, axis, distance):
     count = lax.axis_size(axis)
     return lax.ppermute(block, axis, [((i - distance) % count, i) for i in range(count)])
+
+
+def paired(inner, outer):
+    count = lax.axis_size("ax")
+    near = [(i, i ^ 1) for i in range(count)]
+    far = [(i, (i + 1) % count if i % 2 else (i - 1) % count) for i in range(count)]
+    return lax.ppermute(inner, "ax", near), lax.ppermute(outer, "ax", far)
+
+
+def by_parity(even, odd):
+    return jnp.where(lax.axis_index("ax") % 2 == 0, even, odd)
+
+
+def axial_rims(inner_ref, outer_ref):
+    inner, outer = inner_ref[...], outer_ref[...]
+    return by_parity(outer, inner), by_parity(inner, outer)
 
 
 def lanes(shape):
@@ -272,9 +289,9 @@
     if first:
         state_ref, post_ref, speed_ref = refs
     else:
-        old_ref, behind_ref, ahead_ref, state_ref, post_ref, speed_ref = refs
+        old_ref, inner_ref, outer_ref, state_ref, post_ref, speed_ref = refs
         old = Planes(old_ref, radial, across)
-        behind, ahead = behind_ref[...], ahead_ref[...]
+        behind, ahead = axial_rims(inner_ref, outer_ref)
     state, post = Planes(state_ref, radial, across), Planes(post_ref, radial, across)
     for level in range(radial):
         if first:
@@ -299,9 +316,9 @@
     inbox = refs[4:4 + sectors]
     refs = refs[4 + sectors:]
     if first:
-        post_ref, rise_ref, fall_ref, open_ref, counts_ref, edges_ref = refs
+        post_ref, inner_ref, outer_ref, open_ref, counts_ref, edges_ref = refs
     else:
-        open_ref, post_ref, rise_ref, fall_ref = refs
+        open_ref, post_ref, inner_ref, outer_ref = refs
     del bulk_ref
     across, along = code_ref.shape
     end = radial - 1
@@ -372,8 +389,8 @@
         for place, member in enumerate(SLAB_FALLING):
             slot = place * radial + level
             fall = jnp.where(lane == slot, pltpu.roll(post.get(member, level), slot, 1), fall)
-    rise_ref[...] = rise
-    fall_ref[...] = fall
+    inner_ref[...] = by_parity(rise, fall)
+    outer_ref[...] = by_parity(fall, rise)
 
 
 def wall_kernel(sectors, free_ref, bound_ref, spread_ref, on_ref, off_ref, strut_ref, counts_ref, *refs):
@@ -404,10 +421,10 @@
         top_ref[row:row + 1, :] = free[0:1, :]
 
 
-def send_kernel(sectors, radial, post_ref, behind_ref, ahead_ref, code_ref, edges_ref, top_ref, *outs):
+def send_kernel(sectors, radial, post_ref, inner_ref, outer_ref, code_ref, edges_ref, top_ref, *outs):
     across, along = code_ref.shape
     post = Planes(post_ref, radial, across)
-    behind, ahead = behind_ref[...], ahead_ref[...]
+    behind, ahead = axial_rims(inner_ref, outer_ref)
     end = radial - 1
     row = sublanes((across, along))
     surface = post.get(FLOWS, end) + post.get(FLOWS + 5, end - 1) + post.get(FLOWS + 5, end)
@@ -437,9 +454,9 @@
                 out[base:base + radial, :] = post.rows(member, 0, radial, side)
 
 
-def last_send_kernel(radial, across, post_ref, behind_ref, ahead_ref, up_ref, down_ref):
+def last_send_kernel(radial, across, post_ref, inner_ref, outer_ref, up_ref, down_ref):
     post = Planes(post_ref, radial, across)
-    behind, ahead = behind_ref[...], ahead_ref[...]
+    behind, ahead = axial_rims(inner_ref, outer_ref)
     for out, drug, plus, minus, side in ((up_ref, FLOWS + 3, 7, 10, across - 1), (down_ref, FLOWS + 4, 9, 8, 0)):
         out[0:radial, :] = post.rows(drug, 0, radial, side)
         for level in range(radial):
@@ -448,9 +465,9 @@
             out[radial + level:radial + level + 1, :] = value[side:side + 1, :]
 
 
-def fields_kernel(radial, across, post_ref, behind_ref, ahead_ref, drug_ref, flow_ref):
+def fields_kernel(radial, across, post_ref, inner_ref, outer_ref, drug_ref, flow_ref):
     post = Planes(post_ref, radial, across)
-    behind, ahead = behind_ref[...], ahead_ref[...]
+    behind, ahead = axial_rims(inner_ref, outer_ref)
     for level in range(radial):
         def member_of(member):
             value = streamed(post, member, level, behind, ahead)
@@ -483,11 +500,10 @@
             out[level] = value + jnp.where(row == across - 1, above[place:place + 1, :], 0.0)
 
 
-def kernel_call(body, name, outs, count, micros, aliases=None):
+def kernel_call(body, outs, count, micros, aliases=None):
     shapes = [out if isinstance(out, jax.ShapeDtypeStruct) else jax.ShapeDtypeStruct(out, F32) for out in outs]
     return pl.pallas_call(
         body,
-        name=name,
         out_shape=shapes,
         in_specs=[pl.BlockSpec(memory_space=VMEM)] * count,
         out_specs=[pl.BlockSpec(memory_space=VMEM)] * len(outs),
@@ -498,7 +514,7 @@
 
 
 def first_call(sectors, populations, sector, line, strut, free):
-    members, radial, across, along = populations.shape
+    members, _, across, along = populations.shape
     plane = (across, along)
     sizes = [((5 if hop in (1, sectors - 1) else 4) * across, along) for hop in range(sectors)]
     return pl.pallas_call(
@@ -538,7 +554,7 @@
     inbox = exchange(boxes)
     state = populations.reshape(flat)
     speeds = (3 * across, along)
-    bulk, speed = kernel_call(functools.partial(bulk_kernel, True, radial, across), "bulk", [flat, speeds], 1, 1.5)(state)
+    bulk, speed = kernel_call(functools.partial(bulk_kernel, True, radial, across), [flat, speeds], 1, 1.5)(state)
     free, bound = wall_free, wall_bound
     openness = counts = edges = None
     for step in range(STEPS):
@@ -548,34 +564,34 @@
             outs = outs + [plane, plane, jax.ShapeDtypeStruct(plane, jnp.int32)]
         extra = [] if first else [openness]
         results = kernel_call(
-            functools.partial(flux_kernel, sectors, first, radial), "flux", outs, 4 + sectors + len(extra), 0.8, {1: 0}
+            functools.partial(flux_kernel, sectors, first, radial), outs, 4 + sectors + len(extra), 0.8, {1: 0}
         )(state, bulk, speed, codes, *inbox, *extra)
-        post, rise, fall = results[:3]
+        post = results[0]
         if first:
             openness, counts, edges = results[3:]
-        behind = shifted(rise, "ax", 1)
-        ahead = shifted(fall, "ax", -1)
+        inner, outer = paired(*results[1:3])
         free, bound, top = kernel_call(
-            functools.partial(wall_kernel, sectors), "wall", [wall_free.shape, wall_free.shape, plane], 7 + sectors, 1.3
+            functools.partial(wall_kernel, sectors), [wall_free.shape, wall_free.shape, plane], 7 + sectors, 1.3
         )(free, bound, wall_propagator, rate_on, rate_off, strut, counts, *inbox)
         if last:
             continue
         sizes = [(2 * across + (rims if hop in (1, sectors - 1) else 0), along) for hop in range(sectors)]
-        boxes = kernel_call(functools.partial(send_kernel, sectors, radial), "send", sizes, 6, 0.3)(
-            post, behind, ahead, codes, edges, top
+        boxes = kernel_call(functools.partial(send_kernel, sectors, radial), sizes, 6, 0.3)(
+            post, inner, outer, codes, edges, top
         )
         inbox = exchange(boxes)
         state, bulk, speed = kernel_call(
-            functools.partial(bulk_kernel, False, radial, across), "bulk", [flat, flat, speeds], 3, 2.0
-        )(post, behind, ahead)
+            functools.partial(bulk_kernel, False, radial, across), [flat, flat, speeds], 3, 2.0
+        )(post, inner, outer)
     up, down = kernel_call(
-        functools.partial(last_send_kernel, radial, across), "send", [(2 * radial, along)] * 2, 3, 0.2
-    )(post, behind, ahead)
-    below, above = shifted(up, "th", 1), shifted(down, "th", -1)
+        functools.partial(last_send_kernel, radial, across), [(2 * radial, along)] * 2, 3, 0.2
+    )(post, inner, outer)
+    below = shifted(up, "th", 1)
+    above = shifted(down, "th", -1)
     parts = kernel_call(
-        functools.partial(fields_kernel, radial, across), "fields", [(radial,) + plane] * 2, 3, 1.0
-    )(post, behind, ahead)
-    drug_field, axial_flow = kernel_call(last_kernel, "last", [(radial,) + plane] * 2, 4, 0.3)(*parts, below, above)
+        functools.partial(fields_kernel, radial, across), [(radial,) + plane] * 2, 3, 1.0
+    )(post, inner, outer)
+    drug_field, axial_flow = kernel_call(last_kernel, [(radial,) + plane] * 2, 4, 0.3)(*parts, below, above)
     return drug_field, axial_flow, free, bound
 
 

time: 65.9 us -> 66.1 us (level)
  waiting for transfers between devices: 19.3 us -> 23.2 us
  starting transfers between devices: 30.4 us -> 26.7 us
    ppermute x22 -> x14, starting transfers between devices: 30.4 us -> 19.8 us  [shifted(): lax.ppermute(block, axis, [((i - distance) % count, i) for i in range(cou...]
    ppermute x0 -> x8, starting transfers between devices: none -> 6.93 us  [paired(): return (lax.ppermute(inner, 'ax', near), lax.ppermute(outer, 'ax', far))]
    ppermute x0 -> x8, waiting for transfers between devices: none -> 5.3 us  [paired(): return (lax.ppermute(inner, 'ax', near), lax.ppermute(outer, 'ax', far))]
    ppermute x22 -> x14, waiting for transfers between devices: 19.3 us -> 17.9 us  [shifted(): lax.ppermute(block, axis, [((i - distance) % count, i) for i in range(cou...]
  transfers between devices with their start and end apart: 22 -> 22, of which waited for: 9 -> 13; matrix products, arithmetic and copies ran while one was open for 0% -> 0% of each run, Pallas kernels for 15% -> 15%
where the time goes in v2:
time: 66.1 us; the launch traced here: 65.9 us
  starting transfers between devices  26.7 us (40%)
  waiting for transfers between devices  23.2 us (35%)
  Pallas kernels  15.1 us (23%)
  between operations  0.91 us (1%)
    ppermute x14, starting transfers between devices, shifted(): lax.ppermute(block, axis, [((i - distance) % count, i) for i in range(cou...  19.8 us
    ppermute x14, waiting for transfers between devices, shifted(): lax.ppermute(block, axis, [((i - distance) % count, i) for i in range(cou...  17.9 us
    ppermute x8, starting transfers between devices, paired(): return (lax.ppermute(inner, 'ax', near), lax.ppermute(outer, 'ax', far))  6.93 us
    pallas_call x4, Pallas kernels, per_device(): kernel_call(functools.partial(wall_kernel, sectors), [wall_free.shape, wa...  6.21 us
    ppermute x8, waiting for transfers between devices, paired(): return (lax.ppermute(inner, 'ax', near), lax.ppermute(outer, 'ax', far))  5.3 us
    pallas_call x3, Pallas kernels, per_device(): kernel_call(functools.partial(bulk_kernel, False, radial, across), [flat,...  2.33 us
    pallas_call x1, Pallas kernels, first_call(): pl.pallas_call(functools.partial(first_kernel, sectors), name='first', ou...  1.93 us
    pallas_call x4, Pallas kernels, per_device(): kernel_call(functools.partial(flux_kernel, sectors, first, radial), outs,...  1.82 us
  transfers between devices with their start and end apart: 22, of which 13 were waited for; matrix products, arithmetic and copies ran while one was open for 0% of the time, Pallas kernels for 15%

profile of v2, /device:TPU:0, one launch (start us, length us, event | category | flops | bytes accessed | tf_op | source)
XLA Modules:
  0.0 65.9 jit_solution(8122413828161283903)
XLA Ops:
  0.6 1.9 %first.1 = (s32[8,128]{1,0:T(8,128)}, f32[32,128]{1,0:T(8,128)}, f32[40,128]{1,0:T(8,128)}, f32[32,128]{1,0:T(8,128)}, f32[40,128]{1,0:T(8,128)}) custom-call(f32[26,16,8,128]{3,2,1,0:T(8,128)} %pops_ref.1, s32[8,128]{1,0:T(8,128)} %bitcast.21, s32[8,128]{1,0:T(8,128)} %bitcast.22, s32[8,128]{1,0:T(8,128)} %bitcast.8, f32[128,1024]{1,0:T(8,128)} %free_ref.3), custom_call_target="tpu_custom_call" | custom-call | tf_op jit(solution)/shard_map/first/pallas_call | solution.py:520
  2.6 5.1 %collective-permute-start = (f32[40,128]{1,0:T(8,128)}, f32[40,128]{1,0:T(8,128)S(1)}, u32[]{:S(2)}, u32[]{:S(2)}) collective-permute-start(f32[40,128]{1,0:T(8,128)} %get-tuple-element.68), channel_id=1, source_target_pairs={{1,0},{2,1},{3,2},{0,3},{5,4},{6,5},{7,6},{4,7},{9,8},{10,9},{11,1... | collective-permute-start | bytes 61448 | tf_op jit(solution)/shard_map/ppermute | solution.py:44
  7.7 1.0 %collective-permute-start.1 = (f32[32,128]{1,0:T(8,128)}, f32[32,128]{1,0:T(8,128)S(1)}, u32[]{:S(2)}, u32[]{:S(2)}) collective-permute-start(f32[32,128]{1,0:T(8,128)} %get-tuple-element.69), channel_id=1, source_target_pairs={{2,0},{3,1},{0,2},{1,3},{6,4},{7,5},{4,6},{5,7},{10,8},{11,9},{8,1... | collective-permute-start | bytes 49160 | tf_op jit(solution)/shard_map/ppermute | solution.py:44
  9.4 3.2 %collective-permute-done.1.refs_6_.refs_2_ = f32[32,128]{1,0:T(8,128)S(1)} collective-permute-done((f32[32,128]{1,0:T(8,128)}, f32[32,128]{1,0:T(8,128)S(1)}, u32[]{:S(2)}, u32[]{:S(2)}) %collective-permute-start.1) | collective-permute-done | bytes 16416 | tf_op jit(solution)/shard_map/ppermute | solution.py:44
  12.6 0.9 %collective-permute-done.2.refs_7_.refs_3_ = f32[40,128]{1,0:T(8,128)S(1)} collective-permute-done((f32[40,128]{1,0:T(8,128)}, f32[40,128]{1,0:T(8,128)S(1)}, u32[]{:S(2)}, u32[]{:S(2)}) %collective-permute-start.2) | collective-permute-done | bytes 20512 | tf_op jit(solution)/shard_map/ppermute | solution.py:44
  14.0 2.6 %collective-permute-start.4 = (f32[8,128]{1,0:T(8,128)S(1)}, f32[8,128]{1,0:T(8,128)S(1)}, u32[]{:S(2)}, u32[]{:S(2)}) collective-permute-start(f32[8,128]{1,0:T(8,128)S(1)} %get-tuple-element.73), channel_id=1, source_target_pairs={{0,28},{4,8},{8,4},{12,16},{16,12},{20,24},{24,20},{28,0},{1,29},{... | collective-permute-start | bytes 12296 | tf_op jit(solution)/shard_map/ppermute | solution.py:51
  16.6 1.3 %shard_map.123 = (f32[128,1024]{1,0:T(8,128)S(1)}, f32[128,1024]{1,0:T(8,128)S(1)}, f32[8,128]{1,0:T(8,128)S(1)}) custom-call(f32[128,1024]{1,0:T(8,128)S(1)} %copy-done.1, f32[128,1024]{1,0:T(8,128)S(1)} %copy-done.3, f32[128,128]{1,0:T(8,128)S(1)} %copy-done.2, f32[1,128]{1,0:T(1,128)S(1)} %bitcast.13, f32[1,128]{1,0:T(1,128)S(1)} %bitcast.17, ...), custom_call_target="tpu_custom_call" | custom-call | bytes 3900000 | tf_op jit(solution)/shard_map/pallas_call | solution.py:573
  18.3 3.0 %collective-permute-start.5 = (f32[112,128]{1,0:T(8,128)S(1)}, f32[112,128]{1,0:T(8,128)S(1)}, u32[]{:S(2)}, u32[]{:S(2)}) collective-permute-start(f32[112,128]{1,0:T(8,128)S(1)} %get-tuple-element.81), channel_id=1, source_target_pairs={{1,0},{2,1},{3,2},{0,3},{5,4},{6,5},{7,6},{4,7},{9,8},{10,9},{11,1... | collective-permute-start | bytes 172040 | tf_op jit(solution)/shard_map/ppermute | solution.py:44
  21.3 0.6 collective-permute-start.6
  21.9 0.8 %shard_map.122 = (f32[3328,128]{1,0:T(8,128)S(1)}, f32[3328,128]{1,0:T(8,128)S(1)}, f32[24,128]{1,0:T(8,128)S(1)}) custom-call(f32[3328,128]{1,0:T(8,128)S(1)} %get-tuple-element.71.refs_0_.post_ref, f32[8,128]{1,0:T(8,128)S(1)} %collective-permute-done.3.refs_1_.inner_ref, f32[8,128]{1,0:T(8,128)S(1)} %collective-permute-done.4.refs_2_.outer_ref), custom_call_target="tpu_custom_call" | custom-call | bytes 6000000 | tf_op jit(solution)/shard_map/pallas_call | solution.py:583
  22.7 3.3 %collective-permute-done.6.refs_6_.refs_2_ = f32[16,128]{1,0:T(8,128)S(1)} collective-permute-done((f32[16,128]{1,0:T(8,128)S(1)}, f32[16,128]{1,0:T(8,128)S(1)}, u32[]{:S(2)}, u32[]{:S(2)}) %collective-permute-start.6) | collective-permute-done | bytes 8224 | tf_op jit(solution)/shard_map/ppermute | solution.py:44
  26.0 1.2 %collective-permute-done.7.refs_7_.refs_3_ = f32[112,128]{1,0:T(8,128)S(1)} collective-permute-done((f32[112,128]{1,0:T(8,128)S(1)}, f32[112,128]{1,0:T(8,128)S(1)}, u32[]{:S(2)}, u32[]{:S(2)}) %collective-permute-start.7) | collective-permute-done | bytes 57376 | tf_op jit(solution)/shard_map/ppermute | solution.py:44
  27.8 2.2 %collective-permute-start.9 = (f32[8,128]{1,0:T(8,128)S(1)}, f32[8,128]{1,0:T(8,128)S(1)}, u32[]{:S(2)}, u32[]{:S(2)}) collective-permute-start(f32[8,128]{1,0:T(8,128)S(1)} %get-tuple-element.87), channel_id=1, source_target_pairs={{0,28},{4,8},{8,4},{12,16},{16,12},{20,24},{24,20},{28,0},{1,29},{... | collective-permute-start | bytes 12296 | tf_op jit(solution)/shard_map/ppermute | solution.py:51
  30.0 1.3 %shard_map.127 = (f32[128,1024]{1,0:T(8,128)S(1)}, f32[128,1024]{1,0:T(8,128)S(1)}, f32[8,128]{1,0:T(8,128)S(1)}) custom-call(f32[128,1024]{1,0:T(8,128)S(1)} %get-tuple-element.91.free_ref, f32[128,1024]{1,0:T(8,128)S(1)} %get-tuple-element.92.bound_ref, f32[128,128]{1,0:T(8,128)S(1)} %copy-done.2, f32[1,128]{1,0:T(1,128)S(1)} %bitcast.14, ...), custom_call_target="tpu_custom_call" | custom-call | bytes 3900000 | tf_op jit(solution)/shard_map/pallas_call | solution.py:573
  32.1 2.4 %collective-permute-start.10 = (f32[112,128]{1,0:T(8,128)S(1)}, f32[112,128]{1,0:T(8,128)S(1)}, u32[]{:S(2)}, u32[]{:S(2)}) collective-permute-start(f32[112,128]{1,0:T(8,128)S(1)} %get-tuple-element.95), channel_id=1, source_target_pairs={{1,0},{2,1},{3,2},{0,3},{5,4},{6,5},{7,6},{4,7},{9,8},{10,9},{11,1... | collective-permute-start | bytes 172040 | tf_op jit(solution)/shard_map/ppermute | solution.py:44
  34.6 0.6 collective-permute-start.11
  35.2 0.8 %shard_map.126 = (f32[3328,128]{1,0:T(8,128)S(1)}, f32[3328,128]{1,0:T(8,128)S(1)}, f32[24,128]{1,0:T(8,128)S(1)}) custom-call(f32[3328,128]{1,0:T(8,128)S(1)} %get-tuple-element.85.refs_0_.post_ref, f32[8,128]{1,0:T(8,128)S(1)} %collective-permute-done.8.refs_1_.inner_ref, f32[8,128]{1,0:T(8,128)S(1)} %collective-permute-done.9.refs_2_.outer_ref), custom_call_target="tpu_custom_call" | custom-call | bytes 6000000 | tf_op jit(solution)/shard_map/pallas_call | solution.py:583
  36.0 3.3 %collective-permute-done.11.refs_6_.refs_2_ = f32[16,128]{1,0:T(8,128)S(1)} collective-permute-done((f32[16,128]{1,0:T(8,128)S(1)}, f32[16,128]{1,0:T(8,128)S(1)}, u32[]{:S(2)}, u32[]{:S(2)}) %collective-permute-start.11) | collective-permute-done | bytes 8224 | tf_op jit(solution)/shard_map/ppermute | solution.py:44
  39.3 1.2 %collective-permute-done.12.refs_7_.refs_3_ = f32[112,128]{1,0:T(8,128)S(1)} collective-permute-done((f32[112,128]{1,0:T(8,128)S(1)}, f32[112,128]{1,0:T(8,128)S(1)}, u32[]{:S(2)}, u32[]{:S(2)}) %collective-permute-start.12) | collective-permute-done | bytes 57376 | tf_op jit(solution)/shard_map/ppermute | solution.py:44
  41.1 1.3 %collective-permute-start.14 = (f32[8,128]{1,0:T(8,128)S(1)}, f32[8,128]{1,0:T(8,128)S(1)}, u32[]{:S(2)}, u32[]{:S(2)}) collective-permute-start(f32[8,128]{1,0:T(8,128)S(1)} %get-tuple-element.100), channel_id=1, source_target_pairs={{0,28},{4,8},{8,4},{12,16},{16,12},{20,24},{24,20},{28,0},{1,29},{... | collective-permute-start | bytes 12296 | tf_op jit(solution)/shard_map/ppermute | solution.py:51
  42.4 1.3 %shard_map.131 = (f32[128,1024]{1,0:T(8,128)S(1)}, f32[128,1024]{1,0:T(8,128)S(1)}, f32[8,128]{1,0:T(8,128)S(1)}) custom-call(f32[128,1024]{1,0:T(8,128)S(1)} %get-tuple-element.104.free_ref, f32[128,1024]{1,0:T(8,128)S(1)} %get-tuple-element.105.bound_ref, f32[128,128]{1,0:T(8,128)S(1)} %copy-done.2, f32[1,128]{1,0:T(1,128)S(1)} %bitcast.15, ...), custom_call_target="tpu_custom_call" | custom-call | bytes 3900000 | tf_op jit(solution)/shard_map/pallas_call | solution.py:573
  43.7 1.4 %collective-permute-done.14.refs_2_.outer_ref = f32[8,128]{1,0:T(8,128)S(1)} collective-permute-done((f32[8,128]{1,0:T(8,128)S(1)}, f32[8,128]{1,0:T(8,128)S(1)}, u32[]{:S(2)}, u32[]{:S(2)}) %collective-permute-start.14) | collective-permute-done | bytes 4128 | tf_op jit(solution)/shard_map/ppermute | solution.py:51
  45.4 2.4 %collective-permute-start.15 = (f32[112,128]{1,0:T(8,128)S(1)}, f32[112,128]{1,0:T(8,128)S(1)}, u32[]{:S(2)}, u32[]{:S(2)}) collective-permute-start(f32[112,128]{1,0:T(8,128)S(1)} %get-tuple-element.108), channel_id=1, source_target_pairs={{1,0},{2,1},{3,2},{0,3},{5,4},{6,5},{7,6},{4,7},{9,8},{10,9},{11,1... | collective-permute-start | bytes 172040 | tf_op jit(solution)/shard_map/ppermute | solution.py:44
  48.5 0.8 %shard_map.130 = (f32[3328,128]{1,0:T(8,128)S(1)}, f32[3328,128]{1,0:T(8,128)S(1)}, f32[24,128]{1,0:T(8,128)S(1)}) custom-call(f32[3328,128]{1,0:T(8,128)S(1)} %get-tuple-element.98.refs_0_.post_ref, f32[8,128]{1,0:T(8,128)S(1)} %collective-permute-done.13.refs_1_.inner_ref, f32[8,128]{1,0:T(8,128)S(1)} %collective-permute-done.14.refs_2_.outer_ref), custom_call_target="tpu_custom_call" | custom-call | bytes 6000000 | tf_op jit(solution)/shard_map/pallas_call | solution.py:583
  49.3 3.3 %collective-permute-done.16.refs_6_.refs_2_ = f32[16,128]{1,0:T(8,128)S(1)} collective-permute-done((f32[16,128]{1,0:T(8,128)S(1)}, f32[16,128]{1,0:T(8,128)S(1)}, u32[]{:S(2)}, u32[]{:S(2)}) %collective-permute-start.16) | collective-permute-done | bytes 8224 | tf_op jit(solution)/shard_map/ppermute | solution.py:44
  52.6 1.2 %collective-permute-done.17.refs_7_.refs_3_ = f32[112,128]{1,0:T(8,128)S(1)} collective-permute-done((f32[112,128]{1,0:T(8,128)S(1)}, f32[112,128]{1,0:T(8,128)S(1)}, u32[]{:S(2)}, u32[]{:S(2)}) %collective-permute-start.17) | collective-permute-done | bytes 57376 | tf_op jit(solution)/shard_map/ppermute | solution.py:44
  54.4 0.6 collective-permute-start.19
  55.5 2.8 %collective-permute-done.19.outer_ref = f32[8,128]{1,0:T(8,128)S(1)} collective-permute-done((f32[8,128]{1,0:T(8,128)S(1)}, f32[8,128]{1,0:T(8,128)S(1)}, u32[]{:S(2)}, u32[]{:S(2)}) %collective-permute-start.19) | collective-permute-done | bytes 4128 | tf_op jit(solution)/shard_map/ppermute | solution.py:51
  58.6 0.7 %collective-permute-start.20 = (f32[32,128]{1,0:T(8,128)S(1)}, f32[32,128]{1,0:T(8,128)S(1)}, u32[]{:S(2)}, u32[]{:S(2)}) collective-permute-start(f32[32,128]{1,0:T(8,128)S(1)} %get-tuple-element.116), channel_id=1, source_target_pairs={{3,0},{0,1},{1,2},{2,3},{7,4},{4,5},{5,6},{6,7},{11,8},{8,9},{9,10... | collective-permute-start | bytes 49160 | tf_op jit(solution)/shard_map/ppermute | solution.py:44
  59.3 3.2 %collective-permute-start.21 = (f32[32,128]{1,0:T(8,128)S(1)}, f32[32,128]{1,0:T(8,128)S(1)}, u32[]{:S(2)}, u32[]{:S(2)}) collective-permute-start(f32[32,128]{1,0:T(8,128)S(1)} %get-tuple-element.117), channel_id=1, source_target_pairs={{1,0},{2,1},{3,2},{0,3},{5,4},{6,5},{7,6},{4,7},{9,8},{10,9},{11,1... | collective-permute-start | bytes 49160 | tf_op jit(solution)/shard_map/ppermute | solution.py:44
  62.5 2.3 %shard_map.137 = (f32[128,1024]{1,0:T(8,128)}, f32[128,1024]{1,0:T(8,128)}, f32[8,128]{1,0:T(8,128)}) custom-call(f32[128,1024]{1,0:T(8,128)S(1)} %get-tuple-element.120.free_ref, f32[128,1024]{1,0:T(8,128)S(1)} %get-tuple-element.121.bound_ref, f32[128,128]{1,0:T(8,128)S(1)} %copy-done.2, f32[1,128]{1,0:T(1,128)S(1)} %bitcast.16, f32[1,128]{1,0:T(1,128)S(1)} %bitcast.20, ...), custom_call_target="tpu_custom_call" | custom-call | bytes 3900000 | tf_op jit(solution)/shard_map/pallas_call | solution.py:573
  65.3 0.7 %shard_map.136 = (f32[16,8,128]{2,1,0:T(8,128)}, f32[16,8,128]{2,1,0:T(8,128)}) custom-call(f32[16,8,128]{2,1,0:T(8,128)S(1)} %get-tuple-element.114.drug_part, f32[16,8,128]{2,1,0:T(8,128)S(1)} %get-tuple-element.115.flow_part, f32[32,128]{1,0:T(8,128)S(1)} %collective-permute-done.20.below, f32[32,128]{1,0:T(8,128)S(1)} %collective-permute-done.21.above), custom_call_target="tpu_custom_call" | custom-call | bytes 900000 | tf_op jit(solution)/shard_map/pallas_call | solution.py:594
  (49 shorter events, 6.0 us)
Async XLA Ops:
  0.6 8.1 %copy-start = (f32[26,16,8,128]{3,2,1,0:T(8,128)S(1)}, f32[26,16,8,128]{3,2,1,0:T(8,128)}, u32[]{:S(2)}) copy-start(f32[26,16,8,128]{3,2,1,0:T(8,128)} %pops_ref.1) | copy-start | bytes 5111812
  2.6 10.9 %copy-start.4 = (s32[8,128]{1,0:T(8,128)S(1)}, s32[8,128]{1,0:T(8,128)}, u32[]{:S(2)}) copy-start(s32[8,128]{1,0:T(8,128)} %get-tuple-element.66.refs_3_.code_ref) | copy-start | bytes 12292
  2.6 10.9 %copy-start.6 = (f32[32,128]{1,0:T(8,128)S(1)}, f32[32,128]{1,0:T(8,128)}, u32[]{:S(2)}) copy-start(f32[32,128]{1,0:T(8,128)} %get-tuple-element.67.refs_4_.refs_0_) | copy-start | bytes 49156
  2.6 10.0 %collective-permute-start = (f32[40,128]{1,0:T(8,128)}, f32[40,128]{1,0:T(8,128)S(1)}, u32[]{:S(2)}, u32[]{:S(2)}) collective-permute-start(f32[40,128]{1,0:T(8,128)} %get-tuple-element.68), channel_id=1, source_target_pairs={{1,0},{2,1},{3,2},{0,3},{5,4},{6,5},{7,6},{4,7},{9,8},{10,9},{11,1... | collective-permute-start | bytes 61448 | tf_op jit(solution)/shard_map/ppermute | solution.py:44
  7.7 5.8 %collective-permute-start.2 = (f32[40,128]{1,0:T(8,128)}, f32[40,128]{1,0:T(8,128)S(1)}, u32[]{:S(2)}, u32[]{:S(2)}) collective-permute-start(f32[40,128]{1,0:T(8,128)} %get-tuple-element.70), channel_id=1, source_target_pairs={{3,0},{0,1},{1,2},{2,3},{7,4},{4,5},{5,6},{6,7},{11,8},{8,9},{9,10... | collective-permute-start | bytes 61448 | tf_op jit(solution)/shard_map/ppermute | solution.py:44
  7.7 4.8 %collective-permute-start.1 = (f32[32,128]{1,0:T(8,128)}, f32[32,128]{1,0:T(8,128)S(1)}, u32[]{:S(2)}, u32[]{:S(2)}) collective-permute-start(f32[32,128]{1,0:T(8,128)} %get-tuple-element.69), channel_id=1, source_target_pairs={{2,0},{3,1},{0,2},{1,3},{6,4},{7,5},{4,6},{5,7},{10,8},{11,9},{8,1... | collective-permute-start | bytes 49160 | tf_op jit(solution)/shard_map/ppermute | solution.py:44
  13.5 3.1 %copy-start.1 = (f32[128,1024]{1,0:T(8,128)S(1)}, f32[128,1024]{1,0:T(8,128)}, u32[]{:S(2)}) copy-start(f32[128,1024]{1,0:T(8,128)} %free_ref.3) | copy-start | bytes 1572868
  13.5 3.1 %copy-start.2 = (f32[128,128]{1,0:T(8,128)S(1)}, f32[128,128]{1,0:T(8,128)}, u32[]{:S(2)}) copy-start(f32[128,128]{1,0:T(8,128)} %spread_ref.7) | copy-start | bytes 196612
  13.5 3.1 %copy-start.3 = (f32[128,1024]{1,0:T(8,128)S(1)}, f32[128,1024]{1,0:T(8,128)}, u32[]{:S(2)}) copy-start(f32[128,1024]{1,0:T(8,128)} %bound_ref.1) | copy-start | bytes 1572868
  13.6 3.0 %copy-start.5 = (s32[1024]{0:T(1024)S(1)}, s32[1024]{0:T(1024)}, u32[]{:S(2)}) copy-start(s32[1024]{0:T(1024)} %param.17) | copy-start | bytes 12292
  13.6 3.0 %copy-start.7 = (f32[128]{0:T(128)S(1)}, f32[128]{0:T(128)}, u32[]{:S(2)}) copy-start(f32[128]{0:T(128)} %param.13) | copy-start | bytes 1540
  13.6 3.0 %copy-start.8 = (f32[128]{0:T(128)S(1)}, f32[128]{0:T(128)}, u32[]{:S(2)}) copy-start(f32[128]{0:T(128)} %param.14) | copy-start | bytes 1540
  14.0 3.9 %collective-permute-start.3 = (f32[8,128]{1,0:T(8,128)S(1)}, f32[8,128]{1,0:T(8,128)S(1)}, u32[]{:S(2)}, u32[]{:S(2)}) collective-permute-start(f32[8,128]{1,0:T(8,128)S(1)} %get-tuple-element.72), channel_id=1, source_target_pairs={{0,4},{4,0},{8,12},{12,8},{16,20},{20,16},{24,28},{28,24},{1,5},{5... | collective-permute-start | bytes 12296 | tf_op jit(solution)/shard_map/ppermute | solution.py:51
  14.0 4.0 %collective-permute-start.4 = (f32[8,128]{1,0:T(8,128)S(1)}, f32[8,128]{1,0:T(8,128)S(1)}, u32[]{:S(2)}, u32[]{:S(2)}) collective-permute-start(f32[8,128]{1,0:T(8,128)S(1)} %get-tuple-element.73), channel_id=1, source_target_pairs={{0,28},{4,8},{8,4},{12,16},{16,12},{20,24},{24,20},{28,0},{1,29},{... | collective-permute-start | bytes 12296 | tf_op jit(solution)/shard_map/ppermute | solution.py:51
  18.3 7.7 %collective-permute-start.5 = (f32[112,128]{1,0:T(8,128)S(1)}, f32[112,128]{1,0:T(8,128)S(1)}, u32[]{:S(2)}, u32[]{:S(2)}) collective-permute-start(f32[112,128]{1,0:T(8,128)S(1)} %get-tuple-element.81), channel_id=1, source_target_pairs={{1,0},{2,1},{3,2},{0,3},{5,4},{6,5},{7,6},{4,7},{9,8},{10,9},{11,1... | collective-permute-start | bytes 172040 | tf_op jit(solution)/shard_map/ppermute | solution.py:44
  21.3 6.0 %collective-permute-start.7 = (f32[112,128]{1,0:T(8,128)S(1)}, f32[112,128]{1,0:T(8,128)S(1)}, u32[]{:S(2)}, u32[]{:S(2)}) collective-permute-start(f32[112,128]{1,0:T(8,128)S(1)} %get-tuple-element.83), channel_id=1, source_target_pairs={{3,0},{0,1},{1,2},{2,3},{7,4},{4,5},{5,6},{6,7},{11,8},{8,9},{9,10... | collective-permute-start | bytes 172040 | tf_op jit(solution)/shard_map/ppermute | solution.py:44
  21.3 4.7 %collective-permute-start.6 = (f32[16,128]{1,0:T(8,128)S(1)}, f32[16,128]{1,0:T(8,128)S(1)}, u32[]{:S(2)}, u32[]{:S(2)}) collective-permute-start(f32[16,128]{1,0:T(8,128)S(1)} %get-tuple-element.82), channel_id=1, source_target_pairs={{2,0},{3,1},{0,2},{1,3},{6,4},{7,5},{4,6},{5,7},{10,8},{11,9},{8,1... | collective-permute-start | bytes 24584 | tf_op jit(solution)/shard_map/ppermute | solution.py:44
  27.7 3.6 %collective-permute-start.8 = (f32[8,128]{1,0:T(8,128)S(1)}, f32[8,128]{1,0:T(8,128)S(1)}, u32[]{:S(2)}, u32[]{:S(2)}) collective-permute-start(f32[8,128]{1,0:T(8,128)S(1)} %get-tuple-element.86), channel_id=1, source_target_pairs={{0,4},{4,0},{8,12},{12,8},{16,20},{20,16},{24,28},{28,24},{1,5},{5... | collective-permute-start | bytes 12296 | tf_op jit(solution)/shard_map/ppermute | solution.py:51
  27.8 4.0 %collective-permute-start.9 = (f32[8,128]{1,0:T(8,128)S(1)}, f32[8,128]{1,0:T(8,128)S(1)}, u32[]{:S(2)}, u32[]{:S(2)}) collective-permute-start(f32[8,128]{1,0:T(8,128)S(1)} %get-tuple-element.87), channel_id=1, source_target_pairs={{0,28},{4,8},{8,4},{12,16},{16,12},{20,24},{24,20},{28,0},{1,29},{... | collective-permute-start | bytes 12296 | tf_op jit(solution)/shard_map/ppermute | solution.py:51
  32.1 7.2 %collective-permute-start.10 = (f32[112,128]{1,0:T(8,128)S(1)}, f32[112,128]{1,0:T(8,128)S(1)}, u32[]{:S(2)}, u32[]{:S(2)}) collective-permute-start(f32[112,128]{1,0:T(8,128)S(1)} %get-tuple-element.95), channel_id=1, source_target_pairs={{1,0},{2,1},{3,2},{0,3},{5,4},{6,5},{7,6},{4,7},{9,8},{10,9},{11,1... | collective-permute-start | bytes 172040 | tf_op jit(solution)/shard_map/ppermute | solution.py:44
  34.6 6.0 %collective-permute-start.12 = (f32[112,128]{1,0:T(8,128)S(1)}, f32[112,128]{1,0:T(8,128)S(1)}, u32[]{:S(2)}, u32[]{:S(2)}) collective-permute-start(f32[112,128]{1,0:T(8,128)S(1)} %get-tuple-element.97), channel_id=1, source_target_pairs={{3,0},{0,1},{1,2},{2,3},{7,4},{4,5},{5,6},{6,7},{11,8},{8,9},{9,10... | collective-permute-start | bytes 172040 | tf_op jit(solution)/shard_map/ppermute | solution.py:44
  34.6 4.7 %collective-permute-start.11 = (f32[16,128]{1,0:T(8,128)S(1)}, f32[16,128]{1,0:T(8,128)S(1)}, u32[]{:S(2)}, u32[]{:S(2)}) collective-permute-start(f32[16,128]{1,0:T(8,128)S(1)} %get-tuple-element.96), channel_id=1, source_target_pairs={{2,0},{3,1},{0,2},{1,3},{6,4},{7,5},{4,6},{5,7},{10,8},{11,9},{8,1... | collective-permute-start | bytes 24584 | tf_op jit(solution)/shard_map/ppermute | solution.py:44
  41.0 2.7 %collective-permute-start.13 = (f32[8,128]{1,0:T(8,128)S(1)}, f32[8,128]{1,0:T(8,128)S(1)}, u32[]{:S(2)}, u32[]{:S(2)}) collective-permute-start(f32[8,128]{1,0:T(8,128)S(1)} %get-tuple-element.99), channel_id=1, source_target_pairs={{0,4},{4,0},{8,12},{12,8},{16,20},{20,16},{24,28},{28,24},{1,5},{5... | collective-permute-start | bytes 12296 | tf_op jit(solution)/shard_map/ppermute | solution.py:51
  41.1 4.0 %collective-permute-start.14 = (f32[8,128]{1,0:T(8,128)S(1)}, f32[8,128]{1,0:T(8,128)S(1)}, u32[]{:S(2)}, u32[]{:S(2)}) collective-permute-start(f32[8,128]{1,0:T(8,128)S(1)} %get-tuple-element.100), channel_id=1, source_target_pairs={{0,28},{4,8},{8,4},{12,16},{16,12},{20,24},{24,20},{28,0},{1,29},{... | collective-permute-start | bytes 12296 | tf_op jit(solution)/shard_map/ppermute | solution.py:51
  45.4 7.2 %collective-permute-start.15 = (f32[112,128]{1,0:T(8,128)S(1)}, f32[112,128]{1,0:T(8,128)S(1)}, u32[]{:S(2)}, u32[]{:S(2)}) collective-permute-start(f32[112,128]{1,0:T(8,128)S(1)} %get-tuple-element.108), channel_id=1, source_target_pairs={{1,0},{2,1},{3,2},{0,3},{5,4},{6,5},{7,6},{4,7},{9,8},{10,9},{11,1... | collective-permute-start | bytes 172040 | tf_op jit(solution)/shard_map/ppermute | solution.py:44
  47.8 6.0 %collective-permute-start.17 = (f32[112,128]{1,0:T(8,128)S(1)}, f32[112,128]{1,0:T(8,128)S(1)}, u32[]{:S(2)}, u32[]{:S(2)}) collective-permute-start(f32[112,128]{1,0:T(8,128)S(1)} %get-tuple-element.110), channel_id=1, source_target_pairs={{3,0},{0,1},{1,2},{2,3},{7,4},{4,5},{5,6},{6,7},{11,8},{8,9},{9,10... | collective-permute-start | bytes 172040 | tf_op jit(solution)/shard_map/ppermute | solution.py:44
  47.8 4.7 %collective-permute-start.16 = (f32[16,128]{1,0:T(8,128)S(1)}, f32[16,128]{1,0:T(8,128)S(1)}, u32[]{:S(2)}, u32[]{:S(2)}) collective-permute-start(f32[16,128]{1,0:T(8,128)S(1)} %get-tuple-element.109), channel_id=1, source_target_pairs={{2,0},{3,1},{0,2},{1,3},{6,4},{7,5},{4,6},{5,7},{10,8},{11,9},{8,1... | collective-permute-start | bytes 24584 | tf_op jit(solution)/shard_map/ppermute | solution.py:44
  54.3 1.2 %collective-permute-start.18 = (f32[8,128]{1,0:T(8,128)S(1)}, f32[8,128]{1,0:T(8,128)S(1)}, u32[]{:S(2)}, u32[]{:S(2)}) collective-permute-start(f32[8,128]{1,0:T(8,128)S(1)} %get-tuple-element.112), channel_id=1, source_target_pairs={{0,4},{4,0},{8,12},{12,8},{16,20},{20,16},{24,28},{28,24},{1,5},{5... | collective-permute-start | bytes 12296 | tf_op jit(solution)/shard_map/ppermute | solution.py:51
  54.4 4.0 %collective-permute-start.19 = (f32[8,128]{1,0:T(8,128)S(1)}, f32[8,128]{1,0:T(8,128)S(1)}, u32[]{:S(2)}, u32[]{:S(2)}) collective-permute-start(f32[8,128]{1,0:T(8,128)S(1)} %get-tuple-element.113), channel_id=1, source_target_pairs={{0,28},{4,8},{8,4},{12,16},{16,12},{20,24},{24,20},{28,0},{1,29},{... | collective-permute-start | bytes 12296 | tf_op jit(solution)/shard_map/ppermute | solution.py:51
  58.6 6.7 %collective-permute-start.20 = (f32[32,128]{1,0:T(8,128)S(1)}, f32[32,128]{1,0:T(8,128)S(1)}, u32[]{:S(2)}, u32[]{:S(2)}) collective-permute-start(f32[32,128]{1,0:T(8,128)S(1)} %get-tuple-element.116), channel_id=1, source_target_pairs={{3,0},{0,1},{1,2},{2,3},{7,4},{4,5},{5,6},{6,7},{11,8},{8,9},{9,10... | collective-permute-start | bytes 49160 | tf_op jit(solution)/shard_map/ppermute | solution.py:44
  59.3 6.0 %collective-permute-start.21 = (f32[32,128]{1,0:T(8,128)S(1)}, f32[32,128]{1,0:T(8,128)S(1)}, u32[]{:S(2)}, u32[]{:S(2)}) collective-permute-start(f32[32,128]{1,0:T(8,128)S(1)} %get-tuple-element.117), channel_id=1, source_target_pairs={{1,0},{2,1},{3,2},{0,3},{5,4},{6,5},{7,6},{4,7},{9,8},{10,9},{11,1... | collective-permute-start | bytes 49160 | tf_op jit(solution)/shard_map/ppermute | solution.py:44

commit v3 on v2

--- a/solution.py
+++ b/solution.py
@@ -25,6 +25,9 @@
 SECTOR_FALLING = [4, 8, 9, 16, 18, 23]
 SLAB_RISING = [1, 7, 9, 11, 13, 20]
 SLAB_FALLING = [2, 8, 10, 12, 14, 21]
+LEVEL_KEPT = [0, 3, 4, 5, 6, 15, 16, 17, 18, 19, 22, 23, 24, 25]
+RISE_SLOTS = [(m, 0) for m in SLAB_RISING] + [(m, 0) for m in LEVEL_KEPT] + [(m, 1) for m in SLAB_RISING] + [(14, 0)]
+FALL_SLOTS = [(m, 0) for m in SLAB_FALLING] + [(m, 0) for m in LEVEL_KEPT] + [(m, 1) for m in SLAB_FALLING] + [(11, 0)]
 PAIRS = [(1, 2), (3, 4), (5, 6), (7, 8), (9, 10), (11, 12), (13, 14), (15, 16), (17, 18)]
 FLOWS = 19
 MEMBERS = 26
@@ -55,9 +58,11 @@
     return jnp.where(lax.axis_index("ax") % 2 == 0, even, odd)
 
 
-def axial_rims(inner_ref, outer_ref):
-    inner, outer = inner_ref[...], outer_ref[...]
-    return by_parity(outer, inner), by_parity(inner, outer)
+def axial_rims(packed, first_ref, second_ref, across):
+    first, second = first_ref[0:across, :], second_ref[0:across, :]
+    if not packed:
+        return first, second
+    return by_parity(second, first), by_parity(first, second)
 
 
 def lanes(shape):
@@ -285,13 +290,13 @@
             out[4 * across:5 * across] = jnp.broadcast_to(edge, (across, width)).astype(F32)
 
 
-def bulk_kernel(first, radial, across, *refs):
+def bulk_kernel(first, packed, radial, across, *refs):
     if first:
         state_ref, post_ref, speed_ref = refs
     else:
         old_ref, inner_ref, outer_ref, state_ref, post_ref, speed_ref = refs
         old = Planes(old_ref, radial, across)
-        behind, ahead = axial_rims(inner_ref, outer_ref)
+        behind, ahead = axial_rims(packed, inner_ref, outer_ref, across)
     state, post = Planes(state_ref, radial, across), Planes(post_ref, radial, across)
     for level in range(radial):
         if first:
@@ -310,42 +315,144 @@
             post.put(member, level, value)
 
 
-def flux_kernel(sectors, first, radial, *refs):
+def rim_tiles(post, slots, rising):
+    radial, across = post.radial, post.across
+    along = post.ref.shape[-1]
+    each = along // radial
+    lane = lanes((across, along))
+    tiles = []
+    for place, (member, column) in enumerate(slots):
+        if place % each == 0:
+            tiles.append(jnp.zeros((across, along), F32))
+        origin = along - 1 - column if rising else column
+        only_last = place == len(slots) - 1
+        for level in range(radial - 1 if only_last else 0, radial):
+            slot = (place % each) * radial + level
+            value = pltpu.roll(post.get(member, level), (slot - origin) % along, 1)
+            tiles[-1] = jnp.where(lane == slot, value, tiles[-1])
+    return tiles
+
+
+class Ghosts:
+    def __init__(self, radial, across, along, behind, ahead, rise, fall):
+        self.radial, self.across, self.along = radial, across, along
+        self.behind, self.ahead, self.rise, self.fall = behind, ahead, rise, fall
+        lane = lanes((across, along))
+        self.is_behind = lane < radial
+        self.level = jnp.where(self.is_behind, lane, lane - radial)
+
+    def pick(self, message, slot, target):
+        each = self.along // self.radial
+        tile = message[(slot // each) * self.across:(slot // each + 1) * self.across, :]
+        return pltpu.roll(tile, (target - (slot % each) * self.radial) % self.along, 1)
+
+    def join(self, first, second):
+        return jnp.where(self.is_behind, self.pick(*first, 0), self.pick(*second, self.radial))
+
+    def arriving(self, member):
+        step = VELOCITIES[member][0]
+        rise, fall = RISE_SLOTS.index, FALL_SLOTS.index
+        if step == 1:
+            return self.join((self.behind, rise((member, 1))), (self.rise, rise((member, 0))))
+        if step == -1:
+            return self.join((self.fall, fall((member, 0))), (self.ahead, fall((member, 1))))
+        return self.join((self.behind, rise((member, 0))), (self.ahead, fall((member, 0))))
+
+    def own(self, member):
+        return self.join((self.behind, RISE_SLOTS.index((member, 0))), (self.ahead, FALL_SLOTS.index((member, 0))))
+
+    def risen(self, member):
+        value = self.arriving(member)
+        step = VELOCITIES[member][2]
+        if step == 1:
+            return jnp.where(self.level == 0, self.arriving(MIRROR[member]), pltpu.roll(value, 1, 1))
+        if step == -1:
+            return pltpu.roll(value, self.along - 1, 1)
+        return value
+
+    def streamed(self, member, below_rows, above_rows):
+        value = self.risen(member)
+        row = sublanes(value.shape)
+        step = VELOCITIES[member][1]
+        if step == 1:
+            place = SECTOR_RISING.index(member)
+            value = jnp.where(row == 0, below_rows[place:place + 1, :], pltpu.roll(value, 1, 0))
+        elif step == -1:
+            place = SECTOR_FALLING.index(member)
+            value = jnp.where(row == self.across - 1, above_rows[place:place + 1, :], pltpu.roll(value, self.across - 1, 0))
+        if VELOCITIES[member][2] == -1:
+            value = jnp.where(self.level == self.radial - 1, self.own(OPPOSITE[member]), value)
+        return value
+
+
+def gather_cells(table, codes, width):
+    group = codes // width
+    low = codes - group * width
+    row = jnp.zeros(codes.shape, F32)
+    for place in range(table.shape[0]):
+        row = jnp.where(group == place, table[place:place + 1, :], row)
+    return jnp.sum(jnp.where(lanes(codes.shape) == low, row, 0.0), axis=1, keepdims=True)
+
+
+def table_of(inbox, start, across):
+    return jnp.concatenate([box[start:start + across, :] for box in inbox], axis=0)
+
+
+def flux_kernel(sectors, step, radial, *refs):
+    first, odd = step == 0, step % 2 == 1
     refs = list(refs)
-    state_ref, bulk_ref, speed_ref, code_ref = refs[:4]
-    inbox = refs[4:4 + sectors]
-    refs = refs[4 + sectors:]
-    if first:
-        post_ref, inner_ref, outer_ref, open_ref, counts_ref, edges_ref = refs
-    else:
-        open_ref, post_ref, inner_ref, outer_ref = refs
+    state_ref, bulk_ref, speed_ref, code_ref, strut_ref, coef_ref, on_ref, off_ref = refs[:8]
+    inbox = refs[8:8 + sectors]
+    refs = refs[8 + sectors:]
+    open_ref = counts_ref = ghost_code_ref = ghost_open_ref = None
+    if not first:
+        open_ref, counts_ref = refs[:2]
+        refs = refs[2:]
+    if odd:
+        sent_refs, got_refs = refs[:2], refs[2:4]
+        refs = refs[4:]
+        if step > 1:
+            ghost_code_ref, ghost_open_ref = refs[:2]
+            refs = refs[2:]
+    post_ref, one_ref, two_ref, added_ref, top_ref = refs[:5]
+    refs = refs[5:]
     del bulk_ref
     across, along = code_ref.shape
+    plane = (across, along)
     end = radial - 1
     state, post = Planes(state_ref, radial, across), Planes(post_ref, radial, across)
     codes = code_list(code_ref[...])
-    offset = 2 * across if first else across
-    table = jnp.concatenate([box[offset:offset + across, :] for box in inbox], axis=0)
-    picked = jnp.concatenate(gather_rows(table, codes, along), axis=0)
     below, above = inbox[sectors - 1], inbox[1]
+    base = 2 * across if first else across
+    picked = jnp.concatenate(gather_rows(table_of(inbox, base, across), codes, along), axis=0)
     if first:
-        table = jnp.concatenate([box[3 * across:4 * across, :] for box in inbox], axis=0)
-        openness = jnp.concatenate(gather_rows(table, codes, along), axis=0)
-        open_ref[...] = openness
+        openness = jnp.concatenate(gather_rows(table_of(inbox, 3 * across, across), codes, along), axis=0)
         counts = inbox[0][across:2 * across, :]
         for box in inbox[1:]:
             counts = counts + box[across:2 * across, :]
-        counts_ref[...] = counts
+        refs[0][...] = openness
+        refs[1][...] = counts
         count, limit = across * along, sectors * across * along
         up = above[4 * across:5 * across, :].astype(jnp.int32) + count
         down = below[4 * across:5 * across, :].astype(jnp.int32) - count
         up = jnp.where(up >= limit, up - limit, up)
         down = jnp.where(down < 0, down + limit, down)
-        edges_ref[...] = jnp.where(sublanes(up.shape) == 0, up, down)
+        refs[2][...] = jnp.where(sublanes(plane) == 0, up, down)
     else:
-        openness = open_ref[...]
-    start = 2 * across
-    row = sublanes((across, along))
+        openness, counts = open_ref[...], counts_ref[...]
+    total = inbox[0][0:across, :]
+    for box in inbox[1:]:
+        total = total + box[0:across, :]
+    strut = strut_ref[...].astype(F32)
+    shut = PERMEABILITY * (1.0 - strut)
+    added = shut * (total - counts * inbox[0][base:base + across, :]) + RELEASE_RATE * strut
+    added_ref[...] = added
+    free = coef_ref[0:across, :] + added * coef_ref[across:2 * across, :]
+    bound = coef_ref[2 * across:3 * across, :] + added * coef_ref[3 * across:4 * across, :]
+    top = free - (on_ref[0:1, 0:1] * free * (1.0 - bound) - off_ref[0:1, 0:1] * bound)
+    top_ref[...] = top
+    start = rims_start(step, across)
+    row = sublanes(plane)
     drugs = [state.get(member, end) for member in range(FLOWS, MEMBERS)]
     if not first:
         last = start + SECTOR_RISING.index(FLOWS + 3) * radial + end
@@ -379,52 +486,135 @@
                 results = results + relax_drug(members[FLOWS:], velocity)
                 for member, value in enumerate(results):
                     post.put_rows(member, level, block, side, value)
-    rise = jnp.zeros((across, along), F32)
-    fall = jnp.zeros((across, along), F32)
-    lane = lanes((across, along))
-    for level in range(radial):
-        for place, member in enumerate(SLAB_RISING):
-            slot = place * radial + level
-            rise = jnp.where(lane == slot, pltpu.roll(post.get(member, level), (slot + 1) % along, 1), rise)
-        for place, member in enumerate(SLAB_FALLING):
-            slot = place * radial + level
-            fall = jnp.where(lane == slot, pltpu.roll(post.get(member, level), slot, 1), fall)
-    inner_ref[...] = by_parity(rise, fall)
-    outer_ref[...] = by_parity(fall, rise)
-
-
-def wall_kernel(sectors, free_ref, bound_ref, spread_ref, on_ref, off_ref, strut_ref, counts_ref, *refs):
-    inbox, (new_free, new_bound, top_ref) = refs[:sectors], refs[sectors:]
-    across, width = strut_ref.shape
+    if not odd:
+        rise = rim_tiles(post, RISE_SLOTS, True) + [top]
+        fall = rim_tiles(post, FALL_SLOTS, False) + [top]
+        if first:
+            own = code_ref[...].astype(F32)
+            rise = rise + [shut, pltpu.roll(own, 1, 1)]
+            fall = fall + [shut, own]
+        for place, (up, down) in enumerate(zip(rise, fall, strict=True)):
+            one_ref[place * across:(place + 1) * across, :] = by_parity(up, down)
+            two_ref[place * across:(place + 1) * across, :] = by_parity(down, up)
+        return
+    rise, fall = by_parity(sent_refs[0][...], sent_refs[1][...]), by_parity(sent_refs[1][...], sent_refs[0][...])
+    behind, ahead = by_parity(got_refs[1][...], got_refs[0][...]), by_parity(got_refs[0][...], got_refs[1][...])
+    ghosts = Ghosts(radial, across, along, behind, ahead, rise, fall)
+    tables = [table_of(inbox, (2 + side) * across, across) for side in range(2)]
+    if step == 1:
+        place = code_place(radial, across, along)
+        sides = [message[place:place + across, 0:1].astype(jnp.int32) for message in (behind, ahead)]
+        sides = [jnp.broadcast_to(side, plane) for side in sides]
+        opens = [gather_cells(table_of(inbox, (4 + side) * across, across), sides[side], along) for side in range(2)]
+        for side in range(2):
+            refs[0][side * across:(side + 1) * across, :] = sides[side]
+            refs[1][side * across:(side + 1) * across, :] = jnp.broadcast_to(opens[side], plane)
+    else:
+        sides = [ghost_code_ref[side * across:(side + 1) * across, :] for side in range(2)]
+        opens = [ghost_open_ref[side * across:(side + 1) * across, 0:1] for side in range(2)]
+    tops = [gather_cells(tables[side], sides[side], along) for side in range(2)]
+    ghost_start = start + len(SECTOR_RISING) * radial
+    below_rows = below[ghost_start:ghost_start + across, :]
+    above_rows = above[ghost_start:ghost_start + across, :]
+    members = [ghosts.streamed(member, below_rows, above_rows) for member in range(MEMBERS)]
+    surface = members[FLOWS]
+    for member in range(FLOWS + 1, MEMBERS):
+        surface = surface + members[member]
+    ghost_flux = jnp.where(ghosts.is_behind, opens[0] * (surface - tops[0]), opens[1] * (surface - tops[1]))
+    ghost_flux = jnp.where(ghosts.level == end, ghost_flux, 0.0)
+    members = members[:FLOWS] + [members[member] - WEIGHTS[member] * ghost_flux for member in range(FLOWS, MEMBERS)]
+    results, velocity = relax_flow(members[:FLOWS])
+    results = results + relax_drug(members[FLOWS:], velocity)
+    lane = lanes(plane)
+    behind, ahead = jnp.zeros(plane, F32), jnp.zeros(plane, F32)
+    for place in range(len(SLAB_RISING)):
+        here = (lane >= place * radial) & (lane < (place + 1) * radial)
+        behind = jnp.where(here, pltpu.roll(results[SLAB_RISING[place]], (place * radial) % along, 1), behind)
+        ahead = jnp.where(here, pltpu.roll(results[SLAB_FALLING[place]], ((place - 1) * radial) % along, 1), ahead)
+    one_ref[...] = behind
+    two_ref[...] = ahead
+
+
+def code_place(radial, across, along):
+    return (rim_rows(radial, across, along) // across + 2) * across
+
+
+def rim_rows(radial, across, along):
+    return -(-len(RISE_SLOTS) // (along // radial)) * across
+
+
+def rims_start(step, across):
+    return (6 if step == 1 else 4 if step % 2 else 2) * across
+
+
+def wall_rates(spread_ref, on_ref, off_ref):
     depth = spread_ref.shape[0]
-    total = inbox[0][0:across, :]
-    for box in inbox[1:]:
-        total = total + box[0:across, :]
-    strut = strut_ref[...].astype(F32)
-    first = pack_lines(free_ref[0:1, :], width)
-    added = (PERMEABILITY * (1.0 - strut)) * (total - counts_ref[...] * first) + RELEASE_RATE * strut
-    spread = spread_ref[...]
-    rate_on = jnp.transpose(jnp.broadcast_to(on_ref[...], (depth, depth)))
-    rate_off = jnp.transpose(jnp.broadcast_to(off_ref[...], (depth, depth)))
-    is_top = sublanes((depth, width)) == 0
+    shape = (depth, depth)
+    rate_on = jnp.transpose(jnp.broadcast_to(on_ref[...], shape))
+    rate_off = jnp.transpose(jnp.broadcast_to(off_ref[...], shape))
+    entry = jnp.broadcast_to(spread_ref[:, 0:1], shape)
+    top = jnp.transpose(jnp.broadcast_to(spread_ref[0:1, :], shape))
+    return rate_on, rate_off, entry, top
+
+
+def plan_ahead(spread, rates, free, bound):
+    rate_on, rate_off, entry, top = rates
+    moved = jnp.dot(spread, free, precision=lax.Precision.HIGHEST, preferred_element_type=F32)
+    rate = rate_on * moved * (1.0 - bound) - rate_off * bound
+    gain = rate_on * entry * (1.0 - bound)
+    first = jnp.sum(top * (moved - rate), axis=0, keepdims=True)
+    slope = jnp.sum(top * (entry - gain), axis=0, keepdims=True)
+    return moved, (first, slope, bound[0:1, :] + rate[0:1, :], gain[0:1, :])
+
+
+def plan_kernel(free_ref, bound_ref, spread_ref, on_ref, off_ref, moved_ref, coef_ref):
+    rates = wall_rates(spread_ref, on_ref, off_ref)
+    width = coef_ref.shape[1]
+    across = coef_ref.shape[0] // 4
     for row in range(across):
         place = slice(row * width, (row + 1) * width)
-        free = free_ref[:, place] + jnp.where(is_top, added[row:row + 1, :], 0.0)
+        moved, parts = plan_ahead(spread_ref[...], rates, free_ref[:, place], bound_ref[:, place])
+        moved_ref[:, place] = moved
+        for index, part in enumerate(parts):
+            coef_ref[index * across + row:index * across + row + 1, :] = part
+
+
+def wall_kernel(last, moved_ref, bound_ref, added_ref, spread_ref, on_ref, off_ref, *outs):
+    rates = wall_rates(spread_ref, on_ref, off_ref)
+    rate_on, rate_off, entry, _ = rates
+    across, width = added_ref.shape
+    spread = spread_ref[...]
+    for row in range(across):
+        place = slice(row * width, (row + 1) * width)
+        free = moved_ref[:, place] + entry * added_ref[row:row + 1, :]
         bound = bound_ref[:, place]
-        for _ in range(SUB):
-            free = jnp.dot(spread, free, precision=lax.Precision.HIGHEST, preferred_element_type=F32)
+        for substep in range(SUB):
+            if substep:
+                free = jnp.dot(spread, free, precision=lax.Precision.HIGHEST, preferred_element_type=F32)
             rate = rate_on * free * (1.0 - bound) - rate_off * bound
             free = free - rate
             bound = bound + rate
-        new_free[:, place] = free
-        new_bound[:, place] = bound
-        top_ref[row:row + 1, :] = free[0:1, :]
-
-
-def send_kernel(sectors, radial, post_ref, inner_ref, outer_ref, code_ref, edges_ref, top_ref, *outs):
+        outs[1][:, place] = bound
+        if last:
+            outs[0][:, place] = free
+        else:
+            moved, parts = plan_ahead(spread, rates, free, bound)
+            outs[0][:, place] = moved
+            for index, part in enumerate(parts):
+                outs[2][index * across + row:index * across + row + 1, :] = part
+
+
+def send_kernel(sectors, step, radial, *refs):
+    packed = step % 2 == 0
+    post_ref, one_ref, two_ref, code_ref, edges_ref, top_ref = refs[:6]
+    refs = refs[6:]
+    if packed:
+        sent_refs, outs = refs[:2], refs[2:]
+    else:
+        outs = refs
     across, along = code_ref.shape
     post = Planes(post_ref, radial, across)
-    behind, ahead = axial_rims(inner_ref, outer_ref)
+    behind, ahead = axial_rims(packed, one_ref, two_ref, across)
     end = radial - 1
     row = sublanes((across, along))
     surface = post.get(FLOWS, end) + post.get(FLOWS + 5, end - 1) + post.get(FLOWS + 5, end)
@@ -437,26 +627,43 @@
     values = code_list(surface) + [rising[across - 1:across, :], falling[0:1, :]]
     codes = code_list(code_ref[...]) + [edges_ref[0:1, :], edges_ref[1:2, :]]
     sums = scatter_rows(values, codes, sectors * across, along)
-    top = top_ref[...]
+    parts = [top_ref[...]]
+    if packed:
+        whole_behind = by_parity(two_ref[...], one_ref[...])
+        whole_ahead = by_parity(one_ref[...], two_ref[...])
+        skip = rim_rows(radial, across, along)
+        for index in range(2 if step == 0 else 1):
+            place = skip + index * across
+            parts = parts + [whole_behind[place:place + across, :], whole_ahead[place:place + across, :]]
     for rel in range(sectors):
         outs[rel][0:across] = sums[rel * across:(rel + 1) * across]
-        outs[rel][across:2 * across] = top
-    start = 2 * across
+        for index, part in enumerate(parts):
+            outs[rel][(1 + index) * across:(2 + index) * across] = part
+    start = rims_start(step + 1, across)
     for out, places, side in ((outs[1], SECTOR_RISING, across - 1), (outs[sectors - 1], SECTOR_FALLING, 0)):
         for place, member in enumerate(places):
-            step = VELOCITIES[member][0]
+            moving = VELOCITIES[member][0]
             base = start + place * radial
-            if step:
+            if moving:
                 for level in range(radial):
-                    value = axial_shift(post.get(member, level), step, member, level, radial, behind, ahead)
+                    value = axial_shift(post.get(member, level), moving, member, level, radial, behind, ahead)
                     out[base + level:base + level + 1, :] = value[side:side + 1, :]
             else:
                 out[base:base + radial, :] = post.rows(member, 0, radial, side)
+    if packed:
+        rise, fall = by_parity(sent_refs[0][...], sent_refs[1][...]), by_parity(sent_refs[1][...], sent_refs[0][...])
+        ghosts = Ghosts(radial, across, along, whole_behind, whole_ahead, rise, fall)
+        base = start + len(SECTOR_RISING) * radial
+        for out, places, side in ((outs[1], SECTOR_RISING, across - 1), (outs[sectors - 1], SECTOR_FALLING, 0)):
+            for place, member in enumerate(places):
+                out[base + place:base + place + 1, :] = ghosts.risen(member)[side:side + 1, :]
+            for place in range(len(places), across):
+                out[base + place:base + place + 1, :] = jnp.zeros((1, along), F32)
 
 
 def last_send_kernel(radial, across, post_ref, inner_ref, outer_ref, up_ref, down_ref):
     post = Planes(post_ref, radial, across)
-    behind, ahead = axial_rims(inner_ref, outer_ref)
+    behind, ahead = axial_rims(False, inner_ref, outer_ref, across)
     for out, drug, plus, minus, side in ((up_ref, FLOWS + 3, 7, 10, across - 1), (down_ref, FLOWS + 4, 9, 8, 0)):
         out[0:radial, :] = post.rows(drug, 0, radial, side)
         for level in range(radial):
@@ -467,7 +674,7 @@
 
 def fields_kernel(radial, across, post_ref, inner_ref, outer_ref, drug_ref, flow_ref):
     post = Planes(post_ref, radial, across)
-    behind, ahead = axial_rims(inner_ref, outer_ref)
+    behind, ahead = axial_rims(False, inner_ref, outer_ref, across)
     for level in range(radial):
         def member_of(member):
             value = streamed(post, member, level, behind, ahead)
@@ -554,43 +761,67 @@
     inbox = exchange(boxes)
     state = populations.reshape(flat)
     speeds = (3 * across, along)
-    bulk, speed = kernel_call(functools.partial(bulk_kernel, True, radial, across), [flat, speeds], 1, 1.5)(state)
-    free, bound = wall_free, wall_bound
-    openness = counts = edges = None
+    four = (4 * across, along)
+    two = (2 * across, along)
+    rim = rim_rows(radial, across, along)
+    shapes = wall_free.shape
+    bulk, speed = kernel_call(functools.partial(bulk_kernel, True, True, radial, across), [flat, speeds], 1, 1.5)(state)
+    moved, coefs = kernel_call(plan_kernel, [shapes, four], 5, 1.0)(
+        wall_free, wall_bound, wall_propagator, rate_on, rate_off
+    )
+    bound = wall_bound
+    fixed, ghost = [], []
+    edges = sent = got = None
     for step in range(STEPS):
-        first, last = step == 0, step == STEPS - 1
-        outs = [flat, plane, plane]
-        if first:
+        odd, last = step % 2 == 1, step == STEPS - 1
+        if odd:
+            pair = [plane, plane]
+        else:
+            pair = [(rim + (3 if step == 0 else 1) * across, along)] * 2
+        outs = [flat] + pair + [plane, plane]
+        if step == 0:
             outs = outs + [plane, plane, jax.ShapeDtypeStruct(plane, jnp.int32)]
-        extra = [] if first else [openness]
+        if step == 1:
+            outs = outs + [jax.ShapeDtypeStruct(two, jnp.int32), two]
+        extra = fixed + ([*sent, *got, *ghost] if odd else [])
+        post, one, other, added, top, *rest = kernel_call(
+            functools.partial(flux_kernel, sectors, step, radial), outs, 8 + sectors + len(extra), 0.8, {1: 0}
+        )(state, bulk, speed, codes, strut, coefs, rate_on, rate_off, *inbox, *extra)
+        if step == 0:
+            fixed, edges = rest[:2], rest[2]
+        if step == 1:
+            ghost = rest
+        if odd:
+            rims_in, own = [one, other], []
+        else:
+            sent = [one, other]
+            got = paired(*sent)
+            rims_in, own = [*got], sent
         results = kernel_call(
-            functools.partial(flux_kernel, sectors, first, radial), outs, 4 + sectors + len(extra), 0.8, {1: 0}
-        )(state, bulk, speed, codes, *inbox, *extra)
-        post = results[0]
-        if first:
-            openness, counts, edges = results[3:]
-        inner, outer = paired(*results[1:3])
-        free, bound, top = kernel_call(
-            functools.partial(wall_kernel, sectors), [wall_free.shape, wall_free.shape, plane], 7 + sectors, 1.3
-        )(free, bound, wall_propagator, rate_on, rate_off, strut, counts, *inbox)
+            functools.partial(wall_kernel, last), [shapes, shapes] + ([] if last else [four]), 6, 1.5
+        )(moved, bound, added, wall_propagator, rate_on, rate_off)
         if last:
+            free, bound = results
             continue
-        sizes = [(2 * across + (rims if hop in (1, sectors - 1) else 0), along) for hop in range(sectors)]
-        boxes = kernel_call(functools.partial(send_kernel, sectors, radial), sizes, 6, 0.3)(
-            post, inner, outer, codes, edges, top
-        )
+        moved, bound, coefs = results
+        start = rims_start(step + 1, across)
+        long = start + rims + (0 if odd else across)
+        sizes = [(long if hop in (1, sectors - 1) else start, along) for hop in range(sectors)]
+        boxes = kernel_call(
+            functools.partial(send_kernel, sectors, step, radial), sizes, 6 + len(own), 0.3
+        )(post, *rims_in, codes, edges, top, *own)
         inbox = exchange(boxes)
         state, bulk, speed = kernel_call(
-            functools.partial(bulk_kernel, False, radial, across), [flat, flat, speeds], 3, 2.0
-        )(post, inner, outer)
+            functools.partial(bulk_kernel, False, not odd, radial, across), [flat, flat, speeds], 3, 2.0
+        )(post, *rims_in)
     up, down = kernel_call(
         functools.partial(last_send_kernel, radial, across), [(2 * radial, along)] * 2, 3, 0.2
-    )(post, inner, outer)
+    )(post, *rims_in)
     below = shifted(up, "th", 1)
     above = shifted(down, "th", -1)
     parts = kernel_call(
         functools.partial(fields_kernel, radial, across), [(radial,) + plane] * 2, 3, 1.0
-    )(post, inner, outer)
+    )(post, *rims_in)
     drug_field, axial_flow = kernel_call(last_kernel, [(radial,) + plane] * 2, 4, 0.3)(*parts, below, above)
     return drug_field, axial_flow, free, bound
 

time: 66.1 us -> 59.9 us (0.906)
  waiting for transfers between devices: 23.2 us -> 16.6 us
  Pallas kernels: 15.1 us -> 17.6 us
  starting transfers between devices: 26.7 us -> 24.6 us
    ppermute x14, waiting for transfers between devices: 17.9 us -> 12.7 us  [shifted(): lax.ppermute(block, axis, [((i - distance) % count, i) for i in range(cou...]
    pallas_call x15 -> x16, Pallas kernels: 11.8 us -> 14.3 us  [the longest x4 6.31 us: per_device(): kernel_call(functools.partial(wall_kernel, last), [shapes, shapes] + ([]...]
    ppermute x8 -> x4, starting transfers between devices: 6.93 us -> 4.66 us  [paired(): return (lax.ppermute(inner, 'ax', near), lax.ppermute(outer, 'ax', far))]
    ppermute x8 -> x4, waiting for transfers between devices: 5.3 us -> 3.91 us  [paired(): return (lax.ppermute(inner, 'ax', near), lax.ppermute(outer, 'ax', far))]
  transfers between devices with their start and end apart: 22 -> 18, of which waited for: 13 -> 10; matrix products, arithmetic and copies ran while one was open for 0% -> 0% of each run, Pallas kernels for 15% -> 17%
where the time goes in v3:
time: 59.9 us; the launch traced here: 59.7 us
  starting transfers between devices  24.6 us (41%)
  Pallas kernels  17.6 us (29%)
  waiting for transfers between devices  16.6 us (28%)
  between operations  0.86 us (1%)
    ppermute x14, starting transfers between devices, shifted(): lax.ppermute(block, axis, [((i - distance) % count, i) for i in range(cou...  19.9 us
    ppermute x14, waiting for transfers between devices, shifted(): lax.ppermute(block, axis, [((i - distance) % count, i) for i in range(cou...  12.7 us
    pallas_call x4, Pallas kernels, per_device(): kernel_call(functools.partial(wall_kernel, last), [shapes, shapes] + ([]...  6.31 us
    ppermute x4, starting transfers between devices, paired(): return (lax.ppermute(inner, 'ax', near), lax.ppermute(outer, 'ax', far))  4.66 us
    ppermute x4, waiting for transfers between devices, paired(): return (lax.ppermute(inner, 'ax', near), lax.ppermute(outer, 'ax', far))  3.91 us
    pallas_call x4, Pallas kernels, per_device(): kernel_call(functools.partial(flux_kernel, sectors, step, radial), outs,...  3.5 us
    pallas_call x3, Pallas kernels, per_device(): kernel_call(functools.partial(bulk_kernel, False, not odd, radial, across...  2.31 us
    pallas_call x1, Pallas kernels, first_call(): pl.pallas_call(functools.partial(first_kernel, sectors), name='first', ou...  1.93 us
  transfers between devices with their start and end apart: 18, of which 10 were waited for; matrix products, arithmetic and copies ran while one was open for 0% of the time, Pallas kernels for 17%

profile of v3, /device:TPU:0, one launch (start us, length us, event | category | flops | bytes accessed | tf_op | source)
XLA Modules:
  0.0 59.7 jit_solution(4122380483643032027)
XLA Ops:
  0.7 1.9 %first.1 = (s32[8,128]{1,0:T(8,128)}, f32[32,128]{1,0:T(8,128)}, f32[40,128]{1,0:T(8,128)}, f32[32,128]{1,0:T(8,128)}, f32[40,128]{1,0:T(8,128)}) custom-call(f32[26,16,8,128]{3,2,1,0:T(8,128)} %pops_ref.1, s32[8,128]{1,0:T(8,128)} %bitcast.31, s32[8,128]{1,0:T(8,128)} %bitcast.32, s32[8,128]{1,0:T(8,128)} %bitcast.8, f32[128,1024]{1,0:T(8,128)} %free_ref.3), custom_call_target="tpu_custom_call" | custom-call | tf_op jit(solution)/shard_map/first/pallas_call | solution.py:727
  2.7 5.1 %collective-permute-start = (f32[40,128]{1,0:T(8,128)}, f32[40,128]{1,0:T(8,128)S(1)}, u32[]{:S(2)}, u32[]{:S(2)}) collective-permute-start(f32[40,128]{1,0:T(8,128)} %get-tuple-element.80), channel_id=1, source_target_pairs={{1,0},{2,1},{3,2},{0,3},{5,4},{6,5},{7,6},{4,7},{9,8},{10,9},{11,1... | collective-permute-start | bytes 61448 | tf_op jit(solution)/shard_map/ppermute | solution.py:47
  7.8 1.0 %collective-permute-start.1 = (f32[32,128]{1,0:T(8,128)}, f32[32,128]{1,0:T(8,128)S(1)}, u32[]{:S(2)}, u32[]{:S(2)}) collective-permute-start(f32[32,128]{1,0:T(8,128)} %get-tuple-element.81), channel_id=1, source_target_pairs={{2,0},{3,1},{0,2},{1,3},{6,4},{7,5},{4,6},{5,7},{10,8},{11,9},{8,1... | collective-permute-start | bytes 49160 | tf_op jit(solution)/shard_map/ppermute | solution.py:47
  9.5 0.7 %shard_map.121 = (f32[128,1024]{1,0:T(8,128)S(1)}, f32[32,128]{1,0:T(8,128)S(1)}) custom-call(f32[128,1024]{1,0:T(8,128)S(1)} %copy-done.1, f32[128,1024]{1,0:T(8,128)S(1)} %copy-done.2, f32[128,128]{1,0:T(8,128)S(1)} %copy-done.3, f32[1,128]{1,0:T(1,128)S(1)} %bitcast.13, f32[1,128]{1,0:T(1,128)S(1)} %bitcast.22), custom_call_target="tpu_custom_call" | custom-call | bytes 3000000 | tf_op jit(solution)/shard_map/pallas_call | solution.py:769
  10.2 2.5 %collective-permute-done.1.refs_10_ = f32[32,128]{1,0:T(8,128)S(1)} collective-permute-done((f32[32,128]{1,0:T(8,128)}, f32[32,128]{1,0:T(8,128)S(1)}, u32[]{:S(2)}, u32[]{:S(2)}) %collective-permute-start.1) | collective-permute-done | bytes 16416 | tf_op jit(solution)/shard_map/ppermute | solution.py:47
  12.7 0.9 %collective-permute-done.2.refs_11_ = f32[40,128]{1,0:T(8,128)S(1)} collective-permute-done((f32[40,128]{1,0:T(8,128)}, f32[40,128]{1,0:T(8,128)S(1)}, u32[]{:S(2)}, u32[]{:S(2)}) %collective-permute-start.2) | collective-permute-done | bytes 20512 | tf_op jit(solution)/shard_map/ppermute | solution.py:47
  13.6 1.0 %shard_map.122 = (f32[3328,128]{1,0:T(8,128)S(1)}, f32[56,128]{1,0:T(8,128)S(1)}, f32[56,128]{1,0:T(8,128)S(1)}, f32[8,128]{1,0:T(8,128)S(1)}, f32[8,128]{1,0:T(...) custom-call(f32[3328,128]{1,0:T(8,128)S(1)} %bitcast.7, ...), custom_call_target="tpu_custom_call", output_to_operand_aliasing={{0}: (1, {})} | custom-call | bytes 2400000 | tf_op jit(solution)/shard_map/pallas_call | solution.py:787
  14.7 2.6 %collective-permute-start.4 = (f32[56,128]{1,0:T(8,128)S(1)}, f32[56,128]{1,0:T(8,128)S(1)}, u32[]{:S(2)}, u32[]{:S(2)}) collective-permute-start(f32[56,128]{1,0:T(8,128)S(1)} %get-tuple-element.85.refs_7_.refs_15_), channel_id=1, source_target_pairs={{0,28},{4,8},{8,4},{12,16},{16,12},{20,24},{24,20},{28,0},{1,29},{... | collective-permute-start | bytes 86024 | tf_op jit(solution)/shard_map/ppermute | solution.py:54
  17.2 1.7 %collective-permute-done.4.refs_2_.refs_17_ = f32[56,128]{1,0:T(8,128)S(1)} collective-permute-done((f32[56,128]{1,0:T(8,128)S(1)}, f32[56,128]{1,0:T(8,128)S(1)}, u32[]{:S(2)}, u32[]{:S(2)}) %collective-permute-start.4) | collective-permute-done | bytes 28704 | tf_op jit(solution)/shard_map/ppermute | solution.py:54
  19.3 3.0 %collective-permute-start.5 = (f32[152,128]{1,0:T(8,128)S(1)}, f32[152,128]{1,0:T(8,128)S(1)}, u32[]{:S(2)}, u32[]{:S(2)}) collective-permute-start(f32[152,128]{1,0:T(8,128)S(1)} %get-tuple-element.95), channel_id=1, source_target_pairs={{1,0},{2,1},{3,2},{0,3},{5,4},{6,5},{7,6},{4,7},{9,8},{10,9},{11,1... | collective-permute-start | bytes 233480 | tf_op jit(solution)/shard_map/ppermute | solution.py:47
  22.8 1.5 %shard_map.124 = (f32[128,1024]{1,0:T(8,128)S(1)}, f32[128,1024]{1,0:T(8,128)S(1)}, f32[32,128]{1,0:T(8,128)S(1)}) custom-call(f32[128,1024]{1,0:T(8,128)S(1)} %get-tuple-element.89.moved_ref, f32[128,1024]{1,0:T(8,128)S(1)} %copy-done.2, f32[8,128]{1,0:T(8,128)S(1)} %get-tuple-element.90.added_ref, f32[128,128]{1,0:T(8,128)S(1)} %copy-done.3, ...), custom_call_target="tpu_custom_call" | custom-call | bytes 4500000 | tf_op jit(solution)/shard_map/pallas_call | solution.py:800
  24.3 0.8 %shard_map.123 = (f32[3328,128]{1,0:T(8,128)S(1)}, f32[3328,128]{1,0:T(8,128)S(1)}, f32[24,128]{1,0:T(8,128)S(1)}) custom-call(f32[3328,128]{1,0:T(8,128)S(1)} %get-tuple-element.83.refs_0_, f32[56,128]{1,0:T(8,128)S(1)} %collective-permute-done.3.refs_1_.refs_16_, f32[56,128]{1,0:T(8,128)S(1)} %collective-permute-done.4.refs_2_.refs_17_), custom_call_target="tpu_custom_call" | custom-call | bytes 6000000 | tf_op jit(solution)/shard_map/pallas_call | solution.py:814
  25.1 2.4 %collective-permute-done.6.refs_10_ = f32[48,128]{1,0:T(8,128)S(1)} collective-permute-done((f32[48,128]{1,0:T(8,128)S(1)}, f32[48,128]{1,0:T(8,128)S(1)}, u32[]{:S(2)}, u32[]{:S(2)}) %collective-permute-start.6) | collective-permute-done | bytes 24608 | tf_op jit(solution)/shard_map/ppermute | solution.py:47
  27.5 0.9 %collective-permute-done.7.refs_11_ = f32[152,128]{1,0:T(8,128)S(1)} collective-permute-done((f32[152,128]{1,0:T(8,128)S(1)}, f32[152,128]{1,0:T(8,128)S(1)}, u32[]{:S(2)}, u32[]{:S(2)}) %collective-permute-start.7) | collective-permute-done | bytes 77856 | tf_op jit(solution)/shard_map/ppermute | solution.py:47
  29.1 2.4 %collective-permute-start.8 = (f32[112,128]{1,0:T(8,128)S(1)}, f32[112,128]{1,0:T(8,128)S(1)}, u32[]{:S(2)}, u32[]{:S(2)}) collective-permute-start(f32[112,128]{1,0:T(8,128)S(1)} %get-tuple-element.112), channel_id=1, source_target_pairs={{1,0},{2,1},{3,2},{0,3},{5,4},{6,5},{7,6},{4,7},{9,8},{10,9},{11,1... | collective-permute-start | bytes 172040 | tf_op jit(solution)/shard_map/ppermute | solution.py:47
  32.2 0.8 %shard_map.127 = (f32[3328,128]{1,0:T(8,128)S(1)}, f32[3328,128]{1,0:T(8,128)S(1)}, f32[24,128]{1,0:T(8,128)S(1)}) custom-call(f32[3328,128]{1,0:T(8,128)S(1)} %get-tuple-element.100.refs_0_, f32[8,128]{1,0:T(8,128)S(1)} %get-tuple-element.101.refs_1_, f32[8,128]{1,0:T(8,128)S(1)} %get-tuple-element.102.refs_2_), custom_call_target="tpu_custom_call" | custom-call | bytes 6000000 | tf_op jit(solution)/shard_map/pallas_call | solution.py:814
  33.0 1.5 %shard_map.128 = (f32[128,1024]{1,0:T(8,128)S(1)}, f32[128,1024]{1,0:T(8,128)S(1)}, f32[32,128]{1,0:T(8,128)S(1)}) custom-call(f32[128,1024]{1,0:T(8,128)S(1)} %get-tuple-element.106.moved_ref, f32[128,1024]{1,0:T(8,128)S(1)} %get-tuple-element.107.bound_ref, f32[8,128]{1,0:T(8,128)S(1)} %get-tuple-element.108.added_ref, f32[128,128]{1,0:T(8,128)S(1)} %copy-done.3, ...), custom_call_target="tpu_custom_call" | custom-call | bytes 4500000 | tf_op jit(solution)/shard_map/pallas_call | solution.py:800
  34.5 1.6 %collective-permute-done.9.refs_10_ = f32[16,128]{1,0:T(8,128)S(1)} collective-permute-done((f32[16,128]{1,0:T(8,128)S(1)}, f32[16,128]{1,0:T(8,128)S(1)}, u32[]{:S(2)}, u32[]{:S(2)}) %collective-permute-start.9) | collective-permute-done | bytes 8224 | tf_op jit(solution)/shard_map/ppermute | solution.py:47
  36.1 1.4 %collective-permute-done.10.refs_11_ = f32[112,128]{1,0:T(8,128)S(1)} collective-permute-done((f32[112,128]{1,0:T(8,128)S(1)}, f32[112,128]{1,0:T(8,128)S(1)}, u32[]{:S(2)}, u32[]{:S(2)}) %collective-permute-start.10) | collective-permute-done | bytes 57376 | tf_op jit(solution)/shard_map/ppermute | solution.py:47
  37.5 1.1 %shard_map.130 = (f32[3328,128]{1,0:T(8,128)S(1)}, f32[40,128]{1,0:T(8,128)S(1)}, f32[40,128]{1,0:T(8,128)S(1)}, f32[8,128]{1,0:T(8,128)S(1)}, f32[8,128]{1,0:T(8,128)S(1)}) custom-call(f32[3328,128]{1,0:T(8,128)S(1)} %get-tuple-element.103.refs_0_, f32[3328,128]{1,0:T(8,128)S(1)} %get-tuple-element.104.refs_1_, ...), custom_call_target="tpu_custom_call", output_to_operand_aliasing={{0}: (1, {})} | custom-call | bytes 2400000 | tf_op jit(solution)/shard_map/pallas_call | solution.py:787
  38.7 2.0 %collective-permute-start.12 = (f32[40,128]{1,0:T(8,128)S(1)}, f32[40,128]{1,0:T(8,128)S(1)}, u32[]{:S(2)}, u32[]{:S(2)}) collective-permute-start(f32[40,128]{1,0:T(8,128)S(1)} %get-tuple-element.117.refs_7_.refs_15_), channel_id=1, source_target_pairs={{0,28},{4,8},{8,4},{12,16},{16,12},{20,24},{24,20},{28,0},{1,29},{... | collective-permute-start | bytes 61448 | tf_op jit(solution)/shard_map/ppermute | solution.py:54
  40.7 2.2 %collective-permute-done.12.refs_2_.refs_17_ = f32[40,128]{1,0:T(8,128)S(1)} collective-permute-done((f32[40,128]{1,0:T(8,128)S(1)}, f32[40,128]{1,0:T(8,128)S(1)}, u32[]{:S(2)}, u32[]{:S(2)}) %collective-permute-start.12) | collective-permute-done | bytes 20512 | tf_op jit(solution)/shard_map/ppermute | solution.py:54
  43.2 2.5 %collective-permute-start.13 = (f32[136,128]{1,0:T(8,128)S(1)}, f32[136,128]{1,0:T(8,128)S(1)}, u32[]{:S(2)}, u32[]{:S(2)}) collective-permute-start(f32[136,128]{1,0:T(8,128)S(1)} %get-tuple-element.127), channel_id=1, source_target_pairs={{1,0},{2,1},{3,2},{0,3},{5,4},{6,5},{7,6},{4,7},{9,8},{10,9},{11,1... | collective-permute-start | bytes 208904 | tf_op jit(solution)/shard_map/ppermute | solution.py:47
  45.7 0.8 %collective-permute-start.14 = (f32[32,128]{1,0:T(8,128)S(1)}, f32[32,128]{1,0:T(8,128)S(1)}, u32[]{:S(2)}, u32[]{:S(2)}) collective-permute-start(f32[32,128]{1,0:T(8,128)S(1)} %get-tuple-element.128), channel_id=1, source_target_pairs={{2,0},{3,1},{0,2},{1,3},{6,4},{7,5},{4,6},{5,7},{10,8},{11,9},{8,1... | collective-permute-start | bytes 49160 | tf_op jit(solution)/shard_map/ppermute | solution.py:47
  46.5 1.5 %shard_map.132 = (f32[128,1024]{1,0:T(8,128)S(1)}, f32[128,1024]{1,0:T(8,128)S(1)}, f32[32,128]{1,0:T(8,128)S(1)}) custom-call(f32[128,1024]{1,0:T(8,128)S(1)} %get-tuple-element.121.moved_ref, f32[128,1024]{1,0:T(8,128)S(1)} %get-tuple-element.122.bound_ref, f32[8,128]{1,0:T(8,128)S(1)} %get-tuple-element.123.added_ref, f32[128,128]{1,0:T(8,128)S(1)} %copy-done.3, ...), custom_call_target="tpu_custom_call" | custom-call | bytes 4500000 | tf_op jit(solution)/shard_map/pallas_call | solution.py:800
  48.0 0.8 %shard_map.131 = (f32[3328,128]{1,0:T(8,128)S(1)}, f32[3328,128]{1,0:T(8,128)S(1)}, f32[24,128]{1,0:T(8,128)S(1)}) custom-call(f32[3328,128]{1,0:T(8,128)S(1)} %get-tuple-element.115.refs_0_, f32[40,128]{1,0:T(8,128)S(1)} %collective-permute-done.11.refs_1_.refs_16_, f32[40,128]{1,0:T(8,128)S(1)} %collective-permute-done.12.refs_2_.refs_17_), custom_call_target="tpu_custom_call" | custom-call | bytes 6000000 | tf_op jit(solution)/shard_map/pallas_call | solution.py:814
  48.8 1.9 %collective-permute-done.14.refs_10_ = f32[32,128]{1,0:T(8,128)S(1)} collective-permute-done((f32[32,128]{1,0:T(8,128)S(1)}, f32[32,128]{1,0:T(8,128)S(1)}, u32[]{:S(2)}, u32[]{:S(2)}) %collective-permute-start.14) | collective-permute-done | bytes 16416 | tf_op jit(solution)/shard_map/ppermute | solution.py:47
  50.7 1.1 %collective-permute-done.15.refs_11_ = f32[136,128]{1,0:T(8,128)S(1)} collective-permute-done((f32[136,128]{1,0:T(8,128)S(1)}, f32[136,128]{1,0:T(8,128)S(1)}, u32[]{:S(2)}, u32[]{:S(2)}) %collective-permute-start.15) | collective-permute-done | bytes 69664 | tf_op jit(solution)/shard_map/ppermute | solution.py:47
  51.8 0.9 %shard_map.134 = (f32[3328,128]{1,0:T(8,128)S(1)}, f32[8,128]{1,0:T(8,128)S(1)}, f32[8,128]{1,0:T(8,128)S(1)}, f32[8,128]{1,0:T(8,128)S(1)}, f32[8,128]{1,0:T(8,128)}) custom-call(f32[3328,128]{1,0:T(8,128)S(1)} %get-tuple-element.118.refs_0_, f32[3328,128]{1,0:T(8,128)S(1)} %get-tuple-element.119.refs_1_, ...), custom_call_target="tpu_custom_call", output_to_operand_aliasing={{0}: (1, {})} | custom-call | bytes 2400000 | tf_op jit(solution)/shard_map/pallas_call | solution.py:787
  52.9 0.8 %collective-permute-start.16 = (f32[32,128]{1,0:T(8,128)S(1)}, f32[32,128]{1,0:T(8,128)S(1)}, u32[]{:S(2)}, u32[]{:S(2)}) collective-permute-start(f32[32,128]{1,0:T(8,128)S(1)} %get-tuple-element.137), channel_id=1, source_target_pairs={{3,0},{0,1},{1,2},{2,3},{7,4},{4,5},{5,6},{6,7},{11,8},{8,9},{9,10... | collective-permute-start | bytes 49160 | tf_op jit(solution)/shard_map/ppermute | solution.py:47
  53.7 3.1 %collective-permute-start.17 = (f32[32,128]{1,0:T(8,128)S(1)}, f32[32,128]{1,0:T(8,128)S(1)}, u32[]{:S(2)}, u32[]{:S(2)}) collective-permute-start(f32[32,128]{1,0:T(8,128)S(1)} %get-tuple-element.138), channel_id=1, source_target_pairs={{1,0},{2,1},{3,2},{0,3},{5,4},{6,5},{7,6},{4,7},{9,8},{10,9},{11,1... | collective-permute-start | bytes 49160 | tf_op jit(solution)/shard_map/ppermute | solution.py:47
  57.3 1.8 %shard_map.138 = (f32[128,1024]{1,0:T(8,128)}, f32[128,1024]{1,0:T(8,128)}) custom-call(f32[128,1024]{1,0:T(8,128)S(1)} %get-tuple-element.141.moved_ref, f32[128,1024]{1,0:T(8,128)S(1)} %get-tuple-element.142.bound_ref, f32[8,128]{1,0:T(8,128)S(1)} %get-tuple-element.143.added_ref, f32[128,128]{1,0:T(8,128)S(1)} %copy-done.3, f32[1,128]{1,0:T(1,128)S(1)} %bitcast.21, ...), custom_call_target="tpu_custom_call" | custom-call | bytes 4500000 | tf_op jit(solution)/shard_map/pallas_call | solution.py:800
  (42 shorter events, 4.8 us)
Async XLA Ops:
  0.6 8.2 %copy-start = (f32[26,16,8,128]{3,2,1,0:T(8,128)S(1)}, f32[26,16,8,128]{3,2,1,0:T(8,128)}, u32[]{:S(2)}) copy-start(f32[26,16,8,128]{3,2,1,0:T(8,128)} %pops_ref.1) | copy-start | bytes 5111812
  0.6 8.8 %copy-start.1 = (f32[128,1024]{1,0:T(8,128)S(1)}, f32[128,1024]{1,0:T(8,128)}, u32[]{:S(2)}) copy-start(f32[128,1024]{1,0:T(8,128)} %free_ref.3) | copy-start | bytes 1572868
  0.7 8.8 %copy-start.2 = (f32[128,1024]{1,0:T(8,128)S(1)}, f32[128,1024]{1,0:T(8,128)}, u32[]{:S(2)}) copy-start(f32[128,1024]{1,0:T(8,128)} %bound_ref.3) | copy-start | bytes 1572868
  0.7 8.8 %copy-start.3 = (f32[128,128]{1,0:T(8,128)S(1)}, f32[128,128]{1,0:T(8,128)}, u32[]{:S(2)}) copy-start(f32[128,128]{1,0:T(8,128)} %spread_ref.9) | copy-start | bytes 196612
  0.7 8.8 %copy-start.6 = (f32[128]{0:T(128)S(1)}, f32[128]{0:T(128)}, u32[]{:S(2)}) copy-start(f32[128]{0:T(128)} %param.13) | copy-start | bytes 1540
  0.7 8.8 %copy-start.7 = (f32[128]{0:T(128)S(1)}, f32[128]{0:T(128)}, u32[]{:S(2)}) copy-start(f32[128]{0:T(128)} %param.14) | copy-start | bytes 1540
  2.6 11.0 %copy-start.4 = (s32[8,128]{1,0:T(8,128)S(1)}, s32[8,128]{1,0:T(8,128)}, u32[]{:S(2)}) copy-start(s32[8,128]{1,0:T(8,128)} %get-tuple-element.77.refs_3_) | copy-start | bytes 12292
  2.6 10.9 %copy-start.5 = (s32[1024]{0:T(1024)S(1)}, s32[1024]{0:T(1024)}, u32[]{:S(2)}) copy-start(s32[1024]{0:T(1024)} %param.17) | copy-start | bytes 12292
  2.7 10.9 %copy-start.8 = (f32[32,128]{1,0:T(8,128)S(1)}, f32[32,128]{1,0:T(8,128)}, u32[]{:S(2)}) copy-start(f32[32,128]{1,0:T(8,128)} %get-tuple-element.79.refs_8_) | copy-start | bytes 49156
  2.7 10.0 %collective-permute-start = (f32[40,128]{1,0:T(8,128)}, f32[40,128]{1,0:T(8,128)S(1)}, u32[]{:S(2)}, u32[]{:S(2)}) collective-permute-start(f32[40,128]{1,0:T(8,128)} %get-tuple-element.80), channel_id=1, source_target_pairs={{1,0},{2,1},{3,2},{0,3},{5,4},{6,5},{7,6},{4,7},{9,8},{10,9},{11,1... | collective-permute-start | bytes 61448 | tf_op jit(solution)/shard_map/ppermute | solution.py:47
  7.8 5.8 %collective-permute-start.2 = (f32[40,128]{1,0:T(8,128)}, f32[40,128]{1,0:T(8,128)S(1)}, u32[]{:S(2)}, u32[]{:S(2)}) collective-permute-start(f32[40,128]{1,0:T(8,128)} %get-tuple-element.82), channel_id=1, source_target_pairs={{3,0},{0,1},{1,2},{2,3},{7,4},{4,5},{5,6},{6,7},{11,8},{8,9},{9,10... | collective-permute-start | bytes 61448 | tf_op jit(solution)/shard_map/ppermute | solution.py:47
  7.8 4.8 %collective-permute-start.1 = (f32[32,128]{1,0:T(8,128)}, f32[32,128]{1,0:T(8,128)S(1)}, u32[]{:S(2)}, u32[]{:S(2)}) collective-permute-start(f32[32,128]{1,0:T(8,128)} %get-tuple-element.81), channel_id=1, source_target_pairs={{2,0},{3,1},{0,2},{1,3},{6,4},{7,5},{4,6},{5,7},{10,8},{11,9},{8,1... | collective-permute-start | bytes 49160 | tf_op jit(solution)/shard_map/ppermute | solution.py:47
  14.6 2.6 %collective-permute-start.3 = (f32[56,128]{1,0:T(8,128)S(1)}, f32[56,128]{1,0:T(8,128)S(1)}, u32[]{:S(2)}, u32[]{:S(2)}) collective-permute-start(f32[56,128]{1,0:T(8,128)S(1)} %get-tuple-element.84.refs_6_.refs_14_), channel_id=1, source_target_pairs={{0,4},{4,0},{8,12},{12,8},{16,20},{20,16},{24,28},{28,24},{1,5},{5... | collective-permute-start | bytes 86024 | tf_op jit(solution)/shard_map/ppermute | solution.py:54
  14.7 4.3 %collective-permute-start.4 = (f32[56,128]{1,0:T(8,128)S(1)}, f32[56,128]{1,0:T(8,128)S(1)}, u32[]{:S(2)}, u32[]{:S(2)}) collective-permute-start(f32[56,128]{1,0:T(8,128)S(1)} %get-tuple-element.85.refs_7_.refs_15_), channel_id=1, source_target_pairs={{0,28},{4,8},{8,4},{12,16},{16,12},{20,24},{24,20},{28,0},{1,29},{... | collective-permute-start | bytes 86024 | tf_op jit(solution)/shard_map/ppermute | solution.py:54
  19.3 8.3 %collective-permute-start.5 = (f32[152,128]{1,0:T(8,128)S(1)}, f32[152,128]{1,0:T(8,128)S(1)}, u32[]{:S(2)}, u32[]{:S(2)}) collective-permute-start(f32[152,128]{1,0:T(8,128)S(1)} %get-tuple-element.95), channel_id=1, source_target_pairs={{1,0},{2,1},{3,2},{0,3},{5,4},{6,5},{7,6},{4,7},{9,8},{10,9},{11,1... | collective-permute-start | bytes 233480 | tf_op jit(solution)/shard_map/ppermute | solution.py:47
  22.2 6.2 %collective-permute-start.7 = (f32[152,128]{1,0:T(8,128)S(1)}, f32[152,128]{1,0:T(8,128)S(1)}, u32[]{:S(2)}, u32[]{:S(2)}) collective-permute-start(f32[152,128]{1,0:T(8,128)S(1)} %get-tuple-element.97), channel_id=1, source_target_pairs={{3,0},{0,1},{1,2},{2,3},{7,4},{4,5},{5,6},{6,7},{11,8},{8,9},{9,10... | collective-permute-start | bytes 233480 | tf_op jit(solution)/shard_map/ppermute | solution.py:47
  22.2 5.3 %collective-permute-start.6 = (f32[48,128]{1,0:T(8,128)S(1)}, f32[48,128]{1,0:T(8,128)S(1)}, u32[]{:S(2)}, u32[]{:S(2)}) collective-permute-start(f32[48,128]{1,0:T(8,128)S(1)} %get-tuple-element.96), channel_id=1, source_target_pairs={{2,0},{3,1},{0,2},{1,3},{6,4},{7,5},{4,6},{5,7},{10,8},{11,9},{8,1... | collective-permute-start | bytes 73736 | tf_op jit(solution)/shard_map/ppermute | solution.py:47
  29.1 7.0 %collective-permute-start.8 = (f32[112,128]{1,0:T(8,128)S(1)}, f32[112,128]{1,0:T(8,128)S(1)}, u32[]{:S(2)}, u32[]{:S(2)}) collective-permute-start(f32[112,128]{1,0:T(8,128)S(1)} %get-tuple-element.112), channel_id=1, source_target_pairs={{1,0},{2,1},{3,2},{0,3},{5,4},{6,5},{7,6},{4,7},{9,8},{10,9},{11,1... | collective-permute-start | bytes 172040 | tf_op jit(solution)/shard_map/ppermute | solution.py:47
  31.6 6.0 %collective-permute-start.10 = (f32[112,128]{1,0:T(8,128)S(1)}, f32[112,128]{1,0:T(8,128)S(1)}, u32[]{:S(2)}, u32[]{:S(2)}) collective-permute-start(f32[112,128]{1,0:T(8,128)S(1)} %get-tuple-element.114), channel_id=1, source_target_pairs={{3,0},{0,1},{1,2},{2,3},{7,4},{4,5},{5,6},{6,7},{11,8},{8,9},{9,10... | collective-permute-start | bytes 172040 | tf_op jit(solution)/shard_map/ppermute | solution.py:47
  31.6 4.5 %collective-permute-start.9 = (f32[16,128]{1,0:T(8,128)S(1)}, f32[16,128]{1,0:T(8,128)S(1)}, u32[]{:S(2)}, u32[]{:S(2)}) collective-permute-start(f32[16,128]{1,0:T(8,128)S(1)} %get-tuple-element.113), channel_id=1, source_target_pairs={{2,0},{3,1},{0,2},{1,3},{6,4},{7,5},{4,6},{5,7},{10,8},{11,9},{8,1... | collective-permute-start | bytes 24584 | tf_op jit(solution)/shard_map/ppermute | solution.py:47
  38.7 2.0 %collective-permute-start.11 = (f32[40,128]{1,0:T(8,128)S(1)}, f32[40,128]{1,0:T(8,128)S(1)}, u32[]{:S(2)}, u32[]{:S(2)}) collective-permute-start(f32[40,128]{1,0:T(8,128)S(1)} %get-tuple-element.116.refs_6_.refs_14_), channel_id=1, source_target_pairs={{0,4},{4,0},{8,12},{12,8},{16,20},{20,16},{24,28},{28,24},{1,5},{5... | collective-permute-start | bytes 61448 | tf_op jit(solution)/shard_map/ppermute | solution.py:54
  38.7 4.2 %collective-permute-start.12 = (f32[40,128]{1,0:T(8,128)S(1)}, f32[40,128]{1,0:T(8,128)S(1)}, u32[]{:S(2)}, u32[]{:S(2)}) collective-permute-start(f32[40,128]{1,0:T(8,128)S(1)} %get-tuple-element.117.refs_7_.refs_15_), channel_id=1, source_target_pairs={{0,28},{4,8},{8,4},{12,16},{16,12},{20,24},{24,20},{28,0},{1,29},{... | collective-permute-start | bytes 61448 | tf_op jit(solution)/shard_map/ppermute | solution.py:54
  43.2 7.5 %collective-permute-start.13 = (f32[136,128]{1,0:T(8,128)S(1)}, f32[136,128]{1,0:T(8,128)S(1)}, u32[]{:S(2)}, u32[]{:S(2)}) collective-permute-start(f32[136,128]{1,0:T(8,128)S(1)} %get-tuple-element.127), channel_id=1, source_target_pairs={{1,0},{2,1},{3,2},{0,3},{5,4},{6,5},{7,6},{4,7},{9,8},{10,9},{11,1... | collective-permute-start | bytes 208904 | tf_op jit(solution)/shard_map/ppermute | solution.py:47
  45.7 6.1 %collective-permute-start.15 = (f32[136,128]{1,0:T(8,128)S(1)}, f32[136,128]{1,0:T(8,128)S(1)}, u32[]{:S(2)}, u32[]{:S(2)}) collective-permute-start(f32[136,128]{1,0:T(8,128)S(1)} %get-tuple-element.129), channel_id=1, source_target_pairs={{3,0},{0,1},{1,2},{2,3},{7,4},{4,5},{5,6},{6,7},{11,8},{8,9},{9,10... | collective-permute-start | bytes 208904 | tf_op jit(solution)/shard_map/ppermute | solution.py:47
  45.7 5.0 %collective-permute-start.14 = (f32[32,128]{1,0:T(8,128)S(1)}, f32[32,128]{1,0:T(8,128)S(1)}, u32[]{:S(2)}, u32[]{:S(2)}) collective-permute-start(f32[32,128]{1,0:T(8,128)S(1)} %get-tuple-element.128), channel_id=1, source_target_pairs={{2,0},{3,1},{0,2},{1,3},{6,4},{7,5},{4,6},{5,7},{10,8},{11,9},{8,1... | collective-permute-start | bytes 49160 | tf_op jit(solution)/shard_map/ppermute | solution.py:47
  52.9 6.1 %collective-permute-start.16 = (f32[32,128]{1,0:T(8,128)S(1)}, f32[32,128]{1,0:T(8,128)S(1)}, u32[]{:S(2)}, u32[]{:S(2)}) collective-permute-start(f32[32,128]{1,0:T(8,128)S(1)} %get-tuple-element.137), channel_id=1, source_target_pairs={{3,0},{0,1},{1,2},{2,3},{7,4},{4,5},{5,6},{6,7},{11,8},{8,9},{9,10... | collective-permute-start | bytes 49160 | tf_op jit(solution)/shard_map/ppermute | solution.py:47
  53.7 5.3 %collective-permute-start.17 = (f32[32,128]{1,0:T(8,128)S(1)}, f32[32,128]{1,0:T(8,128)S(1)}, u32[]{:S(2)}, u32[]{:S(2)}) collective-permute-start(f32[32,128]{1,0:T(8,128)S(1)} %get-tuple-element.138), channel_id=1, source_target_pairs={{1,0},{2,1},{3,2},{0,3},{5,4},{6,5},{7,6},{4,7},{9,8},{10,9},{11,1... | collective-permute-start | bytes 49160 | tf_op jit(solution)/shard_map/ppermute | solution.py:47

commit v4 on v3

--- a/solution.py
+++ b/solution.py
@@ -290,7 +290,9 @@
             out[4 * across:5 * across] = jnp.broadcast_to(edge, (across, width)).astype(F32)
 
 
-def bulk_kernel(first, packed, radial, across, *refs):
+def bulk_kernel(first, packed, rims_too, radial, across, *refs):
+    if rims_too:
+        refs, rim_refs = refs[:-2], refs[-2:]
     if first:
         state_ref, post_ref, speed_ref = refs
     else:
@@ -313,6 +315,14 @@
             results = results + relax_drug(members[FLOWS:], velocity)
         for member, value in enumerate(results):
             post.put(member, level, value)
+    if rims_too:
+        for ref, slots, rising in ((rim_refs[0], RISE_SLOTS, True), (rim_refs[1], FALL_SLOTS, False)):
+            for place, tile in enumerate(rim_tiles(post, slots, rising)):
+                ref[place * across:(place + 1) * across, :] = tile
+
+
+def slot_origin(column, along, rising):
+    return along - 1 - column if rising else column
 
 
 def rim_tiles(post, slots, rising):
@@ -324,12 +334,38 @@
     for place, (member, column) in enumerate(slots):
         if place % each == 0:
             tiles.append(jnp.zeros((across, along), F32))
-        origin = along - 1 - column if rising else column
         only_last = place == len(slots) - 1
-        for level in range(radial - 1 if only_last else 0, radial):
+        for level in range(radial - 1 if only_last else 0, radial - 1 if member >= FLOWS else radial):
             slot = (place % each) * radial + level
-            value = pltpu.roll(post.get(member, level), (slot - origin) % along, 1)
+            value = pltpu.roll(post.get(member, level), (slot - slot_origin(column, along, rising)) % along, 1)
             tiles[-1] = jnp.where(lane == slot, value, tiles[-1])
+    return tiles
+
+
+def finished_tiles(ref, slots, rising, radial, across, drugs, fixed_rows):
+    along = ref.shape[-1]
+    each = along // radial
+    lane, row = lanes((across, along)), sublanes((across, along))
+    tiles = []
+    for start in range(0, len(slots), each):
+        tile = ref[(start // each) * across:(start // each + 1) * across, :]
+        here = slots[start:start + each]
+        for place, (member, column) in enumerate(here):
+            if member >= FLOWS:
+                slot = place * radial + radial - 1
+                value = pltpu.roll(drugs[member - FLOWS], (slot - slot_origin(column, along, rising)) % along, 1)
+                tile = jnp.where(lane == slot, value, tile)
+        for side in sorted({side for side, _, _ in fixed_rows}):
+            spread = jnp.zeros((across, along), F32)
+            for other, level, blocks in fixed_rows:
+                if other != side:
+                    continue
+                for place, (member, column) in enumerate(here):
+                    origin = slot_origin(column, along, rising)
+                    value = jnp.broadcast_to(blocks[member][:, origin:origin + 1], (across, along))
+                    spread = jnp.where(lane - row == place * radial + level, value, spread)
+            tile = jnp.where(row == side, jnp.sum(spread, axis=0, keepdims=True), tile)
+        tiles.append(tile)
     return tiles
 
 
@@ -408,14 +444,19 @@
     if not first:
         open_ref, counts_ref = refs[:2]
         refs = refs[2:]
+    if not odd:
+        rim_refs, refs = refs[:2], refs[2:]
     if odd:
         sent_refs, got_refs = refs[:2], refs[2:4]
         refs = refs[4:]
         if step > 1:
             ghost_code_ref, ghost_open_ref = refs[:2]
             refs = refs[2:]
-    post_ref, one_ref, two_ref, added_ref, top_ref = refs[:5]
-    refs = refs[5:]
+    last = step == STEPS - 1
+    post_ref, one_ref, two_ref, added_ref = refs[:4]
+    refs = refs[4:]
+    if not last:
+        top_ref, refs = refs[0], refs[1:]
     del bulk_ref
     across, along = code_ref.shape
     plane = (across, along)
@@ -447,26 +488,29 @@
     shut = PERMEABILITY * (1.0 - strut)
     added = shut * (total - counts * inbox[0][base:base + across, :]) + RELEASE_RATE * strut
     added_ref[...] = added
-    free = coef_ref[0:across, :] + added * coef_ref[across:2 * across, :]
-    bound = coef_ref[2 * across:3 * across, :] + added * coef_ref[3 * across:4 * across, :]
-    top = free - (on_ref[0:1, 0:1] * free * (1.0 - bound) - off_ref[0:1, 0:1] * bound)
-    top_ref[...] = top
+    if not last:
+        free = coef_ref[0:across, :] + added * coef_ref[across:2 * across, :]
+        bound = coef_ref[2 * across:3 * across, :] + added * coef_ref[3 * across:4 * across, :]
+        top = free - (on_ref[0:1, 0:1] * free * (1.0 - bound) - off_ref[0:1, 0:1] * bound)
+        top_ref[...] = top
     start = rims_start(step, across)
     row = sublanes(plane)
     drugs = [state.get(member, end) for member in range(FLOWS, MEMBERS)]
     if not first:
-        last = start + SECTOR_RISING.index(FLOWS + 3) * radial + end
-        drugs[3] = jnp.where(row == 0, below[last:last + 1, :], drugs[3])
-        last = start + SECTOR_FALLING.index(FLOWS + 4) * radial + end
-        drugs[4] = jnp.where(row == across - 1, above[last:last + 1, :], drugs[4])
+        place = start + SECTOR_RISING.index(FLOWS + 3) * radial + end
+        drugs[3] = jnp.where(row == 0, below[place:place + 1, :], drugs[3])
+        place = start + SECTOR_FALLING.index(FLOWS + 4) * radial + end
+        drugs[4] = jnp.where(row == across - 1, above[place:place + 1, :], drugs[4])
     surface = drugs[0]
     for drug in drugs[1:]:
         surface = surface + drug
     flux = openness * (surface - picked)
     drugs = [drug - WEIGHTS[FLOWS + place] * flux for place, drug in enumerate(drugs)]
     velocity = [speed_ref[component * across:(component + 1) * across, :] for component in range(3)]
-    for place, value in enumerate(relax_drug(drugs, velocity)):
+    drugs = relax_drug(drugs, velocity)
+    for place, value in enumerate(drugs):
         post.put(FLOWS + place, end, value)
+    fixed_rows = []
     if not first:
         block = across
         for side, box, places in ((0, below, SECTOR_RISING), (across - 1, above, SECTOR_FALLING)):
@@ -486,9 +530,10 @@
                 results = results + relax_drug(members[FLOWS:], velocity)
                 for member, value in enumerate(results):
                     post.put_rows(member, level, block, side, value)
+                fixed_rows.append((side, level, results))
     if not odd:
-        rise = rim_tiles(post, RISE_SLOTS, True) + [top]
-        fall = rim_tiles(post, FALL_SLOTS, False) + [top]
+        rise = finished_tiles(rim_refs[0], RISE_SLOTS, True, radial, across, drugs, fixed_rows) + [top]
+        fall = finished_tiles(rim_refs[1], FALL_SLOTS, False, radial, across, drugs, fixed_rows) + [top]
         if first:
             own = code_ref[...].astype(F32)
             rise = rise + [shut, pltpu.roll(own, 1, 1)]
@@ -547,19 +592,33 @@
     return (6 if step == 1 else 4 if step % 2 else 2) * across
 
 
-def wall_rates(spread_ref, on_ref, off_ref):
+def wall_rates(spread_ref, on_ref, off_ref, width):
     depth = spread_ref.shape[0]
     shape = (depth, depth)
-    rate_on = jnp.transpose(jnp.broadcast_to(on_ref[...], shape))
-    rate_off = jnp.transpose(jnp.broadcast_to(off_ref[...], shape))
-    entry = jnp.broadcast_to(spread_ref[:, 0:1], shape)
-    top = jnp.transpose(jnp.broadcast_to(spread_ref[0:1, :], shape))
-    return rate_on, rate_off, entry, top
-
-
-def plan_ahead(spread, rates, free, bound):
+    rate_on = jnp.transpose(jnp.broadcast_to(on_ref[...], shape))[:, 0:1]
+    rate_off = jnp.transpose(jnp.broadcast_to(off_ref[...], shape))[:, 0:1]
+    top = jnp.transpose(jnp.broadcast_to(spread_ref[0:1, :], shape))[:, 0:1]
+    return [jnp.broadcast_to(column, (depth, width)) for column in (rate_on, rate_off, spread_ref[:, 0:1], top)]
+
+
+def split2(value):
+    high = value.astype(BF16)
+    return high, (value - high.astype(F32)).astype(BF16)
+
+
+def left_terms(spread):
+    high, low = split2(spread)
+    return jnp.concatenate([high, high, low], axis=1)
+
+
+def product(left, free):
+    high, low = split2(free)
+    return jnp.dot(left, jnp.concatenate([high, low, high], axis=0), preferred_element_type=F32)
+
+
+def plan_ahead(left, rates, free, bound):
     rate_on, rate_off, entry, top = rates
-    moved = jnp.dot(spread, free, precision=lax.Precision.HIGHEST, preferred_element_type=F32)
+    moved = product(left, free)
     rate = rate_on * moved * (1.0 - bound) - rate_off * bound
     gain = rate_on * entry * (1.0 - bound)
     first = jnp.sum(top * (moved - rate), axis=0, keepdims=True)
@@ -567,30 +626,41 @@
     return moved, (first, slope, bound[0:1, :] + rate[0:1, :], gain[0:1, :])
 
 
+def put_coefs(coef_ref, across, width, row, parts):
+    for index, part in enumerate(parts):
+        for step in range(part.shape[1] // width):
+            place = index * across + row + step
+            coef_ref[place:place + 1, :] = part[:, step * width:(step + 1) * width]
+
+
+TOGETHER = 2
+
+
 def plan_kernel(free_ref, bound_ref, spread_ref, on_ref, off_ref, moved_ref, coef_ref):
-    rates = wall_rates(spread_ref, on_ref, off_ref)
     width = coef_ref.shape[1]
     across = coef_ref.shape[0] // 4
-    for row in range(across):
-        place = slice(row * width, (row + 1) * width)
-        moved, parts = plan_ahead(spread_ref[...], rates, free_ref[:, place], bound_ref[:, place])
+    rates = wall_rates(spread_ref, on_ref, off_ref, TOGETHER * width)
+    left = left_terms(spread_ref[...])
+    for row in range(0, across, TOGETHER):
+        place = slice(row * width, (row + TOGETHER) * width)
+        moved, parts = plan_ahead(left, rates, free_ref[:, place], bound_ref[:, place])
         moved_ref[:, place] = moved
-        for index, part in enumerate(parts):
-            coef_ref[index * across + row:index * across + row + 1, :] = part
+        put_coefs(coef_ref, across, width, row, parts)
 
 
 def wall_kernel(last, moved_ref, bound_ref, added_ref, spread_ref, on_ref, off_ref, *outs):
-    rates = wall_rates(spread_ref, on_ref, off_ref)
+    across, width = added_ref.shape
+    rates = wall_rates(spread_ref, on_ref, off_ref, TOGETHER * width)
     rate_on, rate_off, entry, _ = rates
-    across, width = added_ref.shape
-    spread = spread_ref[...]
-    for row in range(across):
-        place = slice(row * width, (row + 1) * width)
-        free = moved_ref[:, place] + entry * added_ref[row:row + 1, :]
+    left = left_terms(spread_ref[...])
+    for row in range(0, across, TOGETHER):
+        place = slice(row * width, (row + TOGETHER) * width)
+        added = jnp.concatenate([added_ref[row + step:row + step + 1, :] for step in range(TOGETHER)], axis=1)
+        free = moved_ref[:, place] + entry * added
         bound = bound_ref[:, place]
         for substep in range(SUB):
             if substep:
-                free = jnp.dot(spread, free, precision=lax.Precision.HIGHEST, preferred_element_type=F32)
+                free = product(left, free)
             rate = rate_on * free * (1.0 - bound) - rate_off * bound
             free = free - rate
             bound = bound + rate
@@ -598,10 +668,9 @@
         if last:
             outs[0][:, place] = free
         else:
-            moved, parts = plan_ahead(spread, rates, free, bound)
+            moved, parts = plan_ahead(left, rates, free, bound)
             outs[0][:, place] = moved
-            for index, part in enumerate(parts):
-                outs[2][index * across + row:index * across + row + 1, :] = part
+            put_coefs(outs[2], across, width, row, parts)
 
 
 def send_kernel(sectors, step, radial, *refs):
@@ -765,7 +834,9 @@
     two = (2 * across, along)
     rim = rim_rows(radial, across, along)
     shapes = wall_free.shape
-    bulk, speed = kernel_call(functools.partial(bulk_kernel, True, True, radial, across), [flat, speeds], 1, 1.5)(state)
+    bulk, speed, *tiles = kernel_call(
+        functools.partial(bulk_kernel, True, True, True, radial, across), [flat, speeds, (rim, along), (rim, along)], 1, 1.5
+    )(state)
     moved, coefs = kernel_call(plan_kernel, [shapes, four], 5, 1.0)(
         wall_free, wall_bound, wall_propagator, rate_on, rate_off
     )
@@ -778,15 +849,17 @@
             pair = [plane, plane]
         else:
             pair = [(rim + (3 if step == 0 else 1) * across, along)] * 2
-        outs = [flat] + pair + [plane, plane]
+        outs = [flat] + pair + [plane] * (1 if last else 2)
         if step == 0:
             outs = outs + [plane, plane, jax.ShapeDtypeStruct(plane, jnp.int32)]
         if step == 1:
             outs = outs + [jax.ShapeDtypeStruct(two, jnp.int32), two]
-        extra = fixed + ([*sent, *got, *ghost] if odd else [])
-        post, one, other, added, top, *rest = kernel_call(
+        extra = fixed + ([*sent, *got, *ghost] if odd else tiles)
+        post, one, other, added, *rest = kernel_call(
             functools.partial(flux_kernel, sectors, step, radial), outs, 8 + sectors + len(extra), 0.8, {1: 0}
         )(state, bulk, speed, codes, strut, coefs, rate_on, rate_off, *inbox, *extra)
+        if not last:
+            top, *rest = rest
         if step == 0:
             fixed, edges = rest[:2], rest[2]
         if step == 1:
@@ -811,8 +884,9 @@
             functools.partial(send_kernel, sectors, step, radial), sizes, 6 + len(own), 0.3
         )(post, *rims_in, codes, edges, top, *own)
         inbox = exchange(boxes)
-        state, bulk, speed = kernel_call(
-            functools.partial(bulk_kernel, False, not odd, radial, across), [flat, flat, speeds], 3, 2.0
+        outs = [flat, flat, speeds] + ([(rim, along)] * 2 if odd else [])
+        state, bulk, speed, *tiles = kernel_call(
+            functools.partial(bulk_kernel, False, not odd, odd, radial, across), outs, 3, 2.0
         )(post, *rims_in)
     up, down = kernel_call(
         functools.partial(last_send_kernel, radial, across), [(2 * radial, along)] * 2, 3, 0.2

time: 59.9 us -> 58 us (0.968)
  Pallas kernels: 17.6 us -> 14.9 us
  waiting for transfers between devices: 16.6 us -> 17.6 us
    pallas_call x4, Pallas kernels: 6.31 us -> 4.32 us  [per_device(): kernel_call(functools.partial(wall_kernel, last), [shapes, shapes] + ([]...]
    pallas_call x4, Pallas kernels: 3.5 us -> 1.78 us  [per_device(): kernel_call(functools.partial(flux_kernel, sectors, step, radial), outs,...]
    pallas_call x4, Pallas kernels: 2.89 us -> 4.19 us  [the longest x3 3.01 us: per_device(): kernel_call(functools.partial(bulk_kernel, False, not odd, odd, radial, a...]
    ppermute x14, waiting for transfers between devices: 12.7 us -> 13.6 us  [shifted(): lax.ppermute(block, axis, [((i - distance) % count, i) for i in range(cou...]
  transfers between devices with their start and end apart: 18 -> 18, of which waited for: 10 -> 10; matrix products, arithmetic and copies ran while one was open for 0% -> 0% of each run, Pallas kernels for 17% -> 16%
where the time goes in v4:
time: 58 us; the launch traced here: 57.8 us
  starting transfers between devices  24.4 us (42%)
  waiting for transfers between devices  17.6 us (30%)
  Pallas kernels  14.9 us (26%)
  between operations  0.87 us (2%)
    ppermute x14, starting transfers between devices, shifted(): lax.ppermute(block, axis, [((i - distance) % count, i) for i in range(cou...  19.8 us
    ppermute x14, waiting for transfers between devices, shifted(): lax.ppermute(block, axis, [((i - distance) % count, i) for i in range(cou...  13.6 us
    ppermute x4, starting transfers between devices, paired(): return (lax.ppermute(inner, 'ax', near), lax.ppermute(outer, 'ax', far))  4.66 us
    pallas_call x4, Pallas kernels, per_device(): kernel_call(functools.partial(wall_kernel, last), [shapes, shapes] + ([]...  4.32 us
    ppermute x4, waiting for transfers between devices, paired(): return (lax.ppermute(inner, 'ax', near), lax.ppermute(outer, 'ax', far))  3.91 us
    pallas_call x3, Pallas kernels, per_device(): kernel_call(functools.partial(bulk_kernel, False, not odd, odd, radial, a...  3.01 us
    pallas_call x1, Pallas kernels, first_call(): pl.pallas_call(functools.partial(first_kernel, sectors), name='first', ou...  1.93 us
    pallas_call x4, Pallas kernels, per_device(): kernel_call(functools.partial(flux_kernel, sectors, step, radial), outs,...  1.78 us
  transfers between devices with their start and end apart: 18, of which 10 were waited for; matrix products, arithmetic and copies ran while one was open for 0% of the time, Pallas kernels for 16%

profile of v4, /device:TPU:0, one launch (start us, length us, event | category | flops | bytes accessed | tf_op | source)
XLA Modules:
  0.0 57.8 jit_solution(7057816177627192389)
XLA Ops:
  0.7 1.9 %first.1 = (s32[8,128]{1,0:T(8,128)}, f32[32,128]{1,0:T(8,128)}, f32[40,128]{1,0:T(8,128)}, f32[32,128]{1,0:T(8,128)}, f32[40,128]{1,0:T(8,128)}) custom-call(f32[26,16,8,128]{3,2,1,0:T(8,128)} %pops_ref.1, s32[8,128]{1,0:T(8,128)} %bitcast.31, s32[8,128]{1,0:T(8,128)} %bitcast.32, s32[8,128]{1,0:T(8,128)} %bitcast.8, f32[128,1024]{1,0:T(8,128)} %free_ref.3), custom_call_target="tpu_custom_call" | custom-call | tf_op jit(solution)/shard_map/first/pallas_call | solution.py:796
  2.7 5.1 %collective-permute-start = (f32[40,128]{1,0:T(8,128)}, f32[40,128]{1,0:T(8,128)S(1)}, u32[]{:S(2)}, u32[]{:S(2)}) collective-permute-start(f32[40,128]{1,0:T(8,128)} %get-tuple-element.84), channel_id=1, source_target_pairs={{1,0},{2,1},{3,2},{0,3},{5,4},{6,5},{7,6},{4,7},{9,8},{10,9},{11,1... | collective-permute-start | bytes 61448 | tf_op jit(solution)/shard_map/ppermute | solution.py:47
  7.8 1.0 %collective-permute-start.1 = (f32[32,128]{1,0:T(8,128)}, f32[32,128]{1,0:T(8,128)S(1)}, u32[]{:S(2)}, u32[]{:S(2)}) collective-permute-start(f32[32,128]{1,0:T(8,128)} %get-tuple-element.85), channel_id=1, source_target_pairs={{2,0},{3,1},{0,2},{1,3},{6,4},{7,5},{4,6},{5,7},{10,8},{11,9},{8,1... | collective-permute-start | bytes 49160 | tf_op jit(solution)/shard_map/ppermute | solution.py:47
  8.8 1.2 %shard_map.120 = (f32[3328,128]{1,0:T(8,128)S(1)}, f32[24,128]{1,0:T(8,128)S(1)}, f32[32,128]{1,0:T(8,128)S(1)}, f32[32,128]{1,0:T(8,128)S(1)}) custom-call(f32[3328,128]{1,0:T(8,128)S(1)} %bitcast.6), custom_call_target="tpu_custom_call" | custom-call | bytes 4500000 | tf_op jit(solution)/shard_map/pallas_call | solution.py:837
  10.5 2.2 %collective-permute-done.1.refs_10_ = f32[32,128]{1,0:T(8,128)S(1)} collective-permute-done((f32[32,128]{1,0:T(8,128)}, f32[32,128]{1,0:T(8,128)S(1)}, u32[]{:S(2)}, u32[]{:S(2)}) %collective-permute-start.1) | collective-permute-done | bytes 16416 | tf_op jit(solution)/shard_map/ppermute | solution.py:47
  12.7 0.9 %collective-permute-done.2.refs_11_ = f32[40,128]{1,0:T(8,128)S(1)} collective-permute-done((f32[40,128]{1,0:T(8,128)}, f32[40,128]{1,0:T(8,128)S(1)}, u32[]{:S(2)}, u32[]{:S(2)}) %collective-permute-start.2) | collective-permute-done | bytes 20512 | tf_op jit(solution)/shard_map/ppermute | solution.py:47
  14.1 2.5 %collective-permute-start.4 = (f32[56,128]{1,0:T(8,128)S(1)}, f32[56,128]{1,0:T(8,128)S(1)}, u32[]{:S(2)}, u32[]{:S(2)}) collective-permute-start(f32[56,128]{1,0:T(8,128)S(1)} %get-tuple-element.91.refs_7_.refs_15_), channel_id=1, source_target_pairs={{0,28},{4,8},{8,4},{12,16},{16,12},{20,24},{24,20},{28,0},{1,29},{... | collective-permute-start | bytes 86024 | tf_op jit(solution)/shard_map/ppermute | solution.py:54
  16.6 1.7 %collective-permute-done.4.refs_2_.refs_17_ = f32[56,128]{1,0:T(8,128)S(1)} collective-permute-done((f32[56,128]{1,0:T(8,128)S(1)}, f32[56,128]{1,0:T(8,128)S(1)}, u32[]{:S(2)}, u32[]{:S(2)}) %collective-permute-start.4) | collective-permute-done | bytes 28704 | tf_op jit(solution)/shard_map/ppermute | solution.py:54
  18.6 2.9 %collective-permute-start.5 = (f32[152,128]{1,0:T(8,128)S(1)}, f32[152,128]{1,0:T(8,128)S(1)}, u32[]{:S(2)}, u32[]{:S(2)}) collective-permute-start(f32[152,128]{1,0:T(8,128)S(1)} %get-tuple-element.101), channel_id=1, source_target_pairs={{1,0},{2,1},{3,2},{0,3},{5,4},{6,5},{7,6},{4,7},{9,8},{10,9},{11,1... | collective-permute-start | bytes 233480 | tf_op jit(solution)/shard_map/ppermute | solution.py:47
  21.6 0.6 %collective-permute-start.6 = (f32[48,128]{1,0:T(8,128)S(1)}, f32[48,128]{1,0:T(8,128)S(1)}, u32[]{:S(2)}, u32[]{:S(2)}) collective-permute-start(f32[48,128]{1,0:T(8,128)S(1)} %get-tuple-element.102), channel_id=1, source_target_pairs={{2,0},{3,1},{0,2},{1,3},{6,4},{7,5},{4,6},{5,7},{10,8},{11,9},{8,1... | collective-permute-start | bytes 73736 | tf_op jit(solution)/shard_map/ppermute | solution.py:47
  22.2 0.9 %shard_map.124 = (f32[128,1024]{1,0:T(8,128)S(1)}, f32[128,1024]{1,0:T(8,128)S(1)}, f32[32,128]{1,0:T(8,128)S(1)}) custom-call(f32[128,1024]{1,0:T(8,128)S(1)} %get-tuple-element.95.moved_ref, f32[128,1024]{1,0:T(8,128)S(1)} %copy-done.2, f32[8,128]{1,0:T(8,128)S(1)} %get-tuple-element.96.added_ref, f32[128,128]{1,0:T(8,128)S(1)} %copy-done.3, ...), custom_call_target="tpu_custom_call" | custom-call | bytes 4500000 | tf_op jit(solution)/shard_map/pallas_call | solution.py:873
  23.1 0.8 %shard_map.123 = (f32[3328,128]{1,0:T(8,128)S(1)}, f32[3328,128]{1,0:T(8,128)S(1)}, f32[24,128]{1,0:T(8,128)S(1)}) custom-call(f32[3328,128]{1,0:T(8,128)S(1)} %get-tuple-element.89.refs_0_, f32[56,128]{1,0:T(8,128)S(1)} %collective-permute-done.3.refs_1_.refs_16_, f32[56,128]{1,0:T(8,128)S(1)} %collective-permute-done.4.refs_2_.refs_17_), custom_call_target="tpu_custom_call" | custom-call | bytes 6000000 | tf_op jit(solution)/shard_map/pallas_call | solution.py:888
  23.9 3.0 %collective-permute-done.6.refs_10_ = f32[48,128]{1,0:T(8,128)S(1)} collective-permute-done((f32[48,128]{1,0:T(8,128)S(1)}, f32[48,128]{1,0:T(8,128)S(1)}, u32[]{:S(2)}, u32[]{:S(2)}) %collective-permute-start.6) | collective-permute-done | bytes 24608 | tf_op jit(solution)/shard_map/ppermute | solution.py:47
  26.9 0.9 %collective-permute-done.7.refs_11_ = f32[152,128]{1,0:T(8,128)S(1)} collective-permute-done((f32[152,128]{1,0:T(8,128)S(1)}, f32[152,128]{1,0:T(8,128)S(1)}, u32[]{:S(2)}, u32[]{:S(2)}) %collective-permute-start.7) | collective-permute-done | bytes 77856 | tf_op jit(solution)/shard_map/ppermute | solution.py:47
  28.5 2.4 %collective-permute-start.8 = (f32[112,128]{1,0:T(8,128)S(1)}, f32[112,128]{1,0:T(8,128)S(1)}, u32[]{:S(2)}, u32[]{:S(2)}) collective-permute-start(f32[112,128]{1,0:T(8,128)S(1)} %get-tuple-element.118), channel_id=1, source_target_pairs={{1,0},{2,1},{3,2},{0,3},{5,4},{6,5},{7,6},{4,7},{9,8},{10,9},{11,1... | collective-permute-start | bytes 172040 | tf_op jit(solution)/shard_map/ppermute | solution.py:47
  30.9 0.7 %collective-permute-start.9 = (f32[16,128]{1,0:T(8,128)S(1)}, f32[16,128]{1,0:T(8,128)S(1)}, u32[]{:S(2)}, u32[]{:S(2)}) collective-permute-start(f32[16,128]{1,0:T(8,128)S(1)} %get-tuple-element.119), channel_id=1, source_target_pairs={{2,0},{3,1},{0,2},{1,3},{6,4},{7,5},{4,6},{5,7},{10,8},{11,9},{8,1... | collective-permute-start | bytes 24584 | tf_op jit(solution)/shard_map/ppermute | solution.py:47
  31.6 1.5 %shard_map.127 = (f32[3328,128]{1,0:T(8,128)S(1)}, f32[3328,128]{1,0:T(8,128)S(1)}, f32[24,128]{1,0:T(8,128)S(1)}, f32[32,128]{1,0:T(8,128)S(1)}, f32[32,128]{1,0:T(8,128)S(1)}) custom-call(f32[3328,128]{1,0:T(8,128)S(1)} %get-tuple-element.106.refs_0_, f32[8,128]{1,0:T(8,128)S(1)} %get-tuple-element.107.refs_1_, f32[8,128]{1,0:T(8,128)S(1)} %get-tuple-element.108.refs_2_), custom_call_target="tpu_custom_call" | custom-call | bytes 6000000 | tf_op jit(solution)/shard_map/pallas_call | solution.py:888
  33.1 0.9 %shard_map.128 = (f32[128,1024]{1,0:T(8,128)S(1)}, f32[128,1024]{1,0:T(8,128)S(1)}, f32[32,128]{1,0:T(8,128)S(1)}) custom-call(f32[128,1024]{1,0:T(8,128)S(1)} %get-tuple-element.112.moved_ref, f32[128,1024]{1,0:T(8,128)S(1)} %get-tuple-element.113.bound_ref, f32[8,128]{1,0:T(8,128)S(1)} %get-tuple-element.114.added_ref, f32[128,128]{1,0:T(8,128)S(1)} %copy-done.3, ...), custom_call_target="tpu_custom_call" | custom-call | bytes 4500000 | tf_op jit(solution)/shard_map/pallas_call | solution.py:873
  34.0 1.5 %collective-permute-done.9.refs_10_ = f32[16,128]{1,0:T(8,128)S(1)} collective-permute-done((f32[16,128]{1,0:T(8,128)S(1)}, f32[16,128]{1,0:T(8,128)S(1)}, u32[]{:S(2)}, u32[]{:S(2)}) %collective-permute-start.9) | collective-permute-done | bytes 8224 | tf_op jit(solution)/shard_map/ppermute | solution.py:47
  35.5 1.4 %collective-permute-done.10.refs_11_ = f32[112,128]{1,0:T(8,128)S(1)} collective-permute-done((f32[112,128]{1,0:T(8,128)S(1)}, f32[112,128]{1,0:T(8,128)S(1)}, u32[]{:S(2)}, u32[]{:S(2)}) %collective-permute-start.10) | collective-permute-done | bytes 57376 | tf_op jit(solution)/shard_map/ppermute | solution.py:47
  37.5 2.0 %collective-permute-start.12 = (f32[40,128]{1,0:T(8,128)S(1)}, f32[40,128]{1,0:T(8,128)S(1)}, u32[]{:S(2)}, u32[]{:S(2)}) collective-permute-start(f32[40,128]{1,0:T(8,128)S(1)} %get-tuple-element.125.refs_7_.refs_15_), channel_id=1, source_target_pairs={{0,28},{4,8},{8,4},{12,16},{16,12},{20,24},{24,20},{28,0},{1,29},{... | collective-permute-start | bytes 61448 | tf_op jit(solution)/shard_map/ppermute | solution.py:54
  39.5 2.2 %collective-permute-done.12.refs_2_.refs_17_ = f32[40,128]{1,0:T(8,128)S(1)} collective-permute-done((f32[40,128]{1,0:T(8,128)S(1)}, f32[40,128]{1,0:T(8,128)S(1)}, u32[]{:S(2)}, u32[]{:S(2)}) %collective-permute-start.12) | collective-permute-done | bytes 20512 | tf_op jit(solution)/shard_map/ppermute | solution.py:54
  42.0 2.5 %collective-permute-start.13 = (f32[136,128]{1,0:T(8,128)S(1)}, f32[136,128]{1,0:T(8,128)S(1)}, u32[]{:S(2)}, u32[]{:S(2)}) collective-permute-start(f32[136,128]{1,0:T(8,128)S(1)} %get-tuple-element.135), channel_id=1, source_target_pairs={{1,0},{2,1},{3,2},{0,3},{5,4},{6,5},{7,6},{4,7},{9,8},{10,9},{11,1... | collective-permute-start | bytes 208904 | tf_op jit(solution)/shard_map/ppermute | solution.py:47
  44.5 0.6 %collective-permute-start.14 = (f32[32,128]{1,0:T(8,128)S(1)}, f32[32,128]{1,0:T(8,128)S(1)}, u32[]{:S(2)}, u32[]{:S(2)}) collective-permute-start(f32[32,128]{1,0:T(8,128)S(1)} %get-tuple-element.136), channel_id=1, source_target_pairs={{2,0},{3,1},{0,2},{1,3},{6,4},{7,5},{4,6},{5,7},{10,8},{11,9},{8,1... | collective-permute-start | bytes 49160 | tf_op jit(solution)/shard_map/ppermute | solution.py:47
  45.1 0.9 %shard_map.132 = (f32[128,1024]{1,0:T(8,128)S(1)}, f32[128,1024]{1,0:T(8,128)S(1)}, f32[32,128]{1,0:T(8,128)S(1)}) custom-call(f32[128,1024]{1,0:T(8,128)S(1)} %get-tuple-element.129.moved_ref, f32[128,1024]{1,0:T(8,128)S(1)} %get-tuple-element.130.bound_ref, f32[8,128]{1,0:T(8,128)S(1)} %get-tuple-element.131.added_ref, f32[128,128]{1,0:T(8,128)S(1)} %copy-done.3, ...), custom_call_target="tpu_custom_call" | custom-call | bytes 4500000 | tf_op jit(solution)/shard_map/pallas_call | solution.py:873
  46.0 0.8 %shard_map.131 = (f32[3328,128]{1,0:T(8,128)S(1)}, f32[3328,128]{1,0:T(8,128)S(1)}, f32[24,128]{1,0:T(8,128)S(1)}) custom-call(f32[3328,128]{1,0:T(8,128)S(1)} %get-tuple-element.123.refs_0_, f32[40,128]{1,0:T(8,128)S(1)} %collective-permute-done.11.refs_1_.refs_16_, f32[40,128]{1,0:T(8,128)S(1)} %collective-permute-done.12.refs_2_.refs_17_), custom_call_target="tpu_custom_call" | custom-call | bytes 6000000 | tf_op jit(solution)/shard_map/pallas_call | solution.py:888
  46.8 2.7 %collective-permute-done.14.refs_10_ = f32[32,128]{1,0:T(8,128)S(1)} collective-permute-done((f32[32,128]{1,0:T(8,128)S(1)}, f32[32,128]{1,0:T(8,128)S(1)}, u32[]{:S(2)}, u32[]{:S(2)}) %collective-permute-start.14) | collective-permute-done | bytes 16416 | tf_op jit(solution)/shard_map/ppermute | solution.py:47
  49.5 1.1 %collective-permute-done.15.refs_11_ = f32[136,128]{1,0:T(8,128)S(1)} collective-permute-done((f32[136,128]{1,0:T(8,128)S(1)}, f32[136,128]{1,0:T(8,128)S(1)}, u32[]{:S(2)}, u32[]{:S(2)}) %collective-permute-start.15) | collective-permute-done | bytes 69664 | tf_op jit(solution)/shard_map/ppermute | solution.py:47
  51.2 0.8 %collective-permute-start.16 = (f32[32,128]{1,0:T(8,128)S(1)}, f32[32,128]{1,0:T(8,128)S(1)}, u32[]{:S(2)}, u32[]{:S(2)}) collective-permute-start(f32[32,128]{1,0:T(8,128)S(1)} %get-tuple-element.145), channel_id=1, source_target_pairs={{3,0},{0,1},{1,2},{2,3},{7,4},{4,5},{5,6},{6,7},{11,8},{8,9},{9,10... | collective-permute-start | bytes 49160 | tf_op jit(solution)/shard_map/ppermute | solution.py:47
  52.0 3.1 %collective-permute-start.17 = (f32[32,128]{1,0:T(8,128)S(1)}, f32[32,128]{1,0:T(8,128)S(1)}, u32[]{:S(2)}, u32[]{:S(2)}) collective-permute-start(f32[32,128]{1,0:T(8,128)S(1)} %get-tuple-element.146), channel_id=1, source_target_pairs={{1,0},{2,1},{3,2},{0,3},{5,4},{6,5},{7,6},{4,7},{9,8},{10,9},{11,1... | collective-permute-start | bytes 49160 | tf_op jit(solution)/shard_map/ppermute | solution.py:47
  55.6 1.6 %shard_map.138 = (f32[128,1024]{1,0:T(8,128)}, f32[128,1024]{1,0:T(8,128)}) custom-call(f32[128,1024]{1,0:T(8,128)S(1)} %get-tuple-element.149.moved_ref, f32[128,1024]{1,0:T(8,128)S(1)} %get-tuple-element.150.bound_ref, f32[8,128]{1,0:T(8,128)S(1)} %get-tuple-element.151.added_ref, f32[128,128]{1,0:T(8,128)S(1)} %copy-done.3, f32[1,128]{1,0:T(1,128)S(1)} %bitcast.21, ...), custom_call_target="tpu_custom_call" | custom-call | bytes 4500000 | tf_op jit(solution)/shard_map/pallas_call | solution.py:873
  57.1 0.7 %shard_map.137 = (f32[16,8,128]{2,1,0:T(8,128)}, f32[16,8,128]{2,1,0:T(8,128)}) custom-call(f32[16,8,128]{2,1,0:T(8,128)S(1)} %get-tuple-element.143.drug_part, f32[16,8,128]{2,1,0:T(8,128)S(1)} %get-tuple-element.144.flow_part, f32[32,128]{1,0:T(8,128)S(1)} %collective-permute-done.16.below, f32[32,128]{1,0:T(8,128)S(1)} %collective-permute-done.17.above), custom_call_target="tpu_custom_call" | custom-call | bytes 900000 | tf_op jit(solution)/shard_map/pallas_call | solution.py:899
  (42 shorter events, 4.0 us)
Async XLA Ops:
  0.6 8.2 %copy-start = (f32[26,16,8,128]{3,2,1,0:T(8,128)S(1)}, f32[26,16,8,128]{3,2,1,0:T(8,128)}, u32[]{:S(2)}) copy-start(f32[26,16,8,128]{3,2,1,0:T(8,128)} %pops_ref.1) | copy-start | bytes 5111812
  0.6 9.3 %copy-start.1 = (f32[128,1024]{1,0:T(8,128)S(1)}, f32[128,1024]{1,0:T(8,128)}, u32[]{:S(2)}) copy-start(f32[128,1024]{1,0:T(8,128)} %free_ref.3) | copy-start | bytes 1572868
  0.7 9.3 %copy-start.2 = (f32[128,1024]{1,0:T(8,128)S(1)}, f32[128,1024]{1,0:T(8,128)}, u32[]{:S(2)}) copy-start(f32[128,1024]{1,0:T(8,128)} %bound_ref.3) | copy-start | bytes 1572868
  0.7 9.3 %copy-start.3 = (f32[128,128]{1,0:T(8,128)S(1)}, f32[128,128]{1,0:T(8,128)}, u32[]{:S(2)}) copy-start(f32[128,128]{1,0:T(8,128)} %spread_ref.9) | copy-start | bytes 196612
  0.7 9.3 %copy-start.6 = (f32[128]{0:T(128)S(1)}, f32[128]{0:T(128)}, u32[]{:S(2)}) copy-start(f32[128]{0:T(128)} %param.13) | copy-start | bytes 1540
  0.7 9.3 %copy-start.7 = (f32[128]{0:T(128)S(1)}, f32[128]{0:T(128)}, u32[]{:S(2)}) copy-start(f32[128]{0:T(128)} %param.14) | copy-start | bytes 1540
  2.6 11.0 %copy-start.4 = (s32[8,128]{1,0:T(8,128)S(1)}, s32[8,128]{1,0:T(8,128)}, u32[]{:S(2)}) copy-start(s32[8,128]{1,0:T(8,128)} %get-tuple-element.81.refs_3_) | copy-start | bytes 12292
  2.6 11.0 %copy-start.5 = (s32[1024]{0:T(1024)S(1)}, s32[1024]{0:T(1024)}, u32[]{:S(2)}) copy-start(s32[1024]{0:T(1024)} %param.17) | copy-start | bytes 12292
  2.7 10.9 %copy-start.8 = (f32[32,128]{1,0:T(8,128)S(1)}, f32[32,128]{1,0:T(8,128)}, u32[]{:S(2)}) copy-start(f32[32,128]{1,0:T(8,128)} %get-tuple-element.83.refs_8_) | copy-start | bytes 49156
  2.7 10.0 %collective-permute-start = (f32[40,128]{1,0:T(8,128)}, f32[40,128]{1,0:T(8,128)S(1)}, u32[]{:S(2)}, u32[]{:S(2)}) collective-permute-start(f32[40,128]{1,0:T(8,128)} %get-tuple-element.84), channel_id=1, source_target_pairs={{1,0},{2,1},{3,2},{0,3},{5,4},{6,5},{7,6},{4,7},{9,8},{10,9},{11,1... | collective-permute-start | bytes 61448 | tf_op jit(solution)/shard_map/ppermute | solution.py:47
  7.8 5.8 %collective-permute-start.2 = (f32[40,128]{1,0:T(8,128)}, f32[40,128]{1,0:T(8,128)S(1)}, u32[]{:S(2)}, u32[]{:S(2)}) collective-permute-start(f32[40,128]{1,0:T(8,128)} %get-tuple-element.86), channel_id=1, source_target_pairs={{3,0},{0,1},{1,2},{2,3},{7,4},{4,5},{5,6},{6,7},{11,8},{8,9},{9,10... | collective-permute-start | bytes 61448 | tf_op jit(solution)/shard_map/ppermute | solution.py:47
  7.8 4.8 %collective-permute-start.1 = (f32[32,128]{1,0:T(8,128)}, f32[32,128]{1,0:T(8,128)S(1)}, u32[]{:S(2)}, u32[]{:S(2)}) collective-permute-start(f32[32,128]{1,0:T(8,128)} %get-tuple-element.85), channel_id=1, source_target_pairs={{2,0},{3,1},{0,2},{1,3},{6,4},{7,5},{4,6},{5,7},{10,8},{11,9},{8,1... | collective-permute-start | bytes 49160 | tf_op jit(solution)/shard_map/ppermute | solution.py:47
  14.0 2.6 %collective-permute-start.3 = (f32[56,128]{1,0:T(8,128)S(1)}, f32[56,128]{1,0:T(8,128)S(1)}, u32[]{:S(2)}, u32[]{:S(2)}) collective-permute-start(f32[56,128]{1,0:T(8,128)S(1)} %get-tuple-element.90.refs_6_.refs_14_), channel_id=1, source_target_pairs={{0,4},{4,0},{8,12},{12,8},{16,20},{20,16},{24,28},{28,24},{1,5},{5... | collective-permute-start | bytes 86024 | tf_op jit(solution)/shard_map/ppermute | solution.py:54
  14.1 4.3 %collective-permute-start.4 = (f32[56,128]{1,0:T(8,128)S(1)}, f32[56,128]{1,0:T(8,128)S(1)}, u32[]{:S(2)}, u32[]{:S(2)}) collective-permute-start(f32[56,128]{1,0:T(8,128)S(1)} %get-tuple-element.91.refs_7_.refs_15_), channel_id=1, source_target_pairs={{0,28},{4,8},{8,4},{12,16},{16,12},{20,24},{24,20},{28,0},{1,29},{... | collective-permute-start | bytes 86024 | tf_op jit(solution)/shard_map/ppermute | solution.py:54
  18.6 8.3 %collective-permute-start.5 = (f32[152,128]{1,0:T(8,128)S(1)}, f32[152,128]{1,0:T(8,128)S(1)}, u32[]{:S(2)}, u32[]{:S(2)}) collective-permute-start(f32[152,128]{1,0:T(8,128)S(1)} %get-tuple-element.101), channel_id=1, source_target_pairs={{1,0},{2,1},{3,2},{0,3},{5,4},{6,5},{7,6},{4,7},{9,8},{10,9},{11,1... | collective-permute-start | bytes 233480 | tf_op jit(solution)/shard_map/ppermute | solution.py:47
  21.6 6.2 %collective-permute-start.7 = (f32[152,128]{1,0:T(8,128)S(1)}, f32[152,128]{1,0:T(8,128)S(1)}, u32[]{:S(2)}, u32[]{:S(2)}) collective-permute-start(f32[152,128]{1,0:T(8,128)S(1)} %get-tuple-element.103), channel_id=1, source_target_pairs={{3,0},{0,1},{1,2},{2,3},{7,4},{4,5},{5,6},{6,7},{11,8},{8,9},{9,10... | collective-permute-start | bytes 233480 | tf_op jit(solution)/shard_map/ppermute | solution.py:47
  21.6 5.3 %collective-permute-start.6 = (f32[48,128]{1,0:T(8,128)S(1)}, f32[48,128]{1,0:T(8,128)S(1)}, u32[]{:S(2)}, u32[]{:S(2)}) collective-permute-start(f32[48,128]{1,0:T(8,128)S(1)} %get-tuple-element.102), channel_id=1, source_target_pairs={{2,0},{3,1},{0,2},{1,3},{6,4},{7,5},{4,6},{5,7},{10,8},{11,9},{8,1... | collective-permute-start | bytes 73736 | tf_op jit(solution)/shard_map/ppermute | solution.py:47
  28.5 7.0 %collective-permute-start.8 = (f32[112,128]{1,0:T(8,128)S(1)}, f32[112,128]{1,0:T(8,128)S(1)}, u32[]{:S(2)}, u32[]{:S(2)}) collective-permute-start(f32[112,128]{1,0:T(8,128)S(1)} %get-tuple-element.118), channel_id=1, source_target_pairs={{1,0},{2,1},{3,2},{0,3},{5,4},{6,5},{7,6},{4,7},{9,8},{10,9},{11,1... | collective-permute-start | bytes 172040 | tf_op jit(solution)/shard_map/ppermute | solution.py:47
  30.9 6.0 %collective-permute-start.10 = (f32[112,128]{1,0:T(8,128)S(1)}, f32[112,128]{1,0:T(8,128)S(1)}, u32[]{:S(2)}, u32[]{:S(2)}) collective-permute-start(f32[112,128]{1,0:T(8,128)S(1)} %get-tuple-element.120), channel_id=1, source_target_pairs={{3,0},{0,1},{1,2},{2,3},{7,4},{4,5},{5,6},{6,7},{11,8},{8,9},{9,10... | collective-permute-start | bytes 172040 | tf_op jit(solution)/shard_map/ppermute | solution.py:47
  30.9 4.5 %collective-permute-start.9 = (f32[16,128]{1,0:T(8,128)S(1)}, f32[16,128]{1,0:T(8,128)S(1)}, u32[]{:S(2)}, u32[]{:S(2)}) collective-permute-start(f32[16,128]{1,0:T(8,128)S(1)} %get-tuple-element.119), channel_id=1, source_target_pairs={{2,0},{3,1},{0,2},{1,3},{6,4},{7,5},{4,6},{5,7},{10,8},{11,9},{8,1... | collective-permute-start | bytes 24584 | tf_op jit(solution)/shard_map/ppermute | solution.py:47
  37.5 2.1 %collective-permute-start.11 = (f32[40,128]{1,0:T(8,128)S(1)}, f32[40,128]{1,0:T(8,128)S(1)}, u32[]{:S(2)}, u32[]{:S(2)}) collective-permute-start(f32[40,128]{1,0:T(8,128)S(1)} %get-tuple-element.124.refs_6_.refs_14_), channel_id=1, source_target_pairs={{0,4},{4,0},{8,12},{12,8},{16,20},{20,16},{24,28},{28,24},{1,5},{5... | collective-permute-start | bytes 61448 | tf_op jit(solution)/shard_map/ppermute | solution.py:54
  37.5 4.2 %collective-permute-start.12 = (f32[40,128]{1,0:T(8,128)S(1)}, f32[40,128]{1,0:T(8,128)S(1)}, u32[]{:S(2)}, u32[]{:S(2)}) collective-permute-start(f32[40,128]{1,0:T(8,128)S(1)} %get-tuple-element.125.refs_7_.refs_15_), channel_id=1, source_target_pairs={{0,28},{4,8},{8,4},{12,16},{16,12},{20,24},{24,20},{28,0},{1,29},{... | collective-permute-start | bytes 61448 | tf_op jit(solution)/shard_map/ppermute | solution.py:54
  42.0 7.5 %collective-permute-start.13 = (f32[136,128]{1,0:T(8,128)S(1)}, f32[136,128]{1,0:T(8,128)S(1)}, u32[]{:S(2)}, u32[]{:S(2)}) collective-permute-start(f32[136,128]{1,0:T(8,128)S(1)} %get-tuple-element.135), channel_id=1, source_target_pairs={{1,0},{2,1},{3,2},{0,3},{5,4},{6,5},{7,6},{4,7},{9,8},{10,9},{11,1... | collective-permute-start | bytes 208904 | tf_op jit(solution)/shard_map/ppermute | solution.py:47
  44.5 6.1 %collective-permute-start.15 = (f32[136,128]{1,0:T(8,128)S(1)}, f32[136,128]{1,0:T(8,128)S(1)}, u32[]{:S(2)}, u32[]{:S(2)}) collective-permute-start(f32[136,128]{1,0:T(8,128)S(1)} %get-tuple-element.137), channel_id=1, source_target_pairs={{3,0},{0,1},{1,2},{2,3},{7,4},{4,5},{5,6},{6,7},{11,8},{8,9},{9,10... | collective-permute-start | bytes 208904 | tf_op jit(solution)/shard_map/ppermute | solution.py:47
  44.5 5.0 %collective-permute-start.14 = (f32[32,128]{1,0:T(8,128)S(1)}, f32[32,128]{1,0:T(8,128)S(1)}, u32[]{:S(2)}, u32[]{:S(2)}) collective-permute-start(f32[32,128]{1,0:T(8,128)S(1)} %get-tuple-element.136), channel_id=1, source_target_pairs={{2,0},{3,1},{0,2},{1,3},{6,4},{7,5},{4,6},{5,7},{10,8},{11,9},{8,1... | collective-permute-start | bytes 49160 | tf_op jit(solution)/shard_map/ppermute | solution.py:47
  51.2 5.9 %collective-permute-start.16 = (f32[32,128]{1,0:T(8,128)S(1)}, f32[32,128]{1,0:T(8,128)S(1)}, u32[]{:S(2)}, u32[]{:S(2)}) collective-permute-start(f32[32,128]{1,0:T(8,128)S(1)} %get-tuple-element.145), channel_id=1, source_target_pairs={{3,0},{0,1},{1,2},{2,3},{7,4},{4,5},{5,6},{6,7},{11,8},{8,9},{9,10... | collective-permute-start | bytes 49160 | tf_op jit(solution)/shard_map/ppermute | solution.py:47
  52.0 5.1 %collective-permute-start.17 = (f32[32,128]{1,0:T(8,128)S(1)}, f32[32,128]{1,0:T(8,128)S(1)}, u32[]{:S(2)}, u32[]{:S(2)}) collective-permute-start(f32[32,128]{1,0:T(8,128)S(1)} %get-tuple-element.146), channel_id=1, source_target_pairs={{1,0},{2,1},{3,2},{0,3},{5,4},{6,5},{7,6},{4,7},{9,8},{10,9},{11,1... | collective-permute-start | bytes 49160 | tf_op jit(solution)/shard_map/ppermute | solution.py:47

commit v5 on v4

--- a/solution.py
+++ b/solution.py
@@ -153,6 +153,16 @@
         return jnp.where(lane == 0, pltpu.roll(behind, (-slot) % along, 1), pltpu.roll(value, 1, 1))
     slot = SLAB_FALLING.index(member) * radial + level
     return jnp.where(lane == along - 1, pltpu.roll(ahead, (along - 1 - slot) % along, 1), pltpu.roll(value, along - 1, 1))
+
+
+def axial_shift_rows(post, member, step, side, behind, ahead):
+    value = post.rows(member, 0, post.radial, side)
+    along = value.shape[-1]
+    tile, slots = (behind, SLAB_RISING) if step == 1 else (ahead, SLAB_FALLING)
+    lane = lanes(value.shape)
+    here = lane - sublanes(value.shape) == slots.index(member) * post.radial
+    column = jnp.sum(jnp.where(here, tile[side:side + 1, :], 0.0), axis=1, keepdims=True)
+    return jnp.where(lane == (0 if step == 1 else along - 1), column, pltpu.roll(value, step % along, 1))
 
 
 def streamed(post, member, level, behind, ahead):
@@ -619,8 +629,9 @@
 def plan_ahead(left, rates, free, bound):
     rate_on, rate_off, entry, top = rates
     moved = product(left, free)
-    rate = rate_on * moved * (1.0 - bound) - rate_off * bound
-    gain = rate_on * entry * (1.0 - bound)
+    room = rate_on * (1.0 - bound)
+    rate = room * moved - rate_off * bound
+    gain = room * entry
     first = jnp.sum(top * (moved - rate), axis=0, keepdims=True)
     slope = jnp.sum(top * (entry - gain), axis=0, keepdims=True)
     return moved, (first, slope, bound[0:1, :] + rate[0:1, :], gain[0:1, :])
@@ -714,9 +725,7 @@
             moving = VELOCITIES[member][0]
             base = start + place * radial
             if moving:
-                for level in range(radial):
-                    value = axial_shift(post.get(member, level), moving, member, level, radial, behind, ahead)
-                    out[base + level:base + level + 1, :] = value[side:side + 1, :]
+                out[base:base + radial, :] = axial_shift_rows(post, member, moving, side, behind, ahead)
             else:
                 out[base:base + radial, :] = post.rows(member, 0, radial, side)
     if packed:
@@ -735,10 +744,8 @@
     behind, ahead = axial_rims(False, inner_ref, outer_ref, across)
     for out, drug, plus, minus, side in ((up_ref, FLOWS + 3, 7, 10, across - 1), (down_ref, FLOWS + 4, 9, 8, 0)):
         out[0:radial, :] = post.rows(drug, 0, radial, side)
-        for level in range(radial):
-            value = axial_shift(post.get(plus, level), 1, plus, level, radial, behind, ahead)
-            value = value - axial_shift(post.get(minus, level), -1, minus, level, radial, behind, ahead)
-            out[radial + level:radial + level + 1, :] = value[side:side + 1, :]
+        value = axial_shift_rows(post, plus, 1, side, behind, ahead)
+        out[radial:2 * radial, :] = value - axial_shift_rows(post, minus, -1, side, behind, ahead)
 
 
 def fields_kernel(radial, across, post_ref, inner_ref, outer_ref, drug_ref, flow_ref):
@@ -807,7 +814,8 @@
             VMEM((across, free.shape[1]), F32),
             pltpu.SemaphoreType.DMA((5,)),
         ],
-    )(populations, sector, line, strut, free)
+        compiler_params=pltpu.CompilerParams(vmem_limit_bytes=24 * 1024 * 1024),
+    )(*[pltpu.with_memory_space_constraint(x, pltpu.HBM) for x in (populations, sector, line, strut, free)])
 
 
 def per_device(populations, wall_free, wall_bound, wall_propagator, bind_on, bind_off, iface_sector, iface_line, strut_mask):

time: 58 us -> 57 us (0.983)
  Pallas kernels: 14.9 us -> 14.1 us
    pallas_call x1, Pallas kernels: 1.93 us -> 1.32 us  [first_call(): pl.pallas_call(functools.partial(first_kernel, sectors), name='first', ou...]
  transfers between devices with their start and end apart: 18 -> 18, of which waited for: 10 -> 10; matrix products, arithmetic and copies ran while one was open for 0% -> 0% of each run, Pallas kernels for 16% -> 17%
where the time goes in v5:
time: 57 us; the launch traced here: 56.8 us
  starting transfers between devices  24.4 us (43%)
  waiting for transfers between devices  17.4 us (31%)
  Pallas kernels  14.1 us (25%)
  between operations  0.88 us (2%)
    ppermute x14, starting transfers between devices, shifted(): lax.ppermute(block, axis, [((i - distance) % count, i) for i in range(cou...  19.8 us
    ppermute x14, waiting for transfers between devices, shifted(): lax.ppermute(block, axis, [((i - distance) % count, i) for i in range(cou...  13.5 us
    ppermute x4, starting transfers between devices, paired(): return (lax.ppermute(inner, 'ax', near), lax.ppermute(outer, 'ax', far))  4.63 us
    pallas_call x4, Pallas kernels, per_device(): kernel_call(functools.partial(wall_kernel, last), [shapes, shapes] + ([]...  4.3 us
    ppermute x4, waiting for transfers between devices, paired(): return (lax.ppermute(inner, 'ax', near), lax.ppermute(outer, 'ax', far))  3.94 us
    pallas_call x3, Pallas kernels, per_device(): kernel_call(functools.partial(bulk_kernel, False, not odd, odd, radial, a...  3.01 us
    pallas_call x4, Pallas kernels, per_device(): kernel_call(functools.partial(flux_kernel, sectors, step, radial), outs,...  1.78 us
    pallas_call x1, Pallas kernels, first_call(): pl.pallas_call(functools.partial(first_kernel, sectors), name='first', ou...  1.32 us
  transfers between devices with their start and end apart: 18, of which 10 were waited for; matrix products, arithmetic and copies ran while one was open for 0% of the time, Pallas kernels for 17%

profile of v5, /device:TPU:0, one launch (start us, length us, event | category | flops | bytes accessed | tf_op | source)
XLA Modules:
  0.0 56.8 jit_solution(7112236409007272641)
XLA Ops:
  0.7 1.3 %first.1 = (s32[8,128]{1,0:T(8,128)S(1)}, f32[32,128]{1,0:T(8,128)S(1)}, f32[40,128]{1,0:T(8,128)S(1)}, f32[32,128]{1,0:T(8,128)S(1)}, f32[40,128]{1,0:T(8,128)S(1)}) custom-call(f32[26,16,8,128]{3,2,1,0:T(8,128)} %pops_ref.1, s32[8,128]{1,0:T(8,128)} %bitcast.31, s32[8,128]{1,0:T(8,128)} %bitcast.32, s32[8,128]{1,0:T(8,128)} %bitcast.8, f32[128,1024]{1,0:T(8,128)} %free_ref.3), custom_call_target="tpu_custom_call" | custom-call | tf_op jit(solution)/shard_map/first/pallas_call | solution.py:803
  2.0 5.1 %collective-permute-start = (f32[40,128]{1,0:T(8,128)S(1)}, f32[40,128]{1,0:T(8,128)S(1)}, u32[]{:S(2)}, u32[]{:S(2)}) collective-permute-start(f32[40,128]{1,0:T(8,128)S(1)} %get-tuple-element.84), channel_id=1, source_target_pairs={{1,0},{2,1},{3,2},{0,3},{5,4},{6,5},{7,6},{4,7},{9,8},{10,9},{11,1... | collective-permute-start | bytes 61448 | tf_op jit(solution)/shard_map/ppermute | solution.py:47
  7.2 1.0 %collective-permute-start.1 = (f32[32,128]{1,0:T(8,128)S(1)}, f32[32,128]{1,0:T(8,128)S(1)}, u32[]{:S(2)}, u32[]{:S(2)}) collective-permute-start(f32[32,128]{1,0:T(8,128)S(1)} %get-tuple-element.85), channel_id=1, source_target_pairs={{2,0},{3,1},{0,2},{1,3},{6,4},{7,5},{4,6},{5,7},{10,8},{11,9},{8,1... | collective-permute-start | bytes 49160 | tf_op jit(solution)/shard_map/ppermute | solution.py:47
  8.2 1.2 %shard_map.120 = (f32[3328,128]{1,0:T(8,128)S(1)}, f32[24,128]{1,0:T(8,128)S(1)}, f32[32,128]{1,0:T(8,128)S(1)}, f32[32,128]{1,0:T(8,128)S(1)}) custom-call(f32[3328,128]{1,0:T(8,128)S(1)} %bitcast.6), custom_call_target="tpu_custom_call" | custom-call | bytes 4500000 | tf_op jit(solution)/shard_map/pallas_call | solution.py:845
  9.8 2.0 %collective-permute-done.1.refs_10_ = f32[32,128]{1,0:T(8,128)S(1)} collective-permute-done((f32[32,128]{1,0:T(8,128)S(1)}, f32[32,128]{1,0:T(8,128)S(1)}, u32[]{:S(2)}, u32[]{:S(2)}) %collective-permute-start.1) | collective-permute-done | bytes 16416 | tf_op jit(solution)/shard_map/ppermute | solution.py:47
  11.8 0.9 %collective-permute-done.2.refs_11_ = f32[40,128]{1,0:T(8,128)S(1)} collective-permute-done((f32[40,128]{1,0:T(8,128)S(1)}, f32[40,128]{1,0:T(8,128)S(1)}, u32[]{:S(2)}, u32[]{:S(2)}) %collective-permute-start.2) | collective-permute-done | bytes 20512 | tf_op jit(solution)/shard_map/ppermute | solution.py:47
  13.2 2.5 %collective-permute-start.4 = (f32[56,128]{1,0:T(8,128)S(1)}, f32[56,128]{1,0:T(8,128)S(1)}, u32[]{:S(2)}, u32[]{:S(2)}) collective-permute-start(f32[56,128]{1,0:T(8,128)S(1)} %get-tuple-element.91.refs_7_.refs_15_), channel_id=1, source_target_pairs={{0,28},{4,8},{8,4},{12,16},{16,12},{20,24},{24,20},{28,0},{1,29},{... | collective-permute-start | bytes 86024 | tf_op jit(solution)/shard_map/ppermute | solution.py:54
  15.8 1.7 %collective-permute-done.4.refs_2_.refs_17_ = f32[56,128]{1,0:T(8,128)S(1)} collective-permute-done((f32[56,128]{1,0:T(8,128)S(1)}, f32[56,128]{1,0:T(8,128)S(1)}, u32[]{:S(2)}, u32[]{:S(2)}) %collective-permute-start.4) | collective-permute-done | bytes 28704 | tf_op jit(solution)/shard_map/ppermute | solution.py:54
  17.8 2.9 %collective-permute-start.5 = (f32[152,128]{1,0:T(8,128)S(1)}, f32[152,128]{1,0:T(8,128)S(1)}, u32[]{:S(2)}, u32[]{:S(2)}) collective-permute-start(f32[152,128]{1,0:T(8,128)S(1)} %get-tuple-element.101), channel_id=1, source_target_pairs={{1,0},{2,1},{3,2},{0,3},{5,4},{6,5},{7,6},{4,7},{9,8},{10,9},{11,1... | collective-permute-start | bytes 233480 | tf_op jit(solution)/shard_map/ppermute | solution.py:47
  20.7 0.6 %collective-permute-start.6 = (f32[48,128]{1,0:T(8,128)S(1)}, f32[48,128]{1,0:T(8,128)S(1)}, u32[]{:S(2)}, u32[]{:S(2)}) collective-permute-start(f32[48,128]{1,0:T(8,128)S(1)} %get-tuple-element.102), channel_id=1, source_target_pairs={{2,0},{3,1},{0,2},{1,3},{6,4},{7,5},{4,6},{5,7},{10,8},{11,9},{8,1... | collective-permute-start | bytes 73736 | tf_op jit(solution)/shard_map/ppermute | solution.py:47
  21.3 0.9 %shard_map.124 = (f32[128,1024]{1,0:T(8,128)S(1)}, f32[128,1024]{1,0:T(8,128)S(1)}, f32[32,128]{1,0:T(8,128)S(1)}) custom-call(f32[128,1024]{1,0:T(8,128)S(1)} %get-tuple-element.95.moved_ref, f32[128,1024]{1,0:T(8,128)S(1)} %copy-done.2, f32[8,128]{1,0:T(8,128)S(1)} %get-tuple-element.96.added_ref, f32[128,128]{1,0:T(8,128)S(1)} %copy-done.3, ...), custom_call_target="tpu_custom_call" | custom-call | bytes 4500000 | tf_op jit(solution)/shard_map/pallas_call | solution.py:881
  22.3 0.8 %shard_map.123 = (f32[3328,128]{1,0:T(8,128)S(1)}, f32[3328,128]{1,0:T(8,128)S(1)}, f32[24,128]{1,0:T(8,128)S(1)}) custom-call(f32[3328,128]{1,0:T(8,128)S(1)} %get-tuple-element.89.refs_0_, f32[56,128]{1,0:T(8,128)S(1)} %collective-permute-done.3.refs_1_.refs_16_, f32[56,128]{1,0:T(8,128)S(1)} %collective-permute-done.4.refs_2_.refs_17_), custom_call_target="tpu_custom_call" | custom-call | bytes 6000000 | tf_op jit(solution)/shard_map/pallas_call | solution.py:896
  23.0 3.0 %collective-permute-done.6.refs_10_ = f32[48,128]{1,0:T(8,128)S(1)} collective-permute-done((f32[48,128]{1,0:T(8,128)S(1)}, f32[48,128]{1,0:T(8,128)S(1)}, u32[]{:S(2)}, u32[]{:S(2)}) %collective-permute-start.6) | collective-permute-done | bytes 24608 | tf_op jit(solution)/shard_map/ppermute | solution.py:47
  26.0 0.9 %collective-permute-done.7.refs_11_ = f32[152,128]{1,0:T(8,128)S(1)} collective-permute-done((f32[152,128]{1,0:T(8,128)S(1)}, f32[152,128]{1,0:T(8,128)S(1)}, u32[]{:S(2)}, u32[]{:S(2)}) %collective-permute-start.7) | collective-permute-done | bytes 77856 | tf_op jit(solution)/shard_map/ppermute | solution.py:47
  27.6 2.4 %collective-permute-start.8 = (f32[112,128]{1,0:T(8,128)S(1)}, f32[112,128]{1,0:T(8,128)S(1)}, u32[]{:S(2)}, u32[]{:S(2)}) collective-permute-start(f32[112,128]{1,0:T(8,128)S(1)} %get-tuple-element.118), channel_id=1, source_target_pairs={{1,0},{2,1},{3,2},{0,3},{5,4},{6,5},{7,6},{4,7},{9,8},{10,9},{11,1... | collective-permute-start | bytes 172040 | tf_op jit(solution)/shard_map/ppermute | solution.py:47
  30.1 0.7 %collective-permute-start.9 = (f32[16,128]{1,0:T(8,128)S(1)}, f32[16,128]{1,0:T(8,128)S(1)}, u32[]{:S(2)}, u32[]{:S(2)}) collective-permute-start(f32[16,128]{1,0:T(8,128)S(1)} %get-tuple-element.119), channel_id=1, source_target_pairs={{2,0},{3,1},{0,2},{1,3},{6,4},{7,5},{4,6},{5,7},{10,8},{11,9},{8,1... | collective-permute-start | bytes 24584 | tf_op jit(solution)/shard_map/ppermute | solution.py:47
  30.7 1.5 %shard_map.127 = (f32[3328,128]{1,0:T(8,128)S(1)}, f32[3328,128]{1,0:T(8,128)S(1)}, f32[24,128]{1,0:T(8,128)S(1)}, f32[32,128]{1,0:T(8,128)S(1)}, f32[32,128]{1,0:T(8,128)S(1)}) custom-call(f32[3328,128]{1,0:T(8,128)S(1)} %get-tuple-element.106.refs_0_, f32[8,128]{1,0:T(8,128)S(1)} %get-tuple-element.107.refs_1_, f32[8,128]{1,0:T(8,128)S(1)} %get-tuple-element.108.refs_2_), custom_call_target="tpu_custom_call" | custom-call | bytes 6000000 | tf_op jit(solution)/shard_map/pallas_call | solution.py:896
  32.2 0.9 %shard_map.128 = (f32[128,1024]{1,0:T(8,128)S(1)}, f32[128,1024]{1,0:T(8,128)S(1)}, f32[32,128]{1,0:T(8,128)S(1)}) custom-call(f32[128,1024]{1,0:T(8,128)S(1)} %get-tuple-element.112.moved_ref, f32[128,1024]{1,0:T(8,128)S(1)} %get-tuple-element.113.bound_ref, f32[8,128]{1,0:T(8,128)S(1)} %get-tuple-element.114.added_ref, f32[128,128]{1,0:T(8,128)S(1)} %copy-done.3, ...), custom_call_target="tpu_custom_call" | custom-call | bytes 4500000 | tf_op jit(solution)/shard_map/pallas_call | solution.py:881
  33.1 1.5 %collective-permute-done.9.refs_10_ = f32[16,128]{1,0:T(8,128)S(1)} collective-permute-done((f32[16,128]{1,0:T(8,128)S(1)}, f32[16,128]{1,0:T(8,128)S(1)}, u32[]{:S(2)}, u32[]{:S(2)}) %collective-permute-start.9) | collective-permute-done | bytes 8224 | tf_op jit(solution)/shard_map/ppermute | solution.py:47
  34.6 1.4 %collective-permute-done.10.refs_11_ = f32[112,128]{1,0:T(8,128)S(1)} collective-permute-done((f32[112,128]{1,0:T(8,128)S(1)}, f32[112,128]{1,0:T(8,128)S(1)}, u32[]{:S(2)}, u32[]{:S(2)}) %collective-permute-start.10) | collective-permute-done | bytes 57376 | tf_op jit(solution)/shard_map/ppermute | solution.py:47
  36.7 1.9 %collective-permute-start.12 = (f32[40,128]{1,0:T(8,128)S(1)}, f32[40,128]{1,0:T(8,128)S(1)}, u32[]{:S(2)}, u32[]{:S(2)}) collective-permute-start(f32[40,128]{1,0:T(8,128)S(1)} %get-tuple-element.125.refs_7_.refs_15_), channel_id=1, source_target_pairs={{0,28},{4,8},{8,4},{12,16},{16,12},{20,24},{24,20},{28,0},{1,29},{... | collective-permute-start | bytes 61448 | tf_op jit(solution)/shard_map/ppermute | solution.py:54
  38.6 2.2 %collective-permute-done.12.refs_2_.refs_17_ = f32[40,128]{1,0:T(8,128)S(1)} collective-permute-done((f32[40,128]{1,0:T(8,128)S(1)}, f32[40,128]{1,0:T(8,128)S(1)}, u32[]{:S(2)}, u32[]{:S(2)}) %collective-permute-start.12) | collective-permute-done | bytes 20512 | tf_op jit(solution)/shard_map/ppermute | solution.py:54
  41.1 2.5 %collective-permute-start.13 = (f32[136,128]{1,0:T(8,128)S(1)}, f32[136,128]{1,0:T(8,128)S(1)}, u32[]{:S(2)}, u32[]{:S(2)}) collective-permute-start(f32[136,128]{1,0:T(8,128)S(1)} %get-tuple-element.135), channel_id=1, source_target_pairs={{1,0},{2,1},{3,2},{0,3},{5,4},{6,5},{7,6},{4,7},{9,8},{10,9},{11,1... | collective-permute-start | bytes 208904 | tf_op jit(solution)/shard_map/ppermute | solution.py:47
  43.6 0.6 %collective-permute-start.14 = (f32[32,128]{1,0:T(8,128)S(1)}, f32[32,128]{1,0:T(8,128)S(1)}, u32[]{:S(2)}, u32[]{:S(2)}) collective-permute-start(f32[32,128]{1,0:T(8,128)S(1)} %get-tuple-element.136), channel_id=1, source_target_pairs={{2,0},{3,1},{0,2},{1,3},{6,4},{7,5},{4,6},{5,7},{10,8},{11,9},{8,1... | collective-permute-start | bytes 49160 | tf_op jit(solution)/shard_map/ppermute | solution.py:47
  44.2 0.9 %shard_map.132 = (f32[128,1024]{1,0:T(8,128)S(1)}, f32[128,1024]{1,0:T(8,128)S(1)}, f32[32,128]{1,0:T(8,128)S(1)}) custom-call(f32[128,1024]{1,0:T(8,128)S(1)} %get-tuple-element.129.moved_ref, f32[128,1024]{1,0:T(8,128)S(1)} %get-tuple-element.130.bound_ref, f32[8,128]{1,0:T(8,128)S(1)} %get-tuple-element.131.added_ref, f32[128,128]{1,0:T(8,128)S(1)} %copy-done.3, ...), custom_call_target="tpu_custom_call" | custom-call | bytes 4500000 | tf_op jit(solution)/shard_map/pallas_call | solution.py:881
  45.1 0.8 %shard_map.131 = (f32[3328,128]{1,0:T(8,128)S(1)}, f32[3328,128]{1,0:T(8,128)S(1)}, f32[24,128]{1,0:T(8,128)S(1)}) custom-call(f32[3328,128]{1,0:T(8,128)S(1)} %get-tuple-element.123.refs_0_, f32[40,128]{1,0:T(8,128)S(1)} %collective-permute-done.11.refs_1_.refs_16_, f32[40,128]{1,0:T(8,128)S(1)} %collective-permute-done.12.refs_2_.refs_17_), custom_call_target="tpu_custom_call" | custom-call | bytes 6000000 | tf_op jit(solution)/shard_map/pallas_call | solution.py:896
  45.9 2.7 %collective-permute-done.14.refs_10_ = f32[32,128]{1,0:T(8,128)S(1)} collective-permute-done((f32[32,128]{1,0:T(8,128)S(1)}, f32[32,128]{1,0:T(8,128)S(1)}, u32[]{:S(2)}, u32[]{:S(2)}) %collective-permute-start.14) | collective-permute-done | bytes 16416 | tf_op jit(solution)/shard_map/ppermute | solution.py:47
  48.6 1.1 %collective-permute-done.15.refs_11_ = f32[136,128]{1,0:T(8,128)S(1)} collective-permute-done((f32[136,128]{1,0:T(8,128)S(1)}, f32[136,128]{1,0:T(8,128)S(1)}, u32[]{:S(2)}, u32[]{:S(2)}) %collective-permute-start.15) | collective-permute-done | bytes 69664 | tf_op jit(solution)/shard_map/ppermute | solution.py:47
  50.2 0.8 %collective-permute-start.16 = (f32[32,128]{1,0:T(8,128)S(1)}, f32[32,128]{1,0:T(8,128)S(1)}, u32[]{:S(2)}, u32[]{:S(2)}) collective-permute-start(f32[32,128]{1,0:T(8,128)S(1)} %get-tuple-element.145), channel_id=1, source_target_pairs={{3,0},{0,1},{1,2},{2,3},{7,4},{4,5},{5,6},{6,7},{11,8},{8,9},{9,10... | collective-permute-start | bytes 49160 | tf_op jit(solution)/shard_map/ppermute | solution.py:47
  51.0 3.1 %collective-permute-start.17 = (f32[32,128]{1,0:T(8,128)S(1)}, f32[32,128]{1,0:T(8,128)S(1)}, u32[]{:S(2)}, u32[]{:S(2)}) collective-permute-start(f32[32,128]{1,0:T(8,128)S(1)} %get-tuple-element.146), channel_id=1, source_target_pairs={{1,0},{2,1},{3,2},{0,3},{5,4},{6,5},{7,6},{4,7},{9,8},{10,9},{11,1... | collective-permute-start | bytes 49160 | tf_op jit(solution)/shard_map/ppermute | solution.py:47
  54.6 1.6 %shard_map.138 = (f32[128,1024]{1,0:T(8,128)}, f32[128,1024]{1,0:T(8,128)}) custom-call(f32[128,1024]{1,0:T(8,128)S(1)} %get-tuple-element.149.moved_ref, f32[128,1024]{1,0:T(8,128)S(1)} %get-tuple-element.150.bound_ref, f32[8,128]{1,0:T(8,128)S(1)} %get-tuple-element.151.added_ref, f32[128,128]{1,0:T(8,128)S(1)} %copy-done.3, f32[1,128]{1,0:T(1,128)S(1)} %bitcast.21, ...), custom_call_target="tpu_custom_call" | custom-call | bytes 4500000 | tf_op jit(solution)/shard_map/pallas_call | solution.py:881
  56.1 0.7 %shard_map.137 = (f32[16,8,128]{2,1,0:T(8,128)}, f32[16,8,128]{2,1,0:T(8,128)}) custom-call(f32[16,8,128]{2,1,0:T(8,128)S(1)} %get-tuple-element.143.drug_part, f32[16,8,128]{2,1,0:T(8,128)S(1)} %get-tuple-element.144.flow_part, f32[32,128]{1,0:T(8,128)S(1)} %collective-permute-done.16.below, f32[32,128]{1,0:T(8,128)S(1)} %collective-permute-done.17.above), custom_call_target="tpu_custom_call" | custom-call | bytes 900000 | tf_op jit(solution)/shard_map/pallas_call | solution.py:907
  (38 shorter events, 3.8 us)
Async XLA Ops:
  0.6 7.5 %copy-start = (f32[26,16,8,128]{3,2,1,0:T(8,128)S(1)}, f32[26,16,8,128]{3,2,1,0:T(8,128)}, u32[]{:S(2)}) copy-start(f32[26,16,8,128]{3,2,1,0:T(8,128)} %pops_ref.1) | copy-start | bytes 5111812
  0.6 8.7 %copy-start.1 = (f32[128,1024]{1,0:T(8,128)S(1)}, f32[128,1024]{1,0:T(8,128)}, u32[]{:S(2)}) copy-start(f32[128,1024]{1,0:T(8,128)} %free_ref.3) | copy-start | bytes 1572868
  0.7 8.7 %copy-start.2 = (f32[128,1024]{1,0:T(8,128)S(1)}, f32[128,1024]{1,0:T(8,128)}, u32[]{:S(2)}) copy-start(f32[128,1024]{1,0:T(8,128)} %bound_ref.3) | copy-start | bytes 1572868
  0.7 8.7 %copy-start.3 = (f32[128,128]{1,0:T(8,128)S(1)}, f32[128,128]{1,0:T(8,128)}, u32[]{:S(2)}) copy-start(f32[128,128]{1,0:T(8,128)} %spread_ref.9) | copy-start | bytes 196612
  0.7 8.7 %copy-start.5 = (f32[128]{0:T(128)S(1)}, f32[128]{0:T(128)}, u32[]{:S(2)}) copy-start(f32[128]{0:T(128)} %param.13) | copy-start | bytes 1540
  0.7 8.7 %copy-start.6 = (f32[128]{0:T(128)S(1)}, f32[128]{0:T(128)}, u32[]{:S(2)}) copy-start(f32[128]{0:T(128)} %param.14) | copy-start | bytes 1540
  2.0 10.7 %copy-start.4 = (s32[1024]{0:T(1024)S(1)}, s32[1024]{0:T(1024)}, u32[]{:S(2)}) copy-start(s32[1024]{0:T(1024)} %param.17) | copy-start | bytes 12292
  2.0 9.8 %collective-permute-start = (f32[40,128]{1,0:T(8,128)S(1)}, f32[40,128]{1,0:T(8,128)S(1)}, u32[]{:S(2)}, u32[]{:S(2)}) collective-permute-start(f32[40,128]{1,0:T(8,128)S(1)} %get-tuple-element.84), channel_id=1, source_target_pairs={{1,0},{2,1},{3,2},{0,3},{5,4},{6,5},{7,6},{4,7},{9,8},{10,9},{11,1... | collective-permute-start | bytes 61448 | tf_op jit(solution)/shard_map/ppermute | solution.py:47
  7.2 5.6 %collective-permute-start.2 = (f32[40,128]{1,0:T(8,128)S(1)}, f32[40,128]{1,0:T(8,128)S(1)}, u32[]{:S(2)}, u32[]{:S(2)}) collective-permute-start(f32[40,128]{1,0:T(8,128)S(1)} %get-tuple-element.86), channel_id=1, source_target_pairs={{3,0},{0,1},{1,2},{2,3},{7,4},{4,5},{5,6},{6,7},{11,8},{8,9},{9,10... | collective-permute-start | bytes 61448 | tf_op jit(solution)/shard_map/ppermute | solution.py:47
  7.2 4.6 %collective-permute-start.1 = (f32[32,128]{1,0:T(8,128)S(1)}, f32[32,128]{1,0:T(8,128)S(1)}, u32[]{:S(2)}, u32[]{:S(2)}) collective-permute-start(f32[32,128]{1,0:T(8,128)S(1)} %get-tuple-element.85), channel_id=1, source_target_pairs={{2,0},{3,1},{0,2},{1,3},{6,4},{7,5},{4,6},{5,7},{10,8},{11,9},{8,1... | collective-permute-start | bytes 49160 | tf_op jit(solution)/shard_map/ppermute | solution.py:47
  13.1 2.6 %collective-permute-start.3 = (f32[56,128]{1,0:T(8,128)S(1)}, f32[56,128]{1,0:T(8,128)S(1)}, u32[]{:S(2)}, u32[]{:S(2)}) collective-permute-start(f32[56,128]{1,0:T(8,128)S(1)} %get-tuple-element.90.refs_6_.refs_14_), channel_id=1, source_target_pairs={{0,4},{4,0},{8,12},{12,8},{16,20},{20,16},{24,28},{28,24},{1,5},{5... | collective-permute-start | bytes 86024 | tf_op jit(solution)/shard_map/ppermute | solution.py:54
  13.2 4.3 %collective-permute-start.4 = (f32[56,128]{1,0:T(8,128)S(1)}, f32[56,128]{1,0:T(8,128)S(1)}, u32[]{:S(2)}, u32[]{:S(2)}) collective-permute-start(f32[56,128]{1,0:T(8,128)S(1)} %get-tuple-element.91.refs_7_.refs_15_), channel_id=1, source_target_pairs={{0,28},{4,8},{8,4},{12,16},{16,12},{20,24},{24,20},{28,0},{1,29},{... | collective-permute-start | bytes 86024 | tf_op jit(solution)/shard_map/ppermute | solution.py:54
  17.8 8.3 %collective-permute-start.5 = (f32[152,128]{1,0:T(8,128)S(1)}, f32[152,128]{1,0:T(8,128)S(1)}, u32[]{:S(2)}, u32[]{:S(2)}) collective-permute-start(f32[152,128]{1,0:T(8,128)S(1)} %get-tuple-element.101), channel_id=1, source_target_pairs={{1,0},{2,1},{3,2},{0,3},{5,4},{6,5},{7,6},{4,7},{9,8},{10,9},{11,1... | collective-permute-start | bytes 233480 | tf_op jit(solution)/shard_map/ppermute | solution.py:47
  20.7 6.2 %collective-permute-start.7 = (f32[152,128]{1,0:T(8,128)S(1)}, f32[152,128]{1,0:T(8,128)S(1)}, u32[]{:S(2)}, u32[]{:S(2)}) collective-permute-start(f32[152,128]{1,0:T(8,128)S(1)} %get-tuple-element.103), channel_id=1, source_target_pairs={{3,0},{0,1},{1,2},{2,3},{7,4},{4,5},{5,6},{6,7},{11,8},{8,9},{9,10... | collective-permute-start | bytes 233480 | tf_op jit(solution)/shard_map/ppermute | solution.py:47
  20.7 5.3 %collective-permute-start.6 = (f32[48,128]{1,0:T(8,128)S(1)}, f32[48,128]{1,0:T(8,128)S(1)}, u32[]{:S(2)}, u32[]{:S(2)}) collective-permute-start(f32[48,128]{1,0:T(8,128)S(1)} %get-tuple-element.102), channel_id=1, source_target_pairs={{2,0},{3,1},{0,2},{1,3},{6,4},{7,5},{4,6},{5,7},{10,8},{11,9},{8,1... | collective-permute-start | bytes 73736 | tf_op jit(solution)/shard_map/ppermute | solution.py:47
  27.6 7.0 %collective-permute-start.8 = (f32[112,128]{1,0:T(8,128)S(1)}, f32[112,128]{1,0:T(8,128)S(1)}, u32[]{:S(2)}, u32[]{:S(2)}) collective-permute-start(f32[112,128]{1,0:T(8,128)S(1)} %get-tuple-element.118), channel_id=1, source_target_pairs={{1,0},{2,1},{3,2},{0,3},{5,4},{6,5},{7,6},{4,7},{9,8},{10,9},{11,1... | collective-permute-start | bytes 172040 | tf_op jit(solution)/shard_map/ppermute | solution.py:47
  30.1 6.0 %collective-permute-start.10 = (f32[112,128]{1,0:T(8,128)S(1)}, f32[112,128]{1,0:T(8,128)S(1)}, u32[]{:S(2)}, u32[]{:S(2)}) collective-permute-start(f32[112,128]{1,0:T(8,128)S(1)} %get-tuple-element.120), channel_id=1, source_target_pairs={{3,0},{0,1},{1,2},{2,3},{7,4},{4,5},{5,6},{6,7},{11,8},{8,9},{9,10... | collective-permute-start | bytes 172040 | tf_op jit(solution)/shard_map/ppermute | solution.py:47
  30.1 4.5 %collective-permute-start.9 = (f32[16,128]{1,0:T(8,128)S(1)}, f32[16,128]{1,0:T(8,128)S(1)}, u32[]{:S(2)}, u32[]{:S(2)}) collective-permute-start(f32[16,128]{1,0:T(8,128)S(1)} %get-tuple-element.119), channel_id=1, source_target_pairs={{2,0},{3,1},{0,2},{1,3},{6,4},{7,5},{4,6},{5,7},{10,8},{11,9},{8,1... | collective-permute-start | bytes 24584 | tf_op jit(solution)/shard_map/ppermute | solution.py:47
  36.6 2.0 %collective-permute-start.11 = (f32[40,128]{1,0:T(8,128)S(1)}, f32[40,128]{1,0:T(8,128)S(1)}, u32[]{:S(2)}, u32[]{:S(2)}) collective-permute-start(f32[40,128]{1,0:T(8,128)S(1)} %get-tuple-element.124.refs_6_.refs_14_), channel_id=1, source_target_pairs={{0,4},{4,0},{8,12},{12,8},{16,20},{20,16},{24,28},{28,24},{1,5},{5... | collective-permute-start | bytes 61448 | tf_op jit(solution)/shard_map/ppermute | solution.py:54
  36.7 4.2 %collective-permute-start.12 = (f32[40,128]{1,0:T(8,128)S(1)}, f32[40,128]{1,0:T(8,128)S(1)}, u32[]{:S(2)}, u32[]{:S(2)}) collective-permute-start(f32[40,128]{1,0:T(8,128)S(1)} %get-tuple-element.125.refs_7_.refs_15_), channel_id=1, source_target_pairs={{0,28},{4,8},{8,4},{12,16},{16,12},{20,24},{24,20},{28,0},{1,29},{... | collective-permute-start | bytes 61448 | tf_op jit(solution)/shard_map/ppermute | solution.py:54
  41.1 7.5 %collective-permute-start.13 = (f32[136,128]{1,0:T(8,128)S(1)}, f32[136,128]{1,0:T(8,128)S(1)}, u32[]{:S(2)}, u32[]{:S(2)}) collective-permute-start(f32[136,128]{1,0:T(8,128)S(1)} %get-tuple-element.135), channel_id=1, source_target_pairs={{1,0},{2,1},{3,2},{0,3},{5,4},{6,5},{7,6},{4,7},{9,8},{10,9},{11,1... | collective-permute-start | bytes 208904 | tf_op jit(solution)/shard_map/ppermute | solution.py:47
  43.6 6.1 %collective-permute-start.15 = (f32[136,128]{1,0:T(8,128)S(1)}, f32[136,128]{1,0:T(8,128)S(1)}, u32[]{:S(2)}, u32[]{:S(2)}) collective-permute-start(f32[136,128]{1,0:T(8,128)S(1)} %get-tuple-element.137), channel_id=1, source_target_pairs={{3,0},{0,1},{1,2},{2,3},{7,4},{4,5},{5,6},{6,7},{11,8},{8,9},{9,10... | collective-permute-start | bytes 208904 | tf_op jit(solution)/shard_map/ppermute | solution.py:47
  43.6 5.0 %collective-permute-start.14 = (f32[32,128]{1,0:T(8,128)S(1)}, f32[32,128]{1,0:T(8,128)S(1)}, u32[]{:S(2)}, u32[]{:S(2)}) collective-permute-start(f32[32,128]{1,0:T(8,128)S(1)} %get-tuple-element.136), channel_id=1, source_target_pairs={{2,0},{3,1},{0,2},{1,3},{6,4},{7,5},{4,6},{5,7},{10,8},{11,9},{8,1... | collective-permute-start | bytes 49160 | tf_op jit(solution)/shard_map/ppermute | solution.py:47
  50.2 5.9 %collective-permute-start.16 = (f32[32,128]{1,0:T(8,128)S(1)}, f32[32,128]{1,0:T(8,128)S(1)}, u32[]{:S(2)}, u32[]{:S(2)}) collective-permute-start(f32[32,128]{1,0:T(8,128)S(1)} %get-tuple-element.145), channel_id=1, source_target_pairs={{3,0},{0,1},{1,2},{2,3},{7,4},{4,5},{5,6},{6,7},{11,8},{8,9},{9,10... | collective-permute-start | bytes 49160 | tf_op jit(solution)/shard_map/ppermute | solution.py:47
  51.0 5.1 %collective-permute-start.17 = (f32[32,128]{1,0:T(8,128)S(1)}, f32[32,128]{1,0:T(8,128)S(1)}, u32[]{:S(2)}, u32[]{:S(2)}) collective-permute-start(f32[32,128]{1,0:T(8,128)S(1)} %get-tuple-element.146), channel_id=1, source_target_pairs={{1,0},{2,1},{3,2},{0,3},{5,4},{6,5},{7,6},{4,7},{9,8},{10,9},{11,1... | collective-permute-start | bytes 49160 | tf_op jit(solution)/shard_map/ppermute | solution.py:47

commit v6 on v5

--- a/solution.py
+++ b/solution.py
@@ -86,18 +86,19 @@
     return jnp.where(sublanes(shape) == low_row, 1.0, 0.0).astype(BF16)
 
 
-def scatter_rows(value_rows, code_rows, groups, width):
+def scatter_rows(value_rows, code_rows, groups, width, counted=False):
     terms, hots = [], []
     for value, code in zip(value_rows, code_rows, strict=True):
         group = code // width
-        shape = (groups, value.shape[-1])
-        hit = sublanes(shape) == group
-        terms.append(jnp.concatenate([jnp.where(hit, part.astype(F32), 0.0) for part in split3(value)], axis=0).astype(BF16))
+        hit = sublanes((groups, value.shape[-1])) == group
+        parts = [part.astype(F32) for part in split3(value)] + ([jnp.ones_like(value)] if counted else [])
+        terms.append(jnp.concatenate([jnp.where(hit, part, 0.0) for part in parts], axis=0).astype(BF16))
         hots.append(one_hot_lines(code - group * width, width))
     left = jnp.concatenate(terms, axis=1)
     right = jnp.concatenate(hots, axis=1)
     total = lax.dot_general(left, right, (((1,), (1,)), ((), ())), preferred_element_type=F32)
-    return total[:groups] + total[groups:2 * groups] + total[2 * groups:3 * groups]
+    sums = total[:groups] + total[groups:2 * groups] + total[2 * groups:3 * groups]
+    return (sums, total[3 * groups:]) if counted else sums
 
 
 def gather_rows(table, code_rows, width):
@@ -285,8 +286,7 @@
         surface = surface + drug[member]
     rows = code_list(codes)
     groups = sectors * across
-    sums = scatter_rows(code_list(surface), rows, groups, width)
-    counts = scatter_rows(code_list(jnp.ones_like(surface)), rows, groups, width)
+    sums, counts = scatter_rows(code_list(surface), rows, groups, width, counted=True)
     first = pack_lines(top[0:1, :], width)
     openness = PERMEABILITY * (1.0 - strut[...].astype(F32))
     for rel in range(sectors):
@@ -546,8 +546,10 @@
         fall = finished_tiles(rim_refs[1], FALL_SLOTS, False, radial, across, drugs, fixed_rows) + [top]
         if first:
             own = code_ref[...].astype(F32)
-            rise = rise + [shut, pltpu.roll(own, 1, 1)]
-            fall = fall + [shut, own]
+            spare, free_lane = len(rise) - 2, lanes(plane) == along - 1
+            rise[spare] = jnp.where(free_lane, own, rise[spare])
+            fall[spare] = jnp.where(free_lane, pltpu.roll(own, along - 1, 1), fall[spare])
+            rise, fall = rise + [shut], fall + [shut]
         for place, (up, down) in enumerate(zip(rise, fall, strict=True)):
             one_ref[place * across:(place + 1) * across, :] = by_parity(up, down)
             two_ref[place * across:(place + 1) * across, :] = by_parity(down, up)
@@ -558,7 +560,7 @@
     tables = [table_of(inbox, (2 + side) * across, across) for side in range(2)]
     if step == 1:
         place = code_place(radial, across, along)
-        sides = [message[place:place + across, 0:1].astype(jnp.int32) for message in (behind, ahead)]
+        sides = [message[place:place + across, along - 1:along].astype(jnp.int32) for message in (behind, ahead)]
         sides = [jnp.broadcast_to(side, plane) for side in sides]
         opens = [gather_cells(table_of(inbox, (4 + side) * across, across), sides[side], along) for side in range(2)]
         for side in range(2):
@@ -591,7 +593,7 @@
 
 
 def code_place(radial, across, along):
-    return (rim_rows(radial, across, along) // across + 2) * across
+    return rim_rows(radial, across, along) - across
 
 
 def rim_rows(radial, across, along):
@@ -644,7 +646,7 @@
             coef_ref[place:place + 1, :] = part[:, step * width:(step + 1) * width]
 
 
-TOGETHER = 2
+TOGETHER = 4
 
 
 def plan_kernel(free_ref, bound_ref, spread_ref, on_ref, off_ref, moved_ref, coef_ref):
@@ -856,7 +858,7 @@
         if odd:
             pair = [plane, plane]
         else:
-            pair = [(rim + (3 if step == 0 else 1) * across, along)] * 2
+            pair = [(rim + (2 if step == 0 else 1) * across, along)] * 2
         outs = [flat] + pair + [plane] * (1 if last else 2)
         if step == 0:
             outs = outs + [plane, plane, jax.ShapeDtypeStruct(plane, jnp.int32)]

time: 57 us -> 56.9 us (level)
  waiting for transfers between devices: 17.4 us -> 16.8 us
    ppermute x14, waiting for transfers between devices: 13.5 us -> 12.9 us  [shifted(): lax.ppermute(block, axis, [((i - distance) % count, i) for i in range(cou...]
    pallas_call x4, Pallas kernels: 4.3 us -> 4.88 us  [per_device(): kernel_call(functools.partial(wall_kernel, last), [shapes, shapes] + ([]...]
  transfers between devices with their start and end apart: 18 -> 18, of which waited for: 10 -> 10; matrix products, arithmetic and copies ran while one was open for 0% -> 0% of each run, Pallas kernels for 17% -> 18%
where the time goes in v6:
time: 56.9 us; the launch traced here: 56.7 us
  starting transfers between devices  24.4 us (43%)
  waiting for transfers between devices  16.8 us (30%)
  Pallas kernels  14.6 us (26%)
  between operations  0.88 us (2%)
    ppermute x14, starting transfers between devices, shifted(): lax.ppermute(block, axis, [((i - distance) % count, i) for i in range(cou...  19.8 us
    ppermute x14, waiting for transfers between devices, shifted(): lax.ppermute(block, axis, [((i - distance) % count, i) for i in range(cou...  12.9 us
    pallas_call x4, Pallas kernels, per_device(): kernel_call(functools.partial(wall_kernel, last), [shapes, shapes] + ([]...  4.88 us
    ppermute x4, starting transfers between devices, paired(): return (lax.ppermute(inner, 'ax', near), lax.ppermute(outer, 'ax', far))  4.64 us
    ppermute x4, waiting for transfers between devices, paired(): return (lax.ppermute(inner, 'ax', near), lax.ppermute(outer, 'ax', far))  3.89 us
    pallas_call x3, Pallas kernels, per_device(): kernel_call(functools.partial(bulk_kernel, False, not odd, odd, radial, a...  3.01 us
    pallas_call x4, Pallas kernels, per_device(): kernel_call(functools.partial(flux_kernel, sectors, step, radial), outs,...  1.78 us
    pallas_call x1, Pallas kernels, first_call(): pl.pallas_call(functools.partial(first_kernel, sectors), name='first', ou...  1.27 us
  transfers between devices with their start and end apart: 18, of which 10 were waited for; matrix products, arithmetic and copies ran while one was open for 0% of the time, Pallas kernels for 18%

profile of v6, /device:TPU:0, one launch (start us, length us, event | category | flops | bytes accessed | tf_op | source)
XLA Modules:
  0.0 56.7 jit_solution(17922056759985398063)
XLA Ops:
  0.7 1.3 %first.1 = (s32[8,128]{1,0:T(8,128)S(1)}, f32[32,128]{1,0:T(8,128)S(1)}, f32[40,128]{1,0:T(8,128)S(1)}, f32[32,128]{1,0:T(8,128)S(1)}, f32[40,128]{1,0:T(8,128)S(1)}) custom-call(f32[26,16,8,128]{3,2,1,0:T(8,128)} %pops_ref.1, s32[8,128]{1,0:T(8,128)} %bitcast.31, s32[8,128]{1,0:T(8,128)} %bitcast.32, s32[8,128]{1,0:T(8,128)} %bitcast.8, f32[128,1024]{1,0:T(8,128)} %free_ref.3), custom_call_target="tpu_custom_call" | custom-call | tf_op jit(solution)/shard_map/first/pallas_call | solution.py:805
  2.0 5.1 %collective-permute-start = (f32[40,128]{1,0:T(8,128)S(1)}, f32[40,128]{1,0:T(8,128)S(1)}, u32[]{:S(2)}, u32[]{:S(2)}) collective-permute-start(f32[40,128]{1,0:T(8,128)S(1)} %get-tuple-element.84), channel_id=1, source_target_pairs={{1,0},{2,1},{3,2},{0,3},{5,4},{6,5},{7,6},{4,7},{9,8},{10,9},{11,1... | collective-permute-start | bytes 61448 | tf_op jit(solution)/shard_map/ppermute | solution.py:47
  7.1 1.0 %collective-permute-start.1 = (f32[32,128]{1,0:T(8,128)S(1)}, f32[32,128]{1,0:T(8,128)S(1)}, u32[]{:S(2)}, u32[]{:S(2)}) collective-permute-start(f32[32,128]{1,0:T(8,128)S(1)} %get-tuple-element.85), channel_id=1, source_target_pairs={{2,0},{3,1},{0,2},{1,3},{6,4},{7,5},{4,6},{5,7},{10,8},{11,9},{8,1... | collective-permute-start | bytes 49160 | tf_op jit(solution)/shard_map/ppermute | solution.py:47
  8.1 1.2 %shard_map.120 = (f32[3328,128]{1,0:T(8,128)S(1)}, f32[24,128]{1,0:T(8,128)S(1)}, f32[32,128]{1,0:T(8,128)S(1)}, f32[32,128]{1,0:T(8,128)S(1)}) custom-call(f32[3328,128]{1,0:T(8,128)S(1)} %bitcast.6), custom_call_target="tpu_custom_call" | custom-call | bytes 4500000 | tf_op jit(solution)/shard_map/pallas_call | solution.py:847
  9.8 1.9 %collective-permute-done.1.refs_10_ = f32[32,128]{1,0:T(8,128)S(1)} collective-permute-done((f32[32,128]{1,0:T(8,128)S(1)}, f32[32,128]{1,0:T(8,128)S(1)}, u32[]{:S(2)}, u32[]{:S(2)}) %collective-permute-start.1) | collective-permute-done | bytes 16416 | tf_op jit(solution)/shard_map/ppermute | solution.py:47
  11.8 0.9 %collective-permute-done.2.refs_11_ = f32[40,128]{1,0:T(8,128)S(1)} collective-permute-done((f32[40,128]{1,0:T(8,128)S(1)}, f32[40,128]{1,0:T(8,128)S(1)}, u32[]{:S(2)}, u32[]{:S(2)}) %collective-permute-start.2) | collective-permute-done | bytes 20512 | tf_op jit(solution)/shard_map/ppermute | solution.py:47
  13.2 2.5 %collective-permute-start.4 = (f32[48,128]{1,0:T(8,128)S(1)}, f32[48,128]{1,0:T(8,128)S(1)}, u32[]{:S(2)}, u32[]{:S(2)}) collective-permute-start(f32[48,128]{1,0:T(8,128)S(1)} %get-tuple-element.91.refs_7_.refs_15_), channel_id=1, source_target_pairs={{0,28},{4,8},{8,4},{12,16},{16,12},{20,24},{24,20},{28,0},{1,29},{... | collective-permute-start | bytes 73736 | tf_op jit(solution)/shard_map/ppermute | solution.py:54
  15.7 1.7 %collective-permute-done.4.refs_2_.refs_17_ = f32[48,128]{1,0:T(8,128)S(1)} collective-permute-done((f32[48,128]{1,0:T(8,128)S(1)}, f32[48,128]{1,0:T(8,128)S(1)}, u32[]{:S(2)}, u32[]{:S(2)}) %collective-permute-start.4) | collective-permute-done | bytes 24608 | tf_op jit(solution)/shard_map/ppermute | solution.py:54
  17.7 2.9 %collective-permute-start.5 = (f32[152,128]{1,0:T(8,128)S(1)}, f32[152,128]{1,0:T(8,128)S(1)}, u32[]{:S(2)}, u32[]{:S(2)}) collective-permute-start(f32[152,128]{1,0:T(8,128)S(1)} %get-tuple-element.101), channel_id=1, source_target_pairs={{1,0},{2,1},{3,2},{0,3},{5,4},{6,5},{7,6},{4,7},{9,8},{10,9},{11,1... | collective-permute-start | bytes 233480 | tf_op jit(solution)/shard_map/ppermute | solution.py:47
  20.6 0.6 %collective-permute-start.6 = (f32[48,128]{1,0:T(8,128)S(1)}, f32[48,128]{1,0:T(8,128)S(1)}, u32[]{:S(2)}, u32[]{:S(2)}) collective-permute-start(f32[48,128]{1,0:T(8,128)S(1)} %get-tuple-element.102), channel_id=1, source_target_pairs={{2,0},{3,1},{0,2},{1,3},{6,4},{7,5},{4,6},{5,7},{10,8},{11,9},{8,1... | collective-permute-start | bytes 73736 | tf_op jit(solution)/shard_map/ppermute | solution.py:47
  21.3 1.1 %shard_map.124 = (f32[128,1024]{1,0:T(8,128)S(1)}, f32[128,1024]{1,0:T(8,128)S(1)}, f32[32,128]{1,0:T(8,128)S(1)}) custom-call(f32[128,1024]{1,0:T(8,128)S(1)} %get-tuple-element.95.moved_ref, f32[128,1024]{1,0:T(8,128)S(1)} %copy-done.2, f32[8,128]{1,0:T(8,128)S(1)} %get-tuple-element.96.added_ref, f32[128,128]{1,0:T(8,128)S(1)} %copy-done.3, ...), custom_call_target="tpu_custom_call" | custom-call | bytes 4500000 | tf_op jit(solution)/shard_map/pallas_call | solution.py:883
  22.4 0.8 %shard_map.123 = (f32[3328,128]{1,0:T(8,128)S(1)}, f32[3328,128]{1,0:T(8,128)S(1)}, f32[24,128]{1,0:T(8,128)S(1)}) custom-call(f32[3328,128]{1,0:T(8,128)S(1)} %get-tuple-element.89.refs_0_, f32[48,128]{1,0:T(8,128)S(1)} %collective-permute-done.3.refs_1_.refs_16_, f32[48,128]{1,0:T(8,128)S(1)} %collective-permute-done.4.refs_2_.refs_17_), custom_call_target="tpu_custom_call" | custom-call | bytes 6000000 | tf_op jit(solution)/shard_map/pallas_call | solution.py:898
  23.1 2.8 %collective-permute-done.6.refs_10_ = f32[48,128]{1,0:T(8,128)S(1)} collective-permute-done((f32[48,128]{1,0:T(8,128)S(1)}, f32[48,128]{1,0:T(8,128)S(1)}, u32[]{:S(2)}, u32[]{:S(2)}) %collective-permute-start.6) | collective-permute-done | bytes 24608 | tf_op jit(solution)/shard_map/ppermute | solution.py:47
  25.9 0.9 %collective-permute-done.7.refs_11_ = f32[152,128]{1,0:T(8,128)S(1)} collective-permute-done((f32[152,128]{1,0:T(8,128)S(1)}, f32[152,128]{1,0:T(8,128)S(1)}, u32[]{:S(2)}, u32[]{:S(2)}) %collective-permute-start.7) | collective-permute-done | bytes 77856 | tf_op jit(solution)/shard_map/ppermute | solution.py:47
  27.6 2.4 %collective-permute-start.8 = (f32[112,128]{1,0:T(8,128)S(1)}, f32[112,128]{1,0:T(8,128)S(1)}, u32[]{:S(2)}, u32[]{:S(2)}) collective-permute-start(f32[112,128]{1,0:T(8,128)S(1)} %get-tuple-element.118), channel_id=1, source_target_pairs={{1,0},{2,1},{3,2},{0,3},{5,4},{6,5},{7,6},{4,7},{9,8},{10,9},{11,1... | collective-permute-start | bytes 172040 | tf_op jit(solution)/shard_map/ppermute | solution.py:47
  30.0 0.7 %collective-permute-start.9 = (f32[16,128]{1,0:T(8,128)S(1)}, f32[16,128]{1,0:T(8,128)S(1)}, u32[]{:S(2)}, u32[]{:S(2)}) collective-permute-start(f32[16,128]{1,0:T(8,128)S(1)} %get-tuple-element.119), channel_id=1, source_target_pairs={{2,0},{3,1},{0,2},{1,3},{6,4},{7,5},{4,6},{5,7},{10,8},{11,9},{8,1... | collective-permute-start | bytes 24584 | tf_op jit(solution)/shard_map/ppermute | solution.py:47
  30.6 1.5 %shard_map.127 = (f32[3328,128]{1,0:T(8,128)S(1)}, f32[3328,128]{1,0:T(8,128)S(1)}, f32[24,128]{1,0:T(8,128)S(1)}, f32[32,128]{1,0:T(8,128)S(1)}, f32[32,128]{1,0:T(8,128)S(1)}) custom-call(f32[3328,128]{1,0:T(8,128)S(1)} %get-tuple-element.106.refs_0_, f32[8,128]{1,0:T(8,128)S(1)} %get-tuple-element.107.refs_1_, f32[8,128]{1,0:T(8,128)S(1)} %get-tuple-element.108.refs_2_), custom_call_target="tpu_custom_call" | custom-call | bytes 6000000 | tf_op jit(solution)/shard_map/pallas_call | solution.py:898
  32.1 1.1 %shard_map.128 = (f32[128,1024]{1,0:T(8,128)S(1)}, f32[128,1024]{1,0:T(8,128)S(1)}, f32[32,128]{1,0:T(8,128)S(1)}) custom-call(f32[128,1024]{1,0:T(8,128)S(1)} %get-tuple-element.112.moved_ref, f32[128,1024]{1,0:T(8,128)S(1)} %get-tuple-element.113.bound_ref, f32[8,128]{1,0:T(8,128)S(1)} %get-tuple-element.114.added_ref, f32[128,128]{1,0:T(8,128)S(1)} %copy-done.3, ...), custom_call_target="tpu_custom_call" | custom-call | bytes 4500000 | tf_op jit(solution)/shard_map/pallas_call | solution.py:883
  33.2 1.3 %collective-permute-done.9.refs_10_ = f32[16,128]{1,0:T(8,128)S(1)} collective-permute-done((f32[16,128]{1,0:T(8,128)S(1)}, f32[16,128]{1,0:T(8,128)S(1)}, u32[]{:S(2)}, u32[]{:S(2)}) %collective-permute-start.9) | collective-permute-done | bytes 8224 | tf_op jit(solution)/shard_map/ppermute | solution.py:47
  34.5 1.4 %collective-permute-done.10.refs_11_ = f32[112,128]{1,0:T(8,128)S(1)} collective-permute-done((f32[112,128]{1,0:T(8,128)S(1)}, f32[112,128]{1,0:T(8,128)S(1)}, u32[]{:S(2)}, u32[]{:S(2)}) %collective-permute-start.10) | collective-permute-done | bytes 57376 | tf_op jit(solution)/shard_map/ppermute | solution.py:47
  36.6 1.9 %collective-permute-start.12 = (f32[40,128]{1,0:T(8,128)S(1)}, f32[40,128]{1,0:T(8,128)S(1)}, u32[]{:S(2)}, u32[]{:S(2)}) collective-permute-start(f32[40,128]{1,0:T(8,128)S(1)} %get-tuple-element.125.refs_7_.refs_15_), channel_id=1, source_target_pairs={{0,28},{4,8},{8,4},{12,16},{16,12},{20,24},{24,20},{28,0},{1,29},{... | collective-permute-start | bytes 61448 | tf_op jit(solution)/shard_map/ppermute | solution.py:54
  38.5 2.2 %collective-permute-done.12.refs_2_.refs_17_ = f32[40,128]{1,0:T(8,128)S(1)} collective-permute-done((f32[40,128]{1,0:T(8,128)S(1)}, f32[40,128]{1,0:T(8,128)S(1)}, u32[]{:S(2)}, u32[]{:S(2)}) %collective-permute-start.12) | collective-permute-done | bytes 20512 | tf_op jit(solution)/shard_map/ppermute | solution.py:54
  41.0 2.5 %collective-permute-start.13 = (f32[136,128]{1,0:T(8,128)S(1)}, f32[136,128]{1,0:T(8,128)S(1)}, u32[]{:S(2)}, u32[]{:S(2)}) collective-permute-start(f32[136,128]{1,0:T(8,128)S(1)} %get-tuple-element.135), channel_id=1, source_target_pairs={{1,0},{2,1},{3,2},{0,3},{5,4},{6,5},{7,6},{4,7},{9,8},{10,9},{11,1... | collective-permute-start | bytes 208904 | tf_op jit(solution)/shard_map/ppermute | solution.py:47
  43.5 0.6 %collective-permute-start.14 = (f32[32,128]{1,0:T(8,128)S(1)}, f32[32,128]{1,0:T(8,128)S(1)}, u32[]{:S(2)}, u32[]{:S(2)}) collective-permute-start(f32[32,128]{1,0:T(8,128)S(1)} %get-tuple-element.136), channel_id=1, source_target_pairs={{2,0},{3,1},{0,2},{1,3},{6,4},{7,5},{4,6},{5,7},{10,8},{11,9},{8,1... | collective-permute-start | bytes 49160 | tf_op jit(solution)/shard_map/ppermute | solution.py:47
  44.1 1.1 %shard_map.132 = (f32[128,1024]{1,0:T(8,128)S(1)}, f32[128,1024]{1,0:T(8,128)S(1)}, f32[32,128]{1,0:T(8,128)S(1)}) custom-call(f32[128,1024]{1,0:T(8,128)S(1)} %get-tuple-element.129.moved_ref, f32[128,1024]{1,0:T(8,128)S(1)} %get-tuple-element.130.bound_ref, f32[8,128]{1,0:T(8,128)S(1)} %get-tuple-element.131.added_ref, f32[128,128]{1,0:T(8,128)S(1)} %copy-done.3, ...), custom_call_target="tpu_custom_call" | custom-call | bytes 4500000 | tf_op jit(solution)/shard_map/pallas_call | solution.py:883
  45.3 0.8 %shard_map.131 = (f32[3328,128]{1,0:T(8,128)S(1)}, f32[3328,128]{1,0:T(8,128)S(1)}, f32[24,128]{1,0:T(8,128)S(1)}) custom-call(f32[3328,128]{1,0:T(8,128)S(1)} %get-tuple-element.123.refs_0_, f32[40,128]{1,0:T(8,128)S(1)} %collective-permute-done.11.refs_1_.refs_16_, f32[40,128]{1,0:T(8,128)S(1)} %collective-permute-done.12.refs_2_.refs_17_), custom_call_target="tpu_custom_call" | custom-call | bytes 6000000 | tf_op jit(solution)/shard_map/pallas_call | solution.py:898
  46.0 2.5 %collective-permute-done.14.refs_10_ = f32[32,128]{1,0:T(8,128)S(1)} collective-permute-done((f32[32,128]{1,0:T(8,128)S(1)}, f32[32,128]{1,0:T(8,128)S(1)}, u32[]{:S(2)}, u32[]{:S(2)}) %collective-permute-start.14) | collective-permute-done | bytes 16416 | tf_op jit(solution)/shard_map/ppermute | solution.py:47
  48.5 1.1 %collective-permute-done.15.refs_11_ = f32[136,128]{1,0:T(8,128)S(1)} collective-permute-done((f32[136,128]{1,0:T(8,128)S(1)}, f32[136,128]{1,0:T(8,128)S(1)}, u32[]{:S(2)}, u32[]{:S(2)}) %collective-permute-start.15) | collective-permute-done | bytes 69664 | tf_op jit(solution)/shard_map/ppermute | solution.py:47
  50.1 0.8 %collective-permute-start.16 = (f32[32,128]{1,0:T(8,128)S(1)}, f32[32,128]{1,0:T(8,128)S(1)}, u32[]{:S(2)}, u32[]{:S(2)}) collective-permute-start(f32[32,128]{1,0:T(8,128)S(1)} %get-tuple-element.145), channel_id=1, source_target_pairs={{3,0},{0,1},{1,2},{2,3},{7,4},{4,5},{5,6},{6,7},{11,8},{8,9},{9,10... | collective-permute-start | bytes 49160 | tf_op jit(solution)/shard_map/ppermute | solution.py:47
  50.9 3.1 %collective-permute-start.17 = (f32[32,128]{1,0:T(8,128)S(1)}, f32[32,128]{1,0:T(8,128)S(1)}, u32[]{:S(2)}, u32[]{:S(2)}) collective-permute-start(f32[32,128]{1,0:T(8,128)S(1)} %get-tuple-element.146), channel_id=1, source_target_pairs={{1,0},{2,1},{3,2},{0,3},{5,4},{6,5},{7,6},{4,7},{9,8},{10,9},{11,1... | collective-permute-start | bytes 49160 | tf_op jit(solution)/shard_map/ppermute | solution.py:47
  54.5 1.6 %shard_map.138 = (f32[128,1024]{1,0:T(8,128)}, f32[128,1024]{1,0:T(8,128)}) custom-call(f32[128,1024]{1,0:T(8,128)S(1)} %get-tuple-element.149.moved_ref, f32[128,1024]{1,0:T(8,128)S(1)} %get-tuple-element.150.bound_ref, f32[8,128]{1,0:T(8,128)S(1)} %get-tuple-element.151.added_ref, f32[128,128]{1,0:T(8,128)S(1)} %copy-done.3, f32[1,128]{1,0:T(1,128)S(1)} %bitcast.21, ...), custom_call_target="tpu_custom_call" | custom-call | bytes 4500000 | tf_op jit(solution)/shard_map/pallas_call | solution.py:883
  56.1 0.7 %shard_map.137 = (f32[16,8,128]{2,1,0:T(8,128)}, f32[16,8,128]{2,1,0:T(8,128)}) custom-call(f32[16,8,128]{2,1,0:T(8,128)S(1)} %get-tuple-element.143.drug_part, f32[16,8,128]{2,1,0:T(8,128)S(1)} %get-tuple-element.144.flow_part, f32[32,128]{1,0:T(8,128)S(1)} %collective-permute-done.16.below, f32[32,128]{1,0:T(8,128)S(1)} %collective-permute-done.17.above), custom_call_target="tpu_custom_call" | custom-call | bytes 900000 | tf_op jit(solution)/shard_map/pallas_call | solution.py:909
  (38 shorter events, 3.8 us)
Async XLA Ops:
  0.6 7.5 %copy-start = (f32[26,16,8,128]{3,2,1,0:T(8,128)S(1)}, f32[26,16,8,128]{3,2,1,0:T(8,128)}, u32[]{:S(2)}) copy-start(f32[26,16,8,128]{3,2,1,0:T(8,128)} %pops_ref.1) | copy-start | bytes 5111812
  0.6 8.7 %copy-start.1 = (f32[128,1024]{1,0:T(8,128)S(1)}, f32[128,1024]{1,0:T(8,128)}, u32[]{:S(2)}) copy-start(f32[128,1024]{1,0:T(8,128)} %free_ref.3) | copy-start | bytes 1572868
  0.7 8.7 %copy-start.2 = (f32[128,1024]{1,0:T(8,128)S(1)}, f32[128,1024]{1,0:T(8,128)}, u32[]{:S(2)}) copy-start(f32[128,1024]{1,0:T(8,128)} %bound_ref.3) | copy-start | bytes 1572868
  0.7 8.7 %copy-start.3 = (f32[128,128]{1,0:T(8,128)S(1)}, f32[128,128]{1,0:T(8,128)}, u32[]{:S(2)}) copy-start(f32[128,128]{1,0:T(8,128)} %spread_ref.9) | copy-start | bytes 196612
  0.7 8.7 %copy-start.5 = (f32[128]{0:T(128)S(1)}, f32[128]{0:T(128)}, u32[]{:S(2)}) copy-start(f32[128]{0:T(128)} %param.13) | copy-start | bytes 1540
  0.7 8.7 %copy-start.6 = (f32[128]{0:T(128)S(1)}, f32[128]{0:T(128)}, u32[]{:S(2)}) copy-start(f32[128]{0:T(128)} %param.14) | copy-start | bytes 1540
  2.0 10.7 %copy-start.4 = (s32[1024]{0:T(1024)S(1)}, s32[1024]{0:T(1024)}, u32[]{:S(2)}) copy-start(s32[1024]{0:T(1024)} %param.17) | copy-start | bytes 12292
  2.0 9.8 %collective-permute-start = (f32[40,128]{1,0:T(8,128)S(1)}, f32[40,128]{1,0:T(8,128)S(1)}, u32[]{:S(2)}, u32[]{:S(2)}) collective-permute-start(f32[40,128]{1,0:T(8,128)S(1)} %get-tuple-element.84), channel_id=1, source_target_pairs={{1,0},{2,1},{3,2},{0,3},{5,4},{6,5},{7,6},{4,7},{9,8},{10,9},{11,1... | collective-permute-start | bytes 61448 | tf_op jit(solution)/shard_map/ppermute | solution.py:47
  7.1 5.6 %collective-permute-start.2 = (f32[40,128]{1,0:T(8,128)S(1)}, f32[40,128]{1,0:T(8,128)S(1)}, u32[]{:S(2)}, u32[]{:S(2)}) collective-permute-start(f32[40,128]{1,0:T(8,128)S(1)} %get-tuple-element.86), channel_id=1, source_target_pairs={{3,0},{0,1},{1,2},{2,3},{7,4},{4,5},{5,6},{6,7},{11,8},{8,9},{9,10... | collective-permute-start | bytes 61448 | tf_op jit(solution)/shard_map/ppermute | solution.py:47
  7.1 4.6 %collective-permute-start.1 = (f32[32,128]{1,0:T(8,128)S(1)}, f32[32,128]{1,0:T(8,128)S(1)}, u32[]{:S(2)}, u32[]{:S(2)}) collective-permute-start(f32[32,128]{1,0:T(8,128)S(1)} %get-tuple-element.85), channel_id=1, source_target_pairs={{2,0},{3,1},{0,2},{1,3},{6,4},{7,5},{4,6},{5,7},{10,8},{11,9},{8,1... | collective-permute-start | bytes 49160 | tf_op jit(solution)/shard_map/ppermute | solution.py:47
  13.1 2.6 %collective-permute-start.3 = (f32[48,128]{1,0:T(8,128)S(1)}, f32[48,128]{1,0:T(8,128)S(1)}, u32[]{:S(2)}, u32[]{:S(2)}) collective-permute-start(f32[48,128]{1,0:T(8,128)S(1)} %get-tuple-element.90.refs_6_.refs_14_), channel_id=1, source_target_pairs={{0,4},{4,0},{8,12},{12,8},{16,20},{20,16},{24,28},{28,24},{1,5},{5... | collective-permute-start | bytes 73736 | tf_op jit(solution)/shard_map/ppermute | solution.py:54
  13.2 4.2 %collective-permute-start.4 = (f32[48,128]{1,0:T(8,128)S(1)}, f32[48,128]{1,0:T(8,128)S(1)}, u32[]{:S(2)}, u32[]{:S(2)}) collective-permute-start(f32[48,128]{1,0:T(8,128)S(1)} %get-tuple-element.91.refs_7_.refs_15_), channel_id=1, source_target_pairs={{0,28},{4,8},{8,4},{12,16},{16,12},{20,24},{24,20},{28,0},{1,29},{... | collective-permute-start | bytes 73736 | tf_op jit(solution)/shard_map/ppermute | solution.py:54
  17.7 8.3 %collective-permute-start.5 = (f32[152,128]{1,0:T(8,128)S(1)}, f32[152,128]{1,0:T(8,128)S(1)}, u32[]{:S(2)}, u32[]{:S(2)}) collective-permute-start(f32[152,128]{1,0:T(8,128)S(1)} %get-tuple-element.101), channel_id=1, source_target_pairs={{1,0},{2,1},{3,2},{0,3},{5,4},{6,5},{7,6},{4,7},{9,8},{10,9},{11,1... | collective-permute-start | bytes 233480 | tf_op jit(solution)/shard_map/ppermute | solution.py:47
  20.6 6.2 %collective-permute-start.7 = (f32[152,128]{1,0:T(8,128)S(1)}, f32[152,128]{1,0:T(8,128)S(1)}, u32[]{:S(2)}, u32[]{:S(2)}) collective-permute-start(f32[152,128]{1,0:T(8,128)S(1)} %get-tuple-element.103), channel_id=1, source_target_pairs={{3,0},{0,1},{1,2},{2,3},{7,4},{4,5},{5,6},{6,7},{11,8},{8,9},{9,10... | collective-permute-start | bytes 233480 | tf_op jit(solution)/shard_map/ppermute | solution.py:47
  20.6 5.3 %collective-permute-start.6 = (f32[48,128]{1,0:T(8,128)S(1)}, f32[48,128]{1,0:T(8,128)S(1)}, u32[]{:S(2)}, u32[]{:S(2)}) collective-permute-start(f32[48,128]{1,0:T(8,128)S(1)} %get-tuple-element.102), channel_id=1, source_target_pairs={{2,0},{3,1},{0,2},{1,3},{6,4},{7,5},{4,6},{5,7},{10,8},{11,9},{8,1... | collective-permute-start | bytes 73736 | tf_op jit(solution)/shard_map/ppermute | solution.py:47
  27.6 7.0 %collective-permute-start.8 = (f32[112,128]{1,0:T(8,128)S(1)}, f32[112,128]{1,0:T(8,128)S(1)}, u32[]{:S(2)}, u32[]{:S(2)}) collective-permute-start(f32[112,128]{1,0:T(8,128)S(1)} %get-tuple-element.118), channel_id=1, source_target_pairs={{1,0},{2,1},{3,2},{0,3},{5,4},{6,5},{7,6},{4,7},{9,8},{10,9},{11,1... | collective-permute-start | bytes 172040 | tf_op jit(solution)/shard_map/ppermute | solution.py:47
  30.0 6.0 %collective-permute-start.10 = (f32[112,128]{1,0:T(8,128)S(1)}, f32[112,128]{1,0:T(8,128)S(1)}, u32[]{:S(2)}, u32[]{:S(2)}) collective-permute-start(f32[112,128]{1,0:T(8,128)S(1)} %get-tuple-element.120), channel_id=1, source_target_pairs={{3,0},{0,1},{1,2},{2,3},{7,4},{4,5},{5,6},{6,7},{11,8},{8,9},{9,10... | collective-permute-start | bytes 172040 | tf_op jit(solution)/shard_map/ppermute | solution.py:47
  30.0 4.5 %collective-permute-start.9 = (f32[16,128]{1,0:T(8,128)S(1)}, f32[16,128]{1,0:T(8,128)S(1)}, u32[]{:S(2)}, u32[]{:S(2)}) collective-permute-start(f32[16,128]{1,0:T(8,128)S(1)} %get-tuple-element.119), channel_id=1, source_target_pairs={{2,0},{3,1},{0,2},{1,3},{6,4},{7,5},{4,6},{5,7},{10,8},{11,9},{8,1... | collective-permute-start | bytes 24584 | tf_op jit(solution)/shard_map/ppermute | solution.py:47
  36.5 2.0 %collective-permute-start.11 = (f32[40,128]{1,0:T(8,128)S(1)}, f32[40,128]{1,0:T(8,128)S(1)}, u32[]{:S(2)}, u32[]{:S(2)}) collective-permute-start(f32[40,128]{1,0:T(8,128)S(1)} %get-tuple-element.124.refs_6_.refs_14_), channel_id=1, source_target_pairs={{0,4},{4,0},{8,12},{12,8},{16,20},{20,16},{24,28},{28,24},{1,5},{5... | collective-permute-start | bytes 61448 | tf_op jit(solution)/shard_map/ppermute | solution.py:54
  36.6 4.2 %collective-permute-start.12 = (f32[40,128]{1,0:T(8,128)S(1)}, f32[40,128]{1,0:T(8,128)S(1)}, u32[]{:S(2)}, u32[]{:S(2)}) collective-permute-start(f32[40,128]{1,0:T(8,128)S(1)} %get-tuple-element.125.refs_7_.refs_15_), channel_id=1, source_target_pairs={{0,28},{4,8},{8,4},{12,16},{16,12},{20,24},{24,20},{28,0},{1,29},{... | collective-permute-start | bytes 61448 | tf_op jit(solution)/shard_map/ppermute | solution.py:54
  41.0 7.5 %collective-permute-start.13 = (f32[136,128]{1,0:T(8,128)S(1)}, f32[136,128]{1,0:T(8,128)S(1)}, u32[]{:S(2)}, u32[]{:S(2)}) collective-permute-start(f32[136,128]{1,0:T(8,128)S(1)} %get-tuple-element.135), channel_id=1, source_target_pairs={{1,0},{2,1},{3,2},{0,3},{5,4},{6,5},{7,6},{4,7},{9,8},{10,9},{11,1... | collective-permute-start | bytes 208904 | tf_op jit(solution)/shard_map/ppermute | solution.py:47
  43.5 6.1 %collective-permute-start.15 = (f32[136,128]{1,0:T(8,128)S(1)}, f32[136,128]{1,0:T(8,128)S(1)}, u32[]{:S(2)}, u32[]{:S(2)}) collective-permute-start(f32[136,128]{1,0:T(8,128)S(1)} %get-tuple-element.137), channel_id=1, source_target_pairs={{3,0},{0,1},{1,2},{2,3},{7,4},{4,5},{5,6},{6,7},{11,8},{8,9},{9,10... | collective-permute-start | bytes 208904 | tf_op jit(solution)/shard_map/ppermute | solution.py:47
  43.5 5.0 %collective-permute-start.14 = (f32[32,128]{1,0:T(8,128)S(1)}, f32[32,128]{1,0:T(8,128)S(1)}, u32[]{:S(2)}, u32[]{:S(2)}) collective-permute-start(f32[32,128]{1,0:T(8,128)S(1)} %get-tuple-element.136), channel_id=1, source_target_pairs={{2,0},{3,1},{0,2},{1,3},{6,4},{7,5},{4,6},{5,7},{10,8},{11,9},{8,1... | collective-permute-start | bytes 49160 | tf_op jit(solution)/shard_map/ppermute | solution.py:47
  50.1 5.9 %collective-permute-start.16 = (f32[32,128]{1,0:T(8,128)S(1)}, f32[32,128]{1,0:T(8,128)S(1)}, u32[]{:S(2)}, u32[]{:S(2)}) collective-permute-start(f32[32,128]{1,0:T(8,128)S(1)} %get-tuple-element.145), channel_id=1, source_target_pairs={{3,0},{0,1},{1,2},{2,3},{7,4},{4,5},{5,6},{6,7},{11,8},{8,9},{9,10... | collective-permute-start | bytes 49160 | tf_op jit(solution)/shard_map/ppermute | solution.py:47
  50.9 5.1 %collective-permute-start.17 = (f32[32,128]{1,0:T(8,128)S(1)}, f32[32,128]{1,0:T(8,128)S(1)}, u32[]{:S(2)}, u32[]{:S(2)}) collective-permute-start(f32[32,128]{1,0:T(8,128)S(1)} %get-tuple-element.146), channel_id=1, source_target_pairs={{1,0},{2,1},{3,2},{0,3},{5,4},{6,5},{7,6},{4,7},{9,8},{10,9},{11,1... | collective-permute-start | bytes 49160 | tf_op jit(solution)/shard_map/ppermute | solution.py:47
